TPU v7x, 32 devices: a whole 2x2x4 slice. The times are simulated.
32 devices in a mesh: rep: 4 (over y, core), fsdp: 8 (over z, x).
Axes of the slice: x: 2, y: 2, z: 4, core: 2. Of those that a mesh axis runs over, the one named last changes fastest.
Arguments:
- dec_input: bfloat16 [96, 176, 768], P(('rep', 'fsdp')), may hold values from -6 to 6
- enc_output: bfloat16 [96, 512, 768], P(('rep', 'fsdp')), may hold values from -6 to 6
- dec_segments: int32 [96, 176], P(('rep', 'fsdp')), may hold values from 0 to 3, as said below
- enc_segments: int32 [96, 512], P(('rep', 'fsdp')), may hold values from 0 to 3, as said below
- cotangent: bfloat16 [96, 176, 768], P(('rep', 'fsdp')), may hold values from -6 to 6
- norm_self: bfloat16 [768], P('fsdp'), may hold values from 0.5 to 1.5
- q_self: bfloat16 [768, 768], P('fsdp'), may hold values from -0.0546875 to 0.0546875
- k_self: bfloat16 [768, 768], P('fsdp'), may hold values from -0.21875 to 0.21875
- v_self: bfloat16 [768, 768], P('fsdp'), may hold values from -0.21875 to 0.21875
- o_self: bfloat16 [768, 768], P('fsdp'), may hold values from -0.625 to 0.625
- rel_table: bfloat16 [32, 12], P('fsdp'), may hold values from -4 to 4
- norm_cross: bfloat16 [768], P('fsdp'), may hold values from 0.5 to 1.5
- q_cross: bfloat16 [768, 768], P('fsdp'), may hold values from -0.0546875 to 0.0546875
- k_cross: bfloat16 [768, 768], P('fsdp'), may hold values from -0.21875 to 0.21875
- v_cross: bfloat16 [768, 768], P('fsdp'), may hold values from -0.21875 to 0.21875
- o_cross: bfloat16 [768, 768], P('fsdp'), may hold values from -0.625 to 0.625
- norm_ffn: bfloat16 [768], P('fsdp'), may hold values from 0.5 to 1.5
- wi_gate: bfloat16 [768, 2048], P('fsdp'), may hold values from -0.21875 to 0.21875
- wi_up: bfloat16 [768, 2048], P('fsdp'), may hold values from -0.21875 to 0.21875
- wo_ffn: bfloat16 [2048, 768], P('fsdp'), may hold values from -0.125 to 0.125
Outputs:
- dec_output: bfloat16 [96, 176, 768], P(('rep', 'fsdp'))
- input_grad: bfloat16 [96, 176, 768], P(('rep', 'fsdp'))
- enc_grad: bfloat16 [96, 512, 768], P(('rep', 'fsdp'))
- grad_norm_self: float32 [768], P('fsdp')
- grad_q_self: float32 [768, 768], P('fsdp')
- grad_k_self: float32 [768, 768], P('fsdp')
- grad_v_self: float32 [768, 768], P('fsdp')
- grad_o_self: float32 [768, 768], P('fsdp')
- grad_rel_table: float32 [32, 12], P('fsdp')
- grad_norm_cross: float32 [768], P('fsdp')
- grad_q_cross: float32 [768, 768], P('fsdp')
- grad_k_cross: float32 [768, 768], P('fsdp')
- grad_v_cross: float32 [768, 768], P('fsdp')
- grad_o_cross: float32 [768, 768], P('fsdp')
- grad_norm_ffn: float32 [768], P('fsdp')
- grad_wi_gate: float32 [768, 2048], P('fsdp')
- grad_wi_up: float32 [768, 2048], P('fsdp')
- grad_wo_ffn: float32 [2048, 768], P('fsdp')
Inputs may be any that keep to these rules, and one draw needn't show every extreme that they name: `dec_segments`: each row holds target documents 1, 2 and 3 in this order, each of 22 positions or more, followed by padding 0 on one position or more; document k of a row's targets belongs to document k of the same row's encoder outputs. `enc_segments`: each row holds encoder documents 1, 2 and 3 in this order, each of 64 positions or more, followed by padding 0 on one position or more.
All inputs are finite; a program needn't handle non-finite values.
Results may differ from a plain program's by a relative error of at most 0.025.
The roundings to bfloat16 on the way count: a program that leaves them out, or rounds other values in their place, can miss the bound.
Values may be sent and summed in bfloat16 or wider, within the bound.
No kernel may reach another device: no remote copies, remote signals or barrier semaphores. Data moves between devices by JAX's collectives and lax.ppermute only.
A program may use at most 192 MiB of HBM per device.

v0:
```python
import math

import jax
import jax.numpy as jnp
from jax import lax
from jax.sharding import PartitionSpec as P

HEADS = 12
HEAD = 64
BUCKETS = 32
MAXDIST = 128


norm_epsilon = 1e-06
masked_score = -1000000000.0


def bucket_of(distance):
    exact_part = BUCKETS // 2
    log_part = BUCKETS - exact_part
    bucket = jnp.minimum(distance, exact_part)
    for degree in range(1, log_part):
        threshold = math.ceil(exact_part * (MAXDIST / exact_part) ** (degree / log_part))
        bucket = bucket + (distance >= threshold).astype(jnp.int32)
    return bucket


def bucket_lookup_table(length):
    positions = jnp.arange(length, dtype=jnp.int32)
    distance = jnp.maximum(positions[:, None] - positions[None, :], 0)
    levels = jnp.arange(BUCKETS, dtype=jnp.int32)
    return (bucket_of(distance)[None] == levels[:, None, None]).astype(jnp.bfloat16)


def rms_scale(values, gain):
    return (
        values * lax.rsqrt(jnp.mean(values * values, axis=-1, keepdims=True) + norm_epsilon) * gain
    )


def gated(gate_values, up_values):
    return jax.nn.gelu(gate_values, approximate=True) * up_values


def project(values, matrix):
    return jnp.einsum("rld,de->rle", values, matrix, preferred_element_type=jnp.float32)


def weight_grad(values, grads):
    return jnp.einsum("rld,rle->de", values, grads, preferred_element_type=jnp.float32)


def back_project(grads, matrix):
    return jnp.einsum("rle,de->rld", grads, matrix, preferred_element_type=jnp.float32)


def split_heads(values):
    return values.reshape(values.shape[0], values.shape[1], HEADS, HEAD)


def attention_scores(query_vectors, key_vectors, relative_position_bias, allowed):
    scores = (
        jnp.einsum(
            "rqhd,rkhd->rhqk",
            split_heads(query_vectors),
            split_heads(key_vectors),
            preferred_element_type=jnp.float32,
        )
        + relative_position_bias
    )
    return jnp.where(allowed[:, None], scores, masked_score)


def attention_forward(query_vectors, key_vectors, value_vectors, relative_position_bias, allowed):
    scores = attention_scores(query_vectors, key_vectors, relative_position_bias, allowed)
    highest_score = jnp.max(scores, axis=-1, keepdims=True)
    expanded = jnp.exp(scores - highest_score)
    totals = jnp.sum(expanded, axis=-1, keepdims=True)
    attention_weights = (expanded / totals).astype(jnp.bfloat16)
    context = jnp.einsum(
        "rhqk,rkhd->rqhd",
        attention_weights,
        split_heads(value_vectors),
        preferred_element_type=jnp.float32,
    )
    return (
        context.reshape(query_vectors.shape).astype(jnp.bfloat16),
        highest_score + jnp.log(totals),
    )


def attention_backward(
    query_vectors,
    key_vectors,
    value_vectors,
    relative_position_bias,
    allowed,
    log_total,
    context_grad,
):
    scores = attention_scores(query_vectors, key_vectors, relative_position_bias, allowed)
    attention_weights = jnp.exp(scores - log_total)
    grad_heads = split_heads(context_grad)
    weight_grads = jnp.einsum(
        "rqhd,rkhd->rhqk",
        grad_heads,
        split_heads(value_vectors),
        preferred_element_type=jnp.float32,
    )
    row_dot = jnp.sum(attention_weights * weight_grads, axis=-1, keepdims=True)
    score_grads = (attention_weights * (weight_grads - row_dot)).astype(jnp.bfloat16)
    query_grads = jnp.einsum(
        "rhqk,rkhd->rqhd", score_grads, split_heads(key_vectors), preferred_element_type=jnp.float32
    )
    key_grads = jnp.einsum(
        "rhqk,rqhd->rkhd",
        score_grads,
        split_heads(query_vectors),
        preferred_element_type=jnp.float32,
    )
    value_grads = jnp.einsum(
        "rhqk,rqhd->rkhd",
        attention_weights.astype(jnp.bfloat16),
        grad_heads,
        preferred_element_type=jnp.float32,
    )
    return (
        query_grads.reshape(query_vectors.shape).astype(jnp.bfloat16),
        key_grads.reshape(key_vectors.shape).astype(jnp.bfloat16),
        value_grads.reshape(value_vectors.shape).astype(jnp.bfloat16),
        score_grads,
    )


def shards(
    dec_input,
    enc_output,
    dec_segments,
    enc_segments,
    cotangent,
    norm_self,
    q_self,
    k_self,
    v_self,
    o_self,
    rel_table,
    norm_cross,
    q_cross,
    k_cross,
    v_cross,
    o_cross,
    norm_ffn,
    wi_gate,
    wi_up,
    wo_ffn,
):
    self_set = (
        lax.all_gather(norm_self, "fsdp", axis=0, tiled=True),
        lax.all_gather(q_self, "fsdp", axis=0, tiled=True),
        lax.all_gather(k_self, "fsdp", axis=0, tiled=True),
        lax.all_gather(v_self, "fsdp", axis=0, tiled=True),
        lax.all_gather(o_self, "fsdp", axis=0, tiled=True),
        lax.all_gather(rel_table, "fsdp", axis=0, tiled=True),
    )
    gain_self, query_self, key_self, value_self, out_self, self_bias_table = self_set
    decoder_length = dec_input.shape[1]
    bucket_indices = bucket_lookup_table(decoder_length)
    positions = jnp.arange(decoder_length, dtype=jnp.int32)
    causal = positions[:, None] >= positions[None, :]
    self_allowed = (dec_segments[:, :, None] == dec_segments[:, None, :]) & causal[None]
    cross_allowed = dec_segments[:, :, None] == enc_segments[:, None, :]
    relative_position_bias = jnp.einsum(
        "oul,os->sul", bucket_indices, self_bias_table, preferred_element_type=jnp.float32
    )
    dec_float = dec_input.astype(jnp.float32)
    normed_self = rms_scale(dec_float, gain_self.astype(jnp.float32)).astype(jnp.bfloat16)
    self_queries = project(normed_self, query_self).astype(jnp.bfloat16)
    self_keys = project(normed_self, key_self).astype(jnp.bfloat16)
    self_values = project(normed_self, value_self).astype(jnp.bfloat16)
    self_context, self_total = attention_forward(
        self_queries, self_keys, self_values, relative_position_bias, self_allowed
    )
    middle = dec_float + project(self_context, out_self)
    cross_set = (
        lax.all_gather(norm_cross, "fsdp", axis=0, tiled=True),
        lax.all_gather(q_cross, "fsdp", axis=0, tiled=True),
        lax.all_gather(k_cross, "fsdp", axis=0, tiled=True),
        lax.all_gather(v_cross, "fsdp", axis=0, tiled=True),
        lax.all_gather(o_cross, "fsdp", axis=0, tiled=True),
    )
    gain_cross, query_cross, key_cross, value_cross, out_cross = cross_set
    normed_cross = rms_scale(middle, gain_cross.astype(jnp.float32)).astype(jnp.bfloat16)
    cross_queries = project(normed_cross, query_cross).astype(jnp.bfloat16)
    cross_keys = project(enc_output, key_cross).astype(jnp.bfloat16)
    cross_values = project(enc_output, value_cross).astype(jnp.bfloat16)
    cross_context, cross_total = attention_forward(
        cross_queries, cross_keys, cross_values, 0.0, cross_allowed
    )
    late = middle + project(cross_context, out_cross)
    ffn_set = (
        lax.all_gather(norm_ffn, "fsdp", axis=0, tiled=True),
        lax.all_gather(wi_gate, "fsdp", axis=0, tiled=True),
        lax.all_gather(wi_up, "fsdp", axis=0, tiled=True),
        lax.all_gather(wo_ffn, "fsdp", axis=0, tiled=True),
    )
    gain_ffn, gate_matrix, up_matrix, down_matrix = ffn_set
    normed_ffn = rms_scale(late, gain_ffn.astype(jnp.float32)).astype(jnp.bfloat16)
    gate_values = project(normed_ffn, gate_matrix)
    up_values = project(normed_ffn, up_matrix)
    hidden = gated(gate_values, up_values).astype(jnp.bfloat16)
    dec_output = (late + project(hidden, down_matrix)).astype(jnp.bfloat16)
    ffn_back = (
        lax.all_gather(norm_ffn, "fsdp", axis=0, tiled=True),
        lax.all_gather(wi_gate, "fsdp", axis=0, tiled=True),
        lax.all_gather(wi_up, "fsdp", axis=0, tiled=True),
        lax.all_gather(wo_ffn, "fsdp", axis=0, tiled=True),
    )
    gain_ffn_b, gate_back, up_back, down_back = ffn_back
    grad_down = weight_grad(hidden, cotangent)
    hidden_grad = back_project(cotangent, down_back)
    gated_out, gated_pull = jax.vjp(gated, gate_values, up_values)
    gate_grad, up_grad = gated_pull(hidden_grad)
    gate_grad = gate_grad.astype(jnp.bfloat16)
    up_grad = up_grad.astype(jnp.bfloat16)
    grad_gate = weight_grad(normed_ffn, gate_grad)
    grad_up = weight_grad(normed_ffn, up_grad)
    ffn_in_grad = back_project(gate_grad, gate_back) + back_project(up_grad, up_back)
    norm_out, norm_pull = jax.vjp(rms_scale, late, gain_ffn_b.astype(jnp.float32))
    late_part, grad_gain_ffn = norm_pull(ffn_in_grad)
    late_grad = cotangent.astype(jnp.float32) + late_part
    ffn_sums = (
        lax.psum_scatter(
            grad_gain_ffn.astype(jnp.bfloat16), "fsdp", scatter_dimension=0, tiled=True
        ).astype(jnp.float32),
        lax.psum_scatter(
            grad_gate.astype(jnp.bfloat16), "fsdp", scatter_dimension=0, tiled=True
        ).astype(jnp.float32),
        lax.psum_scatter(
            grad_up.astype(jnp.bfloat16), "fsdp", scatter_dimension=0, tiled=True
        ).astype(jnp.float32),
        lax.psum_scatter(
            grad_down.astype(jnp.bfloat16), "fsdp", scatter_dimension=0, tiled=True
        ).astype(jnp.float32),
    )
    cross_back = (
        lax.all_gather(norm_cross, "fsdp", axis=0, tiled=True),
        lax.all_gather(q_cross, "fsdp", axis=0, tiled=True),
        lax.all_gather(k_cross, "fsdp", axis=0, tiled=True),
        lax.all_gather(v_cross, "fsdp", axis=0, tiled=True),
        lax.all_gather(o_cross, "fsdp", axis=0, tiled=True),
    )
    gain_cross_b, query_cross_b, key_cross_b, value_cross_b, out_cross_b = cross_back
    late_gradb = late_grad.astype(jnp.bfloat16)
    grad_out_cross = weight_grad(cross_context, late_gradb)
    cross_context_grad = back_project(late_gradb, out_cross_b).astype(jnp.bfloat16)
    cross_q_grad, cross_k_grad, cross_v_grad, cross_ds = attention_backward(
        cross_queries, cross_keys, cross_values, 0.0, cross_allowed, cross_total, cross_context_grad
    )
    grad_query_cross = weight_grad(normed_cross, cross_q_grad)
    grad_key_cross = weight_grad(enc_output, cross_k_grad)
    grad_value_cross = weight_grad(enc_output, cross_v_grad)
    enc_grad = (
        back_project(cross_k_grad, key_cross_b) + back_project(cross_v_grad, value_cross_b)
    ).astype(jnp.bfloat16)
    cross_in_grad = back_project(cross_q_grad, query_cross_b)
    norm_out, norm_pull = jax.vjp(rms_scale, middle, gain_cross_b.astype(jnp.float32))
    middle_part, grad_gain_cross = norm_pull(cross_in_grad)
    middle_grad = late_grad + middle_part
    cross_sums = (
        lax.psum_scatter(
            grad_gain_cross.astype(jnp.bfloat16), "fsdp", scatter_dimension=0, tiled=True
        ).astype(jnp.float32),
        lax.psum_scatter(
            grad_query_cross.astype(jnp.bfloat16), "fsdp", scatter_dimension=0, tiled=True
        ).astype(jnp.float32),
        lax.psum_scatter(
            grad_key_cross.astype(jnp.bfloat16), "fsdp", scatter_dimension=0, tiled=True
        ).astype(jnp.float32),
        lax.psum_scatter(
            grad_value_cross.astype(jnp.bfloat16), "fsdp", scatter_dimension=0, tiled=True
        ).astype(jnp.float32),
        lax.psum_scatter(
            grad_out_cross.astype(jnp.bfloat16), "fsdp", scatter_dimension=0, tiled=True
        ).astype(jnp.float32),
    )
    self_back = (
        lax.all_gather(norm_self, "fsdp", axis=0, tiled=True),
        lax.all_gather(q_self, "fsdp", axis=0, tiled=True),
        lax.all_gather(k_self, "fsdp", axis=0, tiled=True),
        lax.all_gather(v_self, "fsdp", axis=0, tiled=True),
        lax.all_gather(o_self, "fsdp", axis=0, tiled=True),
        lax.all_gather(rel_table, "fsdp", axis=0, tiled=True),
    )
    gain_self_b, query_self_b, key_self_b, value_self_b, out_self_b, table_pullback = self_back
    bias_pullback_fn = jnp.einsum(
        "oul,os->sul", bucket_indices, table_pullback, preferred_element_type=jnp.float32
    )
    middle_gradb = middle_grad.astype(jnp.bfloat16)
    grad_out_self = weight_grad(self_context, middle_gradb)
    self_context_grad = back_project(middle_gradb, out_self_b).astype(jnp.bfloat16)
    self_q_grad, self_k_grad, self_v_grad, self_score_gradient = attention_backward(
        self_queries,
        self_keys,
        self_values,
        bias_pullback_fn,
        self_allowed,
        self_total,
        self_context_grad,
    )
    table_gradient = jnp.einsum(
        "cgj,tugj->cu", bucket_indices, self_score_gradient, preferred_element_type=jnp.float32
    )
    grad_query_self = weight_grad(normed_self, self_q_grad)
    grad_key_self = weight_grad(normed_self, self_k_grad)
    grad_value_self = weight_grad(normed_self, self_v_grad)
    self_in_grad = (
        back_project(self_q_grad, query_self_b)
        + back_project(self_k_grad, key_self_b)
        + back_project(self_v_grad, value_self_b)
    )
    norm_out, norm_pull = jax.vjp(rms_scale, dec_float, gain_self_b.astype(jnp.float32))
    input_part, grad_gain_self = norm_pull(self_in_grad)
    input_grad = (middle_grad + input_part).astype(jnp.bfloat16)
    self_sums = (
        lax.psum_scatter(
            grad_gain_self.astype(jnp.bfloat16), "fsdp", scatter_dimension=0, tiled=True
        ).astype(jnp.float32),
        lax.psum_scatter(
            grad_query_self.astype(jnp.bfloat16), "fsdp", scatter_dimension=0, tiled=True
        ).astype(jnp.float32),
        lax.psum_scatter(
            grad_key_self.astype(jnp.bfloat16), "fsdp", scatter_dimension=0, tiled=True
        ).astype(jnp.float32),
        lax.psum_scatter(
            grad_value_self.astype(jnp.bfloat16), "fsdp", scatter_dimension=0, tiled=True
        ).astype(jnp.float32),
        lax.psum_scatter(
            grad_out_self.astype(jnp.bfloat16), "fsdp", scatter_dimension=0, tiled=True
        ).astype(jnp.float32),
        lax.psum_scatter(
            table_gradient.astype(jnp.bfloat16), "fsdp", scatter_dimension=0, tiled=True
        ).astype(jnp.float32),
    )
    summed = (
        lax.psum(self_sums[0].astype(jnp.bfloat16), "rep").astype(jnp.float32),
        lax.psum(self_sums[1].astype(jnp.bfloat16), "rep").astype(jnp.float32),
        lax.psum(self_sums[2].astype(jnp.bfloat16), "rep").astype(jnp.float32),
        lax.psum(self_sums[3].astype(jnp.bfloat16), "rep").astype(jnp.float32),
        lax.psum(self_sums[4].astype(jnp.bfloat16), "rep").astype(jnp.float32),
        lax.psum(self_sums[5].astype(jnp.bfloat16), "rep").astype(jnp.float32),
        lax.psum(cross_sums[0].astype(jnp.bfloat16), "rep").astype(jnp.float32),
        lax.psum(cross_sums[1].astype(jnp.bfloat16), "rep").astype(jnp.float32),
        lax.psum(cross_sums[2].astype(jnp.bfloat16), "rep").astype(jnp.float32),
        lax.psum(cross_sums[3].astype(jnp.bfloat16), "rep").astype(jnp.float32),
        lax.psum(cross_sums[4].astype(jnp.bfloat16), "rep").astype(jnp.float32),
        lax.psum(ffn_sums[0].astype(jnp.bfloat16), "rep").astype(jnp.float32),
        lax.psum(ffn_sums[1].astype(jnp.bfloat16), "rep").astype(jnp.float32),
        lax.psum(ffn_sums[2].astype(jnp.bfloat16), "rep").astype(jnp.float32),
        lax.psum(ffn_sums[3].astype(jnp.bfloat16), "rep").astype(jnp.float32),
    )
    return (
        dec_output,
        input_grad,
        enc_grad,
        summed[0],
        summed[1],
        summed[2],
        summed[3],
        summed[4],
        summed[5],
        summed[6],
        summed[7],
        summed[8],
        summed[9],
        summed[10],
        summed[11],
        summed[12],
        summed[13],
        summed[14],
    )


def solution(mesh):
    placed = (
        P(("rep", "fsdp"), None, None),
        P(("rep", "fsdp"), None, None),
        P(("rep", "fsdp"), None),
        P(("rep", "fsdp"), None),
        P(("rep", "fsdp"), None, None),
        P("fsdp"),
        P("fsdp", None),
        P("fsdp", None),
        P("fsdp", None),
        P("fsdp", None),
        P("fsdp", None),
        P("fsdp"),
        P("fsdp", None),
        P("fsdp", None),
        P("fsdp", None),
        P("fsdp", None),
        P("fsdp"),
        P("fsdp", None),
        P("fsdp", None),
        P("fsdp", None),
    )
    return jax.shard_map(
        shards,
        mesh=mesh,
        in_specs=placed,
        out_specs=(
            P(("rep", "fsdp"), None, None),
            P(("rep", "fsdp"), None, None),
            P(("rep", "fsdp"), None, None),
            P("fsdp"),
            P("fsdp", None),
            P("fsdp", None),
            P("fsdp", None),
            P("fsdp", None),
            P("fsdp", None),
            P("fsdp"),
            P("fsdp", None),
            P("fsdp", None),
            P("fsdp", None),
            P("fsdp", None),
            P("fsdp"),
            P("fsdp", None),
            P("fsdp", None),
            P("fsdp", None),
        ),
        check_vma=False,
    )
```

profile of v0, /device:TPU:0, one launch (start us, length us, event | category | flops | bytes accessed | tf_op | source)
XLA Modules:
  0.0 1422.0 jit_solution(5525499779942495843)
XLA Ops:
  17.1 23.6 %all-reduce.8 = (bf16[768]{0:T(1024)(128)(2,1)S(1)}, bf16[768]{0:T(1024)(128)(2,1)S(1)}, bf16[768]{0:T(1024)(128)(2,1)S(1)}) all-reduce(bf16[768]{0:T(1024)(128)(2,1)S(1)} %dynamic-update-slice, bf16[768]{0:T(1024)(128)(2,1)S(1)} %dynamic-update-slice.1, bf16[768]{0:T(1024)(128)(2,1)S(1)} %dynamic-update-slice.2), channel_id=1, replica_groups=mesh['rep'=4,'fsdp'=8] {'fsdp'}, use_global_device_ids=true, to_apply=%add | all-reduce | flops 2304 | bytes 9216
  41.0 16.3 %all-gather = bf16[8,4,12]{2,1,0:T(4,128)(2,1)S(1)} all-gather(bf16[1,4,12]{2,1,0:T(4,128)(2,1)S(1)} %bitcast.232), channel_id=1, replica_groups=mesh['rep'=4,'fsdp'=8] {'fsdp'}, dimensions={0}, use_global_device_ids=true | all-gather | bytes 864 | tf_op jit(solution)/shard_map/all_gather | solution.py:163
  70.6 25.7 %all-gather.17.cloned.1.call-done = bf16[768,768]{1,0:T(8,128)(2,1)} async-done(((bf16[96,768]{1,0:T(8,128)(2,1)}), bf16[768,768]{1,0:T(8,128)(2,1)}) %all-gather.17.cloned.1.call-update) | async-done | bytes 1179664 | tf_op jit(solution)/shard_map/all_gather | solution.py:160
  100.9 37.5 %all-gather.13.cloned.1.call-done = bf16[768,768]{1,0:T(8,128)(2,1)} async-done(((bf16[96,768]{1,0:T(8,128)(2,1)}), bf16[768,768]{1,0:T(8,128)(2,1)}) %all-gather.13.cloned.1.call-update) | async-done | bytes 1179664 | tf_op jit(solution)/shard_map/all_gather | solution.py:161
  143.9 36.3 %all-gather.21.cloned.1.call-done = bf16[768,768]{1,0:T(8,128)(2,1)} async-done(((bf16[96,768]{1,0:T(8,128)(2,1)}), bf16[768,768]{1,0:T(8,128)(2,1)}) %all-gather.21.cloned.1.call-update) | async-done | bytes 1179664 | tf_op jit(solution)/shard_map/all_gather | solution.py:188
  189.2 32.9 %all-gather.25.cloned.1.call-done = bf16[768,768]{1,0:T(8,128)(2,1)} async-done(((bf16[96,768]{1,0:T(8,128)(2,1)}), bf16[768,768]{1,0:T(8,128)(2,1)}) %all-gather.25.cloned.1.call-update) | async-done | bytes 1179664 | tf_op jit(solution)/shard_map/all_gather | solution.py:187
  240.0 24.1 %all-gather.19.cloned.1.call-done = bf16[768,768]{1,0:T(8,128)(2,1)} async-done(((bf16[96,768]{1,0:T(8,128)(2,1)}), bf16[768,768]{1,0:T(8,128)(2,1)}) %all-gather.19.cloned.1.call-update) | async-done | bytes 1179664 | tf_op jit(solution)/shard_map/all_gather | solution.py:162
  267.8 38.3 %all-gather.23.cloned.1.call-done = bf16[768,768]{1,0:T(8,128)(2,1)} async-done(((bf16[96,768]{1,0:T(8,128)(2,1)}), bf16[768,768]{1,0:T(8,128)(2,1)}) %all-gather.23.cloned.1.call-update) | async-done | bytes 1179664 | tf_op jit(solution)/shard_map/all_gather | solution.py:186
  326.0 22.1 %all-gather.27.cloned.1.call-done = bf16[768,768]{1,0:T(8,128)(2,1)} async-done(((bf16[96,768]{1,0:T(8,128)(2,1)}), bf16[768,768]{1,0:T(8,128)(2,1)}) %all-gather.27.cloned.1.call-update) | async-done | bytes 1179664 | tf_op jit(solution)/shard_map/all_gather | solution.py:189
  353.6 56.0 %all-gather.33.cloned.1.call-done = bf16[2048,768]{1,0:T(8,128)(2,1)} async-done(((bf16[256,768]{1,0:T(8,128)(2,1)}), bf16[2048,768]{1,0:T(8,128)(2,1)}) %all-gather.33.cloned.1.call-update) | async-done | bytes 3145744 | tf_op jit(solution)/shard_map/all_gather | solution.py:204
  409.6 6.0 fusion.23
  415.7 55.1 %all-gather.31.cloned.1.call-done = bf16[768,2048]{1,0:T(8,128)(2,1)} async-done(((bf16[96,2048]{1,0:T(8,128)(2,1)}), bf16[768,2048]{1,0:T(8,128)(2,1)}) %all-gather.31.cloned.1.call-update) | async-done | bytes 3145744 | tf_op jit(solution)/shard_map/all_gather | solution.py:203
  470.8 6.1 fusion.29
  476.8 55.2 %all-gather.29.cloned.1.call-done = bf16[768,2048]{1,0:T(8,128)(2,1)} async-done(((bf16[96,2048]{1,0:T(8,128)(2,1)}), bf16[768,2048]{1,0:T(8,128)(2,1)}) %all-gather.29.cloned.1.call-update) | async-done | bytes 3145744 | tf_op jit(solution)/shard_map/all_gather | solution.py:202
  532.1 9.9 fusion.18
  554.6 8.2 fusion.37
  562.8 14.0 multiply_reduce_fusion
  582.2 10.0 multiply_convert_fusion
  639.8 6.3 convert_reduce_fusion
  660.4 5.9 bitcast_convert_fusion
  692.1 34.7 %all-reduce.7 = (bf16[768]{0:T(1024)(128)(2,1)S(1)}, bf16[32,12]{1,0:T(8,128)(2,1)S(1)}, bf16[768]{0:T(1024)(128)(2,1)S(1)}, bf16[768]{0:T(1024)(128)(2,1)S(1)}) all-reduce(bf16[768]{0:T(1024)(128)(2,1)S(1)} %get-tuple-element.76, bf16[32,12]{1,0:T(8,128)(2,1)S(1)} %fusion.84, ...), channel_id=2, replica_groups=mesh['rep'=4,'fsdp'=8] {'fsdp'}, use_global_device_ids=true, to_apply=%region_13.14.clone | all-reduce | flops 2688 | bytes 10752
  738.1 39.5 %reduce-scatter.26.cloned.1.call-done = bf16[96,768]{1,0:T(8,128)(2,1)} async-done(((bf16[768,768]{1,0:T(8,128)(2,1)}), bf16[96,768]{1,0:T(8,128)(2,1)}) %reduce-scatter.26.cloned.1.call-update) | async-done | bytes 147472 | tf_op jit(solution)/shard_map/reduce_scatter | solution.py:282
  777.6 66.3 %reduce-scatter.22.cloned.1.call-done = bf16[96,768]{1,0:T(8,128)(2,1)} async-done(((bf16[768,768]{1,0:T(8,128)(2,1)}), bf16[96,768]{1,0:T(8,128)(2,1)}) %reduce-scatter.22.cloned.1.call-update) | async-done | bytes 147472 | tf_op jit(solution)/shard_map/reduce_scatter | solution.py:337
  843.9 66.2 %reduce-scatter.24.cloned.1.call-done = bf16[96,768]{1,0:T(8,128)(2,1)} async-done(((bf16[768,768]{1,0:T(8,128)(2,1)}), bf16[96,768]{1,0:T(8,128)(2,1)}) %reduce-scatter.24.cloned.1.call-update) | async-done | bytes 147472 | tf_op jit(solution)/shard_map/reduce_scatter | solution.py:273
  910.1 66.2 %reduce-scatter.20.cloned.1.call-done = bf16[96,768]{1,0:T(8,128)(2,1)} async-done(((bf16[768,768]{1,0:T(8,128)(2,1)}), bf16[96,768]{1,0:T(8,128)(2,1)}) %reduce-scatter.20.cloned.1.call-update) | async-done | bytes 147472 | tf_op jit(solution)/shard_map/reduce_scatter | solution.py:334
  976.3 66.3 %reduce-scatter.18.cloned.1.call-done = bf16[96,768]{1,0:T(8,128)(2,1)} async-done(((bf16[768,768]{1,0:T(8,128)(2,1)}), bf16[96,768]{1,0:T(8,128)(2,1)}) %reduce-scatter.18.cloned.1.call-update) | async-done | bytes 147472 | tf_op jit(solution)/shard_map/reduce_scatter | solution.py:331
  1042.6 66.4 %reduce-scatter.16.cloned.1.call-done = bf16[96,768]{1,0:T(8,128)(2,1)} async-done(((bf16[768,768]{1,0:T(8,128)(2,1)}), bf16[96,768]{1,0:T(8,128)(2,1)}) %reduce-scatter.16.cloned.1.call-update) | async-done | bytes 147472 | tf_op jit(solution)/shard_map/reduce_scatter | solution.py:328
  1109.1 77.0 %reduce-scatter.32.cloned.1.call-done = bf16[256,768]{1,0:T(8,128)(2,1)} async-done(((bf16[2048,768]{1,0:T(8,128)(2,1)}), bf16[256,768]{1,0:T(8,128)(2,1)}) %reduce-scatter.32.cloned.1.call-update) | async-done | bytes 393232 | tf_op jit(solution)/shard_map/reduce_scatter | solution.py:241
  1186.0 77.0 %reduce-scatter.28.cloned.1.call-done = bf16[96,2048]{1,0:T(8,128)(2,1)} async-done(((bf16[768,2048]{1,0:T(8,128)(2,1)}), bf16[96,2048]{1,0:T(8,128)(2,1)}) %reduce-scatter.28.cloned.1.call-update) | async-done | bytes 393232 | tf_op jit(solution)/shard_map/reduce_scatter | solution.py:235
  1263.0 77.2 %reduce-scatter.30.cloned.1.call-done = bf16[96,2048]{1,0:T(8,128)(2,1)} async-done(((bf16[768,2048]{1,0:T(8,128)(2,1)}), bf16[96,2048]{1,0:T(8,128)(2,1)}) %reduce-scatter.30.cloned.1.call-update) | async-done | bytes 393232 | tf_op jit(solution)/shard_map/reduce_scatter | solution.py:238
  1340.4 6.2 all-reduce.9
  1356.5 45.9 %all-reduce.13.cloned.1.call-done = (bf16[96,768]{0,1:T(8,128)(2,1)}, bf16[96,768]{0,1:T(8,128)(2,1)}, bf16[96,768]{1,0:T(8,128)(2,1)}, bf16[96,768]{1,0:T(8,128...) async-done(((bf16[96,768]{0,1:T(8,128)(2,1)}, ...) | async-done | bytes 2359312 | tf_op jit(solution)/shard_map/psum | solution.py:353
  (330 shorter events, 226.1 us)
Async XLA Ops:
  7.2 173.1 %copy-start = (bf16[3,512,768]{2,1,0:T(8,128)(2,1)S(1)}, bf16[3,512,768]{2,1,0:T(8,128)(2,1)}, u32[]{:S(2)}) copy-start(bf16[3,512,768]{2,1,0:T(8,128)(2,1)} %param.21) | copy-start | bytes 7077892
  7.3 58.0 %all-gather.15.cloned.1.call-start = ((), (), s32[]{:S(2)}) async-start(), calls=%async_computation.12 | async-start | bytes 1327104 | tf_op jit(solution)/shard_map/all_gather | solution.py:159
  8.0 88.3 %all-gather.17.cloned.1.call-start = ((), (), s32[]{:S(2)}) async-start(), calls=%async_computation.13 | async-start | bytes 1327104 | tf_op jit(solution)/shard_map/all_gather | solution.py:160
  8.8 48.5 %copy-start.60 = (s32[3,176]{1,0:T(4,128)S(1)}, s32[3,176]{1,0:T(4,128)}, u32[]{:S(2)}) copy-start(s32[3,176]{1,0:T(4,128)} %param.22) | copy-start | bytes 6340
  8.8 129.6 %all-gather.13.cloned.1.call-start = ((), (), s32[]{:S(2)}) async-start(), calls=%async_computation.11 | async-start | bytes 1327104 | tf_op jit(solution)/shard_map/all_gather | solution.py:161
  9.5 48.6 %copy-start.73 = (s32[3,512]{1,0:T(4,128)S(1)}, s32[3,512]{1,0:T(4,128)}, u32[]{:S(2)}) copy-start(s32[3,512]{1,0:T(4,128)} %param.23) | copy-start | bytes 18436
  9.5 170.8 %all-gather.21.cloned.1.call-start = ((), (), s32[]{:S(2)}) async-start(), calls=%async_computation.15 | async-start | bytes 1327104 | tf_op jit(solution)/shard_map/all_gather | solution.py:188
  10.1 212.1 %all-gather.25.cloned.1.call-start = ((), (), s32[]{:S(2)}) async-start(), calls=%async_computation.17 | async-start | bytes 1327104 | tf_op jit(solution)/shard_map/all_gather | solution.py:187
  10.7 253.4 %all-gather.19.cloned.1.call-start = ((), (), s32[]{:S(2)}) async-start(), calls=%async_computation.14 | async-start | bytes 1327104 | tf_op jit(solution)/shard_map/all_gather | solution.py:162
  11.2 294.8 %all-gather.23.cloned.1.call-start = ((), (), s32[]{:S(2)}) async-start(), calls=%async_computation.16 | async-start | bytes 1327104 | tf_op jit(solution)/shard_map/all_gather | solution.py:186
  12.0 336.2 %all-gather.27.cloned.1.call-start = ((), (), s32[]{:S(2)}) async-start(), calls=%async_computation.18 | async-start | bytes 1327104 | tf_op jit(solution)/shard_map/all_gather | solution.py:189
  12.7 396.9 %all-gather.33.cloned.1.call-start = ((), (), s32[]{:S(2)}) async-start(), calls=%async_computation.21 | async-start | bytes 3538944 | tf_op jit(solution)/shard_map/all_gather | solution.py:204
  13.5 457.3 %all-gather.31.cloned.1.call-start = ((), (), s32[]{:S(2)}) async-start(), calls=%async_computation.20 | async-start | bytes 3538944 | tf_op jit(solution)/shard_map/all_gather | solution.py:203
  14.1 518.0 %all-gather.29.cloned.1.call-start = ((), (), s32[]{:S(2)}) async-start(), calls=%async_computation.19 | async-start | bytes 3538944 | tf_op jit(solution)/shard_map/all_gather | solution.py:202
  14.8 719.9 %reduce-scatter.36.cloned.1.call-start = ((), (), s32[]{:S(2)}) async-start(), calls=%async_computation.32 | async-start | bytes 1327104
  15.1 46.6 %copy-start.46 = (s32[176,176]{1,0:T(8,128)}, s32[176,176]{1,0:T(8,128)S(1)}, u32[]{:S(2)}) copy-start(s32[176,176]{1,0:T(8,128)S(1)} %convert_add_fusion.1) | copy-start | bytes 371716
  40.7 265.4 %copy-start.67 = (f32[768]{0:T(1024)}, f32[768]{0:T(1024)S(1)}, u32[]{:S(2)}) copy-start(f32[768]{0:T(1024)S(1)} %convert_element_type.456) | copy-start | bytes 9220
  41.0 97.4 %copy-start.63 = (f32[3,176]{1,0:T(4,128)}, f32[3,176]{1,0:T(4,128)S(1)}, u32[]{:S(2)}) copy-start(f32[3,176]{1,0:T(4,128)S(1)} %fusion.105) | copy-start | bytes 6340
  100.8 130.5 %copy-start.8 = (bf16[3,176,768]{1,2,0:T(8,128)(2,1)}, bf16[3,176,768]{1,2,0:T(8,128)(2,1)S(1)}, u32[]{:S(2)}) copy-start(bf16[3,176,768]{1,2,0:T(8,128)(2,1)S(1)} %copy.108) | copy-start | bytes 2433028
  267.7 41.9 %copy-start.65 = (f32[3,176]{1,0:T(4,128)}, f32[3,176]{1,0:T(4,128)S(1)}, u32[]{:S(2)}) copy-start(f32[3,176]{1,0:T(4,128)S(1)} %get-tuple-element.109) | copy-start | bytes 6340
  267.8 38.3 %copy-start.69 = (f32[3,176]{1,0:T(4,128)}, f32[3,176]{1,0:T(4,128)S(1)}, u32[]{:S(2)}) copy-start(f32[3,176]{1,0:T(4,128)S(1)} %fusion.106) | copy-start | bytes 6340
  582.2 154.2 %reduce-scatter.34.cloned.1.call-start = ((), (), s32[]{:S(2)}) async-start(), calls=%async_computation.31 | async-start | bytes 1327104
  599.8 177.8 %reduce-scatter.26.cloned.1.call-start = ((), (), s32[]{:S(2)}) async-start(), calls=%async_computation.27 | async-start | bytes 1327104 | tf_op jit(solution)/shard_map/reduce_scatter | solution.py:282
  603.9 240.0 %reduce-scatter.22.cloned.1.call-start = ((), (), s32[]{:S(2)}) async-start(), calls=%async_computation.25 | async-start | bytes 1327104 | tf_op jit(solution)/shard_map/reduce_scatter | solution.py:337
  615.9 294.3 %reduce-scatter.24.cloned.1.call-start = ((), (), s32[]{:S(2)}) async-start(), calls=%async_computation.26 | async-start | bytes 1327104 | tf_op jit(solution)/shard_map/reduce_scatter | solution.py:273
  619.7 356.6 %reduce-scatter.20.cloned.1.call-start = ((), (), s32[]{:S(2)}) async-start(), calls=%async_computation.24 | async-start | bytes 1327104 | tf_op jit(solution)/shard_map/reduce_scatter | solution.py:334
  634.1 408.5 %reduce-scatter.18.cloned.1.call-start = ((), (), s32[]{:S(2)}) async-start(), calls=%async_computation.23 | async-start | bytes 1327104 | tf_op jit(solution)/shard_map/reduce_scatter | solution.py:331
  652.9 456.2 %reduce-scatter.16.cloned.1.call-start = ((), (), s32[]{:S(2)}) async-start(), calls=%async_computation.22 | async-start | bytes 1327104 | tf_op jit(solution)/shard_map/reduce_scatter | solution.py:328
  660.3 525.7 %reduce-scatter.32.cloned.1.call-start = ((), (), s32[]{:S(2)}) async-start(), calls=%async_computation.30 | async-start | bytes 3538944 | tf_op jit(solution)/shard_map/reduce_scatter | solution.py:241
  666.3 596.7 %reduce-scatter.28.cloned.1.call-start = ((), (), s32[]{:S(2)}) async-start(), calls=%async_computation.28 | async-start | bytes 3538944 | tf_op jit(solution)/shard_map/reduce_scatter | solution.py:235
  673.2 667.0 %reduce-scatter.30.cloned.1.call-start = ((), (), s32[]{:S(2)}) async-start(), calls=%async_computation.29 | async-start | bytes 3538944 | tf_op jit(solution)/shard_map/reduce_scatter | solution.py:238
  679.1 723.4 %all-reduce.13.cloned.1.call-start = ((), (), s32[]{:S(2)}) async-start(), calls=%async_computation.33 | async-start | bytes 4915200 | tf_op jit(solution)/shard_map/psum | solution.py:353
  (80 other events, 459.2 us)
Sparse Core Ops, SparseCore 0:
  10.3 43.9 all-gather.14
  56.5 39.7 all-gather.16
  98.5 39.8 all-gather.12
  140.4 39.8 all-gather.20
  182.3 39.8 all-gather.24
  224.2 39.8 all-gather.18
  266.2 39.8 all-gather.22
  308.3 39.8 all-gather.26
  350.4 59.2 all-gather.32
  411.7 59.0 all-gather.30
  473.0 59.0 all-gather.28
  582.3 62.6 reduce-scatter.35
  648.4 62.8 reduce-scatter.33
  714.5 63.0 reduce-scatter.25
  780.9 62.9 reduce-scatter.21
  847.1 62.9 reduce-scatter.23
  913.4 62.9 reduce-scatter.19
  979.6 63.0 reduce-scatter.17
  1046.0 62.9 reduce-scatter.15
  1112.5 73.5 reduce-scatter.31
  1189.6 73.3 reduce-scatter.27
  1266.6 73.5 reduce-scatter.29
  1343.9 58.4 all-reduce.12
where the time goes:
time: 1430 us; the launch traced here: 1420 us
  waiting for transfers between devices  1040 us (73%)
  matrix products  185 us (13%)
  blocking collectives  80.8 us (6%)
  local copies, waits for them, and re-layouts  56.1 us (4%)
  other arithmetic  42.5 us (3%)
  between operations  17.4 us (1%)
    reduce_scatter x1, waiting for transfers between devices, shards(): lax.psum_scatter(grad_up.astype(jnp.bfloat16), 'fsdp', scatter_dimension=...  77.2 us
    reduce_scatter x1, waiting for transfers between devices, shards(): lax.psum_scatter(grad_down.astype(jnp.bfloat16), 'fsdp', scatter_dimensio...  77 us
    reduce_scatter x1, waiting for transfers between devices, shards(): lax.psum_scatter(grad_gate.astype(jnp.bfloat16), 'fsdp', scatter_dimensio...  77 us
    reduce_scatter x1, waiting for transfers between devices, shards(): lax.psum_scatter(grad_query_self.astype(jnp.bfloat16), 'fsdp', scatter_di...  66.4 us
    reduce_scatter x1, waiting for transfers between devices, shards(): lax.psum_scatter(grad_key_self.astype(jnp.bfloat16), 'fsdp', scatter_dime...  66.3 us
    reduce_scatter x1, waiting for transfers between devices, shards(): lax.psum_scatter(grad_out_self.astype(jnp.bfloat16), 'fsdp', scatter_dime...  66.3 us
    reduce_scatter x1, waiting for transfers between devices, shards(): lax.psum_scatter(grad_query_cross.astype(jnp.bfloat16), 'fsdp', scatter_d...  66.2 us
    reduce_scatter x1, waiting for transfers between devices, shards(): lax.psum_scatter(grad_value_self.astype(jnp.bfloat16), 'fsdp', scatter_di...  66.2 us
  transfers between devices with their start and end apart: 23, of which 20 were waited for; matrix products, arithmetic and copies ran while one was open for 15% of the time, Pallas kernels for 0%

commit v1 on v0

v1 whole, which is shorter than its diff:
```python
import functools
import math

import jax
import jax.numpy as jnp
from jax import lax
from jax.experimental import pallas as pl
from jax.experimental.pallas import tpu as pltpu
from jax.sharding import PartitionSpec as P

HEADS = 12
HEAD = 64
BUCKETS = 32
MAXDIST = 128


norm_epsilon = 1e-06
masked_score = -1000000000.0


def bucket_of(distance):
    exact_part = BUCKETS // 2
    log_part = BUCKETS - exact_part
    bucket = jnp.minimum(distance, exact_part)
    for degree in range(1, log_part):
        threshold = math.ceil(exact_part * (MAXDIST / exact_part) ** (degree / log_part))
        bucket = bucket + (distance >= threshold).astype(jnp.int32)
    return bucket


def bucket_lookup_table(length):
    positions = jnp.arange(length, dtype=jnp.int32)
    distance = jnp.maximum(positions[:, None] - positions[None, :], 0)
    levels = jnp.arange(BUCKETS, dtype=jnp.int32)
    return (bucket_of(distance)[None] == levels[:, None, None]).astype(jnp.bfloat16)


PARTS = 4


def rms_scale(values, gain):
    return (
        values * lax.rsqrt(jnp.mean(values * values, axis=-1, keepdims=True) + norm_epsilon) * gain
    )


def gated(gate_values, up_values):
    return jax.nn.gelu(gate_values, approximate=True) * up_values

def project(values, matrix):
    return jnp.einsum("rld,de->rle", values, matrix, preferred_element_type=jnp.float32)


def weight_grad(values, grads):
    return jnp.einsum("rld,rle->de", values, grads, preferred_element_type=jnp.float32)


def back_project(grads, matrix):
    return jnp.einsum("rle,de->rld", grads, matrix, preferred_element_type=jnp.float32)


def split_heads(values):
    return values.reshape(values.shape[0], values.shape[1], HEADS, HEAD)


def attention_scores(query_vectors, key_vectors, relative_position_bias, allowed):
    scores = (
        jnp.einsum(
            "rqhd,rkhd->rhqk",
            split_heads(query_vectors),
            split_heads(key_vectors),
            preferred_element_type=jnp.float32,
        )
        + relative_position_bias
    )
    return jnp.where(allowed[:, None], scores, masked_score)


def attention_forward(query_vectors, key_vectors, value_vectors, relative_position_bias, allowed):
    scores = attention_scores(query_vectors, key_vectors, relative_position_bias, allowed)
    highest_score = jnp.max(scores, axis=-1, keepdims=True)
    expanded = jnp.exp(scores - highest_score)
    totals = jnp.sum(expanded, axis=-1, keepdims=True)
    attention_weights = (expanded / totals).astype(jnp.bfloat16)
    context = jnp.einsum(
        "rhqk,rkhd->rqhd",
        attention_weights,
        split_heads(value_vectors),
        preferred_element_type=jnp.float32,
    )
    return (
        context.reshape(query_vectors.shape).astype(jnp.bfloat16),
        highest_score + jnp.log(totals),
    )


def attention_backward(
    query_vectors,
    key_vectors,
    value_vectors,
    relative_position_bias,
    allowed,
    log_total,
    context_grad,
):
    scores = attention_scores(query_vectors, key_vectors, relative_position_bias, allowed)
    attention_weights = jnp.exp(scores - log_total)
    grad_heads = split_heads(context_grad)
    weight_grads = jnp.einsum(
        "rqhd,rkhd->rhqk",
        grad_heads,
        split_heads(value_vectors),
        preferred_element_type=jnp.float32,
    )
    row_dot = jnp.sum(attention_weights * weight_grads, axis=-1, keepdims=True)
    score_grads = (attention_weights * (weight_grads - row_dot)).astype(jnp.bfloat16)
    query_grads = jnp.einsum(
        "rhqk,rkhd->rqhd", score_grads, split_heads(key_vectors), preferred_element_type=jnp.float32
    )
    key_grads = jnp.einsum(
        "rhqk,rqhd->rkhd",
        score_grads,
        split_heads(query_vectors),
        preferred_element_type=jnp.float32,
    )
    value_grads = jnp.einsum(
        "rhqk,rqhd->rkhd",
        attention_weights.astype(jnp.bfloat16),
        grad_heads,
        preferred_element_type=jnp.float32,
    )
    return (
        query_grads.reshape(query_vectors.shape).astype(jnp.bfloat16),
        key_grads.reshape(key_vectors.shape).astype(jnp.bfloat16),
        value_grads.reshape(value_vectors.shape).astype(jnp.bfloat16),
        score_grads,
    )


CORE, ROW = [(i, i ^ 1) for i in range(4)], [(i, i ^ 2) for i in range(4)]
ACROSS, NEAR, FAR = (
    [(i, i ^ 1) for i in range(8)],
    [(i, i ^ 2) for i in range(8)],
    [(i, i ^ 4) for i in range(8)],
)


def over_core(values):
    return lax.ppermute(values, "rep", CORE)


def over_row(values):
    return lax.ppermute(values, "rep", ROW)


def over_across(values):
    return lax.ppermute(values, "fsdp", ACROSS)


def over_near(values):
    return lax.ppermute(values, "fsdp", NEAR)


def over_far(values):
    return lax.ppermute(values, "fsdp", FAR)


def pick(values, index, axis):
    return lax.dynamic_index_in_dim(values, index, axis, keepdims=False)


def place_pieces(position, pieces, by_shard):
    low, high = pieces[0].shape[2], pieces[2].shape[2]
    rows, columns = low + high, pieces[0].shape[3]
    shape = (8, PARTS, rows, columns) if by_shard else (PARTS, 8, rows, columns)

    def kernel(position_ref, *refs):
        sources, target, semaphores = refs[:8], refs[8], refs[9]
        part, shard = position_ref[0], position_ref[1]
        copies = []
        for core in range(2):
            for kind in range(4):
                for outer in range(2):
                    for inner in range(4):
                        if kind < 2:
                            row, across = kind, outer
                        else:
                            row, across = outer, kind - 2
                        to_part = part ^ (core + 2 * row)
                        to_shard = shard ^ (across + 4 * (inner & 1) + 2 * (inner >> 1))
                        start, size = (0, low) if kind < 2 else (low, high)
                        index = (to_shard, to_part) if by_shard else (to_part, to_shard)
                        copies.append(
                            pltpu.make_async_copy(
                                sources[core * 4 + kind].at[outer, inner],
                                target.at[index[0], index[1], pl.ds(start, size)],
                                semaphores.at[len(copies)],
                            )
                        )
        for copy in copies:
            copy.start()
        for copy in copies:
            copy.wait()

    return pl.pallas_call(
        kernel,
        out_shape=jax.ShapeDtypeStruct(shape, pieces[0].dtype),
        in_specs=[pl.BlockSpec(memory_space=pltpu.SMEM)]
        + [pl.BlockSpec(memory_space=pl.ANY)] * 8,
        out_specs=pl.BlockSpec(memory_space=pl.ANY),
        scratch_shapes=[pltpu.SemaphoreType.DMA((64,))],
    )(position, *pieces)


def gather_parts(parts, position, by_shard=False):
    held = pick(parts, position[0], 0)[None]
    held = jnp.concatenate([held, over_far(held)], 0)
    held = jnp.concatenate([held, over_near(held)], 0)
    half = held.shape[1] // 2
    first, second = held[:, :half], held[:, half:]
    first = jnp.stack([first, over_across(first)])
    second = jnp.stack([second, over_row(second)])
    pieces = [first, over_row(first), second, over_across(second)]
    pieces = pieces + [over_core(piece) for piece in pieces]
    return place_pieces(position, pieces, by_shard)


def gather_small(values, position):
    held = values[None]
    for bit, move in ((2, over_far), (1, over_near), (0, over_across)):
        other = move(held)
        mine = (position[1] >> bit) & 1
        held = jnp.where(mine == 0, jnp.stack([held, other], 1), jnp.stack([other, held], 1))
        held = held.reshape(-1, *values.shape)
    return held


def add_up(kept, received):
    return (kept.astype(jnp.float32) + received.astype(jnp.float32)).astype(jnp.bfloat16)


def scatter_parts(grads, position):
    part, shard = position[0], position[1]
    core, row = part & 1, part >> 1
    across, near, far = shard & 1, (shard >> 1) & 1, shard >> 2
    rows, columns = grads.shape[2], grads.shape[3]
    half = rows // 2
    grads = grads.astype(jnp.bfloat16).reshape(2, 2, 2, 2, 2, rows, columns)
    sums = add_up(pick(grads, core, 1), over_core(pick(grads, 1 - core, 1)))
    first, second = sums[..., :half, :], sums[..., half:, :]
    from_row, from_across = over_row(pick(first, 1 - row, 0)), over_across(pick(second, 1 - across, 3))
    first, second = add_up(pick(first, row, 0), from_row), add_up(pick(second, across, 3), from_across)
    from_across, from_row = over_across(pick(first, 1 - across, 2)), over_row(pick(second, 1 - row, 0))
    first, second = add_up(pick(first, across, 2), from_across), add_up(pick(second, row, 0), from_row)
    sums = jnp.concatenate([first, second], 2)
    sums = add_up(pick(sums, near, 1), over_near(pick(sums, 1 - near, 1)))
    sums = add_up(pick(sums, far, 0), over_far(pick(sums, 1 - far, 0)))
    other = over_row(sums)
    both = jnp.where(row == 0, jnp.stack([sums, other]), jnp.stack([other, sums]))
    others = over_core(both)
    return jnp.where(core == 0, jnp.stack([both, others], 1), jnp.stack([others, both], 1)).reshape(PARTS, rows, columns).astype(jnp.float32)


def total_small(values):
    for move in (over_core, over_row, over_across, over_near, over_far):
        values = values + move(values)
    return values


def shards(
    fast,
    dec_input,
    enc_output,
    dec_segments,
    enc_segments,
    cotangent,
    norm_self,
    q_self,
    k_self,
    v_self,
    o_self,
    rel_table,
    norm_cross,
    q_cross,
    k_cross,
    v_cross,
    o_cross,
    norm_ffn,
    wi_gate,
    wi_up,
    wo_ffn,
):
    gain_rows = norm_self.shape[0]
    table_rows = rel_table.shape[0]
    width = wi_gate.shape[1] // PARTS
    position = jnp.stack([lax.axis_index("rep"), lax.axis_index("fsdp")]).astype(jnp.int32)
    self_parts = jnp.stack([q_self, k_self, v_self, o_self])
    cross_parts = jnp.stack([q_cross, k_cross, v_cross, o_cross])
    inner_parts = jnp.stack(
        [
            jnp.concatenate(
                [wi_gate[:, i * width : (i + 1) * width], wi_up[:, i * width : (i + 1) * width]], 1
            )
            for i in range(PARTS)
        ]
    )
    small = jnp.concatenate([norm_self, norm_cross, norm_ffn, rel_table.reshape(-1)])
    if fast:
        small_all = gather_small(small, position)
        self_matrices = gather_parts(self_parts, position).reshape(PARTS, -1, self_parts.shape[2])
        cross_matrices = gather_parts(cross_parts, position).reshape(PARTS, -1, cross_parts.shape[2])
        inner = gather_parts(inner_parts, position).reshape(PARTS, -1, 2 * width)
        down_parts = wo_ffn.reshape(PARTS, -1, wo_ffn.shape[1])
        down_matrix = gather_parts(down_parts, position, True).reshape(-1, wo_ffn.shape[1])
    else:
        small_all = lax.all_gather(small, "fsdp", axis=0)
        self_matrices = lax.all_gather(self_parts, "fsdp", axis=1, tiled=True)
        cross_matrices = lax.all_gather(cross_parts, "fsdp", axis=1, tiled=True)
        inner = lax.all_gather(inner_parts, "fsdp", axis=1, tiled=True)
        down_matrix = lax.all_gather(wo_ffn, "fsdp", axis=0, tiled=True)
    gain_self = small_all[:, :gain_rows].reshape(-1)
    gain_cross = small_all[:, gain_rows : 2 * gain_rows].reshape(-1)
    gain_ffn = small_all[:, 2 * gain_rows : 3 * gain_rows].reshape(-1)
    self_bias_table = small_all[:, 3 * gain_rows :].reshape(BUCKETS, HEADS)
    query_self, key_self, value_self, out_self = (self_matrices[i] for i in range(4))
    query_cross, key_cross, value_cross, out_cross = (cross_matrices[i] for i in range(4))

    decoder_length = dec_input.shape[1]
    bucket_indices = bucket_lookup_table(decoder_length)
    positions = jnp.arange(decoder_length, dtype=jnp.int32)
    causal = positions[:, None] >= positions[None, :]
    self_allowed = (dec_segments[:, :, None] == dec_segments[:, None, :]) & causal[None]
    cross_allowed = dec_segments[:, :, None] == enc_segments[:, None, :]
    relative_position_bias = jnp.einsum(
        "oul,os->sul", bucket_indices, self_bias_table, preferred_element_type=jnp.float32
    )
    dec_float = dec_input.astype(jnp.float32)
    normed_self = rms_scale(dec_float, gain_self.astype(jnp.float32)).astype(jnp.bfloat16)
    self_queries = project(normed_self, query_self).astype(jnp.bfloat16)
    self_keys = project(normed_self, key_self).astype(jnp.bfloat16)
    self_values = project(normed_self, value_self).astype(jnp.bfloat16)
    self_context, self_total = attention_forward(
        self_queries, self_keys, self_values, relative_position_bias, self_allowed
    )
    middle = dec_float + project(self_context, out_self)
    normed_cross = rms_scale(middle, gain_cross.astype(jnp.float32)).astype(jnp.bfloat16)
    cross_queries = project(normed_cross, query_cross).astype(jnp.bfloat16)
    cross_keys = project(enc_output, key_cross).astype(jnp.bfloat16)
    cross_values = project(enc_output, value_cross).astype(jnp.bfloat16)
    cross_context, cross_total = attention_forward(
        cross_queries, cross_keys, cross_values, 0.0, cross_allowed
    )
    late = middle + project(cross_context, out_cross)
    normed_ffn = rms_scale(late, gain_ffn.astype(jnp.float32)).astype(jnp.bfloat16)

    inner_values = jnp.einsum(
        "rld,pde->prle", normed_ffn, inner, preferred_element_type=jnp.float32
    )
    gate_values, up_values = inner_values[..., :width], inner_values[..., width:]
    hidden = gated(gate_values, up_values).astype(jnp.bfloat16)
    down_blocks = down_matrix.reshape(PARTS, width, -1)
    dec_output = (
        late
        + jnp.einsum("prle,ped->rld", hidden, down_blocks, preferred_element_type=jnp.float32)
    ).astype(jnp.bfloat16)

    grad_down = jnp.einsum(
        "prle,rld->ped", hidden, cotangent, preferred_element_type=jnp.float32
    )
    hidden_grad = jnp.einsum(
        "rld,ped->prle", cotangent, down_blocks, preferred_element_type=jnp.float32
    )
    gated_out, gated_pull = jax.vjp(gated, gate_values, up_values)
    gate_grad, up_grad = gated_pull(hidden_grad)
    inner_back = jnp.concatenate([gate_grad, up_grad], -1).astype(jnp.bfloat16)
    grad_inner = jnp.einsum(
        "rld,prle->pde", normed_ffn, inner_back, preferred_element_type=jnp.float32
    )
    ffn_in_grad = jnp.einsum("prle,pde->rld", inner_back, inner, preferred_element_type=jnp.float32)
    norm_out, norm_pull = jax.vjp(rms_scale, late, gain_ffn.astype(jnp.float32))
    late_part, grad_gain_ffn = norm_pull(ffn_in_grad)
    late_grad = cotangent.astype(jnp.float32) + late_part

    late_gradb = late_grad.astype(jnp.bfloat16)
    grad_out_cross = weight_grad(cross_context, late_gradb)
    cross_context_grad = back_project(late_gradb, out_cross).astype(jnp.bfloat16)
    cross_q_grad, cross_k_grad, cross_v_grad, cross_ds = attention_backward(
        cross_queries, cross_keys, cross_values, 0.0, cross_allowed, cross_total, cross_context_grad
    )
    grad_query_cross = weight_grad(normed_cross, cross_q_grad)
    grad_key_cross = weight_grad(enc_output, cross_k_grad)
    grad_value_cross = weight_grad(enc_output, cross_v_grad)
    enc_grad = (
        back_project(cross_k_grad, key_cross) + back_project(cross_v_grad, value_cross)
    ).astype(jnp.bfloat16)
    cross_in_grad = back_project(cross_q_grad, query_cross)
    norm_out, norm_pull = jax.vjp(rms_scale, middle, gain_cross.astype(jnp.float32))
    middle_part, grad_gain_cross = norm_pull(cross_in_grad)
    middle_grad = late_grad + middle_part

    middle_gradb = middle_grad.astype(jnp.bfloat16)
    grad_out_self = weight_grad(self_context, middle_gradb)
    self_context_grad = back_project(middle_gradb, out_self).astype(jnp.bfloat16)
    self_q_grad, self_k_grad, self_v_grad, self_score_gradient = attention_backward(
        self_queries,
        self_keys,
        self_values,
        relative_position_bias,
        self_allowed,
        self_total,
        self_context_grad,
    )
    table_gradient = jnp.einsum(
        "cgj,tugj->cu", bucket_indices, self_score_gradient, preferred_element_type=jnp.float32
    )
    grad_query_self = weight_grad(normed_self, self_q_grad)
    grad_key_self = weight_grad(normed_self, self_k_grad)
    grad_value_self = weight_grad(normed_self, self_v_grad)
    self_in_grad = (
        back_project(self_q_grad, query_self)
        + back_project(self_k_grad, key_self)
        + back_project(self_v_grad, value_self)
    )
    norm_out, norm_pull = jax.vjp(rms_scale, dec_float, gain_self.astype(jnp.float32))
    input_part, grad_gain_self = norm_pull(self_in_grad)
    input_grad = (middle_grad + input_part).astype(jnp.bfloat16)

    self_grads = jnp.stack(
        [
            g.astype(jnp.bfloat16)
            for g in (grad_query_self, grad_key_self, grad_value_self, grad_out_self)
        ]
    )
    cross_grads = jnp.stack(
        [
            g.astype(jnp.bfloat16)
            for g in (grad_query_cross, grad_key_cross, grad_value_cross, grad_out_cross)
        ]
    )
    inner_grads = grad_inner.astype(jnp.bfloat16)
    down_grads = grad_down.reshape(-1, grad_down.shape[2]).astype(jnp.bfloat16)
    count = grad_gain_self.shape[0] // gain_rows
    small_grads = jnp.concatenate(
        [
            grad_gain_self.reshape(count, -1),
            grad_gain_cross.reshape(count, -1),
            grad_gain_ffn.reshape(count, -1),
            table_gradient.reshape(count, -1),
        ],
        1,
    )
    if fast:
        split = lambda g: g.reshape(PARTS, 8, -1, g.shape[2])
        down_split = down_grads.reshape(8, PARTS, -1, down_grads.shape[1]).transpose(1, 0, 2, 3)
        down_sum = scatter_parts(down_split, position).reshape(wo_ffn.shape)
        inner_sum = scatter_parts(split(inner_grads), position)
        cross_sum = scatter_parts(split(cross_grads), position)
        self_sum = scatter_parts(split(self_grads), position)
        small_sum = pick(total_small(small_grads), position[1], 0)
    else:
        reduce = lambda g, d: lax.psum(
            lax.psum_scatter(g, "fsdp", scatter_dimension=d, tiled=True), "rep"
        ).astype(jnp.float32)
        down_sum = reduce(down_grads, 0)
        inner_sum = reduce(inner_grads, 1)
        cross_sum = reduce(cross_grads, 1)
        self_sum = reduce(self_grads, 1)
        small_sum = reduce(small_grads.reshape(-1), 0)
    gate_sum = inner_sum[:, :, :width].transpose(1, 0, 2).reshape(wi_gate.shape)
    up_sum = inner_sum[:, :, width:].transpose(1, 0, 2).reshape(wi_up.shape)
    return (
        dec_output,
        input_grad,
        enc_grad,
        small_sum[:gain_rows],
        self_sum[0],
        self_sum[1],
        self_sum[2],
        self_sum[3],
        small_sum[3 * gain_rows :].reshape(table_rows, HEADS),
        small_sum[gain_rows : 2 * gain_rows],
        cross_sum[0],
        cross_sum[1],
        cross_sum[2],
        cross_sum[3],
        small_sum[2 * gain_rows : 3 * gain_rows],
        gate_sum,
        up_sum,
        down_sum,
    )


def solution(mesh):
    placed = (
        P(("rep", "fsdp"), None, None),
        P(("rep", "fsdp"), None, None),
        P(("rep", "fsdp"), None),
        P(("rep", "fsdp"), None),
        P(("rep", "fsdp"), None, None),
        P("fsdp"),
        P("fsdp", None),
        P("fsdp", None),
        P("fsdp", None),
        P("fsdp", None),
        P("fsdp", None),
        P("fsdp"),
        P("fsdp", None),
        P("fsdp", None),
        P("fsdp", None),
        P("fsdp", None),
        P("fsdp"),
        P("fsdp", None),
        P("fsdp", None),
        P("fsdp", None),
    )
    fast = mesh.shape["rep"] == 4 and mesh.shape["fsdp"] == 8
    return jax.shard_map(
        functools.partial(shards, fast),
        mesh=mesh,
        in_specs=placed,
        out_specs=(
            P(("rep", "fsdp"), None, None),
            P(("rep", "fsdp"), None, None),
            P(("rep", "fsdp"), None, None),
            P("fsdp"),
            P("fsdp", None),
            P("fsdp", None),
            P("fsdp", None),
            P("fsdp", None),
            P("fsdp", None),
            P("fsdp"),
            P("fsdp", None),
            P("fsdp", None),
            P("fsdp", None),
            P("fsdp", None),
            P("fsdp"),
            P("fsdp", None),
            P("fsdp", None),
            P("fsdp", None),
        ),
        check_vma=False,
    )
```

time: 1430 us -> 1100 us (0.77)
  waiting for transfers between devices: 1040 us -> 157 us
  Pallas kernels: 0 us -> 581 us
  blocking collectives: 80.8 us -> 0 us
  starting transfers between devices: 1.71 us -> 58.5 us
  matrix products: 185 us -> 157 us
  other arithmetic: 42.5 us -> 64.6 us
  between operations: 17.4 us -> 2.94 us
  local copies, waits for them, and re-layouts: 56.1 us -> 70.4 us
    reduce_scatter x9 -> x0, waiting for transfers between devices: 602 us -> none  [the longest x1 77.2 us: shards(): lax.psum_scatter(grad_up.astype(jnp.bfloat16), 'fsdp', scatter_dimension=...]
    pallas_call x0 -> x4, Pallas kernels: none -> 581 us  [place_pieces(): pl.pallas_call(kernel, out_shape=jax.ShapeDtypeStruct(shape, pieces[0].dt...]
    all_gather x11 -> x0, waiting for transfers between devices: 383 us -> none  [the longest x1 56 us: shards(): lax.all_gather(wo_ffn, 'fsdp', axis=0, tiled=True)]
    ppermute x0 -> x84, waiting for transfers between devices: none -> 157 us  [the longest x21 47.8 us: over_row(): return lax.ppermute(values, 'rep', ROW)]
    ppermute x0 -> x84, starting transfers between devices: none -> 58.5 us  [the longest x21 21.6 us: over_row(): return lax.ppermute(values, 'rep', ROW)]
    unnamed x2 -> x0, blocking collectives: 58.3 us -> none
    psum x1 -> x0, waiting for transfers between devices: 45.9 us -> none  [shards(): lax.psum(cross_sums[2].astype(jnp.bfloat16), 'rep').astype(jnp.float32)]
    dot_general x0 -> x6, matrix products: none -> 34.6 us  [the longest x1 7.71 us: shards(): jnp.einsum('rld,pde->prle', normed_ffn, inner, preferred_element_type=jnp...]
  transfers between devices with their start and end apart: 23 -> 84, of which waited for: 20 -> 42; matrix products, arithmetic and copies ran while one was open for 15% -> 13% of each run, Pallas kernels for 0% -> 36%
where the time goes in v1:
time: 1100 us; the launch traced here: 1090 us
  Pallas kernels  581 us (53%)
  waiting for transfers between devices  157 us (14%)
  matrix products  157 us (14%)
  local copies, waits for them, and re-layouts  70.4 us (6%)
  other arithmetic  64.6 us (6%)
  starting transfers between devices  58.5 us (5%)
    pallas_call x4, Pallas kernels, place_pieces(): pl.pallas_call(kernel, out_shape=jax.ShapeDtypeStruct(shape, pieces[0].dt...  581 us
    ppermute x21, waiting for transfers between devices, over_row(): return lax.ppermute(values, 'rep', ROW)  47.8 us
    ppermute x18, waiting for transfers between devices, over_across(): return lax.ppermute(values, 'fsdp', ACROSS)  45 us
    ppermute x10, waiting for transfers between devices, over_near(): return lax.ppermute(values, 'fsdp', NEAR)  35.2 us
    ppermute x10, waiting for transfers between devices, over_far(): return lax.ppermute(values, 'fsdp', FAR)  28.1 us
    dot_general x8, matrix products, back_project(): jnp.einsum('rle,de->rld', grads, matrix, preferred_element_type=jnp.float32)  25.4 us
  transfers between devices with their start and end apart: 84, of which 42 were waited for; matrix products, arithmetic and copies ran while one was open for 13% of the time, Pallas kernels for 36%

profile of v1, /device:TPU:0, one launch (start us, length us, event | category | flops | bytes accessed | tf_op | source)
XLA Modules:
  0.0 1091.7 jit_solution(611133079591828843)
XLA Ops:
  42.6 10.0 collective-permute-done.4
  68.8 10.5 collective-permute-done.17
  86.6 5.1 collective-permute-done.38.refs_3_
  105.4 4.6 collective-permute-done.16.refs_1_
  110.6 4.7 collective-permute-done.18.refs_3_
  135.0 97.6 %shard_map.334 = bf16[8,4,64,768]{3,2,1,0:T(8,128)(2,1)} custom-call(s32[2]{0:T(128)} %pad_add_fusion.position_ref, bf16[2,4,32,768]{3,2,1,0:T(8,128)(2,1)} %copy-done.40, bf16[2,4,32,768]{3,2,1,0:T(8,128)(2,1)} %collective-permute-done.36.refs_1_, bf16[2,4,32,768]{3,2,1,0:T(8,128)(2,1)} %pad_maximum_fusion.17.refs_2_, ...), custom_call_target="tpu_custom_call" | custom-call | tf_op jit(solution)/shard_map/pallas_call | solution.py:205
  232.7 145.3 %shard_map.332 = bf16[4,8,96,768]{3,2,1,0:T(8,128)(2,1)} custom-call(s32[2]{0:T(128)} %pad_add_fusion.position_ref, bf16[2,4,48,768]{3,2,1,0:T(8,128)(2,1)} %pad_maximum_fusion.12.refs_0_, bf16[2,4,48,768]{3,2,1,0:T(8,128)(2,1)} %collective-permute-done.16.refs_1_, bf16[2,4,48,768]{3,2,1,0:T(8,128)(2,1)} %pad_maximum_fusion.13.refs_2_, ...), custom_call_target="tpu_custom_call" | custom-call | tf_op jit(solution)/shard_map/pallas_call | solution.py:205
  378.0 4.6 fusion.153
  383.6 145.3 %shard_map.331 = bf16[4,8,96,768]{3,2,1,0:T(8,128)(2,1)} custom-call(s32[2]{0:T(128)} %pad_add_fusion.position_ref, bf16[2,4,48,768]{3,2,1,0:T(8,128)(2,1)} %pad_maximum_fusion.9.refs_0_, bf16[2,4,48,768]{3,2,1,0:T(8,128)(2,1)} %collective-permute-done.6.refs_1_, bf16[2,4,48,768]{3,2,1,0:T(8,128)(2,1)} %pad_maximum_fusion.10.refs_2_, ...), custom_call_target="tpu_custom_call" | custom-call | tf_op jit(solution)/shard_map/pallas_call | solution.py:205
  549.3 4.9 convolution_convert_fusion
  586.0 192.9 %shard_map.333 = bf16[4,8,96,1024]{3,2,1,0:T(8,128)(2,1)} custom-call(s32[2]{0:T(128)} %pad_add_fusion.position_ref, bf16[2,4,48,1024]{3,2,1,0:T(8,128)(2,1)} %pad_maximum_fusion.6.refs_0_, bf16[2,4,48,1024]{3,2,1,0:T(8,128)(2,1)} %collective-permute-done.26.refs_1_, bf16[2,4,48,1024]{3,2,1,0:T(8,128)(2,1)} %pad_maximum_fusion.7.refs_2_, ...), custom_call_target="tpu_custom_call" | custom-call | tf_op jit(solution)/shard_map/pallas_call | solution.py:205
  779.0 7.7 convolution_bitcast_fusion
  786.8 6.7 fusion.21
  793.5 6.0 fusion.44
  805.1 7.4 bitcast_convert_fusion
  822.0 8.0 fusion.31
  834.5 6.6 fusion.164
  841.2 8.9 multiply_reduce_fusion
  850.1 6.9 multiply_convert_fusion
  873.6 5.2 fusion.49
  878.8 7.9 multiply_reduce_fusion.1
  886.6 6.4 convert_reduce_fusion
  906.3 5.8 constant_dynamic-slice_fusion.3
  933.6 5.2 fusion.37
  969.1 4.5 collective-permute-done.76
  993.0 5.3 collective-permute-done.81
  998.6 4.5 collective-permute-done.82
  1008.2 11.2 %collective-permute-done.51 = bf16[2,2,2,48,768]{4,3,2,1,0:T(8,128)(2,1)S(1)} collective-permute-done((bf16[2,2,2,48,768]{4,3,2,1,0:T(8,128)(2,1)S(1)}, bf16[2,2,2,48,768]{4,3,2,1,0:T(8,128)(2,1)S(1)}, u32[]{:S(2)}, u32[]{:S(2)}) %collective-permute-start.51) | collective-permute-done | bytes 589856 | tf_op jit(solution)/shard_map/ppermute | solution.py:157
  1036.9 7.8 collective-permute-done.53
  1054.2 6.0 collective-permute-done.68
  1065.2 7.1 collective-permute-done.71
  1073.0 8.2 collective-permute-done.72
  (577 shorter events, 319.8 us)
Async XLA Ops:
  7.4 19.1 %collective-permute-start.33 = (bf16[1,64,768]{2,1,0:T(8,128)(2,1)S(1)}, bf16[1,64,768]{2,1,0:T(8,128)(2,1)}, u32[]{:S(2)}, u32[]{:S(2)}) collective-permute-start(bf16[1,64,768]{2,1,0:T(8,128)(2,1)S(1)} %constant_dynamic-slice_fusion.9), channel_id=1, source_target_pairs={{0,4},{1,5},{2,6},{3,7},{4,0},{5,1},{6,2},{7,3},{8,12},{9,13},{10,... | collective-permute-start | bytes 294920 | tf_op jit(solution)/shard_map/ppermute | solution.py:165
  8.5 21.1 %collective-permute-start.13 = (bf16[1,96,768]{2,1,0:T(8,128)(2,1)S(1)}, bf16[1,96,768]{2,1,0:T(8,128)(2,1)S(1)}, u32[]{:S(2)}, u32[]{:S(2)}) collective-permute-start(bf16[1,96,768]{2,1,0:T(8,128)(2,1)S(1)} %fusion.132), channel_id=1, source_target_pairs={{0,4},{1,5},{2,6},{3,7},{4,0},{5,1},{6,2},{7,3},{8,12},{9,13},{10,... | collective-permute-start | bytes 442376 | tf_op jit(solution)/shard_map/ppermute | solution.py:165
  12.5 20.3 %collective-permute-start.3 = (bf16[1,96,768]{2,1,0:T(8,128)(2,1)S(1)}, bf16[1,96,768]{2,1,0:T(8,128)(2,1)}, u32[]{:S(2)}, u32[]{:S(2)}) collective-permute-start(bf16[1,96,768]{2,1,0:T(8,128)(2,1)S(1)} %fusion.135), channel_id=1, source_target_pairs={{0,4},{1,5},{2,6},{3,7},{4,0},{5,1},{6,2},{7,3},{8,12},{9,13},{10,... | collective-permute-start | bytes 442376 | tf_op jit(solution)/shard_map/ppermute | solution.py:165
  12.9 22.9 %collective-permute-start.23 = (bf16[1,96,1024]{2,1,0:T(8,128)(2,1)S(1)}, bf16[1,96,1024]{2,1,0:T(8,128)(2,1)S(1)}, u32[]{:S(2)}, u32[]{:S(2)}) collective-permute-start(bf16[1,96,1024]{2,1,0:T(8,128)(2,1)S(1)} %fusion.112), channel_id=1, source_target_pairs={{0,4},{1,5},{2,6},{3,7},{4,0},{5,1},{6,2},{7,3},{8,12},{9,13},{10,... | collective-permute-start | bytes 589832 | tf_op jit(solution)/shard_map/ppermute | solution.py:165
  21.5 39.5 %collective-permute-start.2 = (bf16[4,336]{1,0:T(4,128)(2,1)S(1)}, bf16[4,336]{1,0:T(4,128)(2,1)S(1)}, u32[]{:S(2)}, u32[]{:S(2)}) collective-permute-start(bf16[4,336]{1,0:T(4,128)(2,1)S(1)} %select_n.291), channel_id=1, source_target_pairs={{0,1},{1,0},{2,3},{3,2},{4,5},{5,4},{6,7},{7,6},{8,9},{9,8},{10,11... | collective-permute-start | bytes 8072 | tf_op jit(solution)/shard_map/ppermute | solution.py:157
  29.6 26.5 %collective-permute-start.14 = (bf16[2,96,768]{2,1,0:T(8,128)(2,1)S(1)}, bf16[2,96,768]{2,1,0:T(8,128)(2,1)S(1)}, u32[]{:S(2)}, u32[]{:S(2)}) collective-permute-start(bf16[2,96,768]{2,1,0:T(8,128)(2,1)S(1)} %pad_maximum_fusion.19), channel_id=1, source_target_pairs={{0,2},{1,3},{2,0},{3,1},{4,6},{5,7},{6,4},{7,5},{8,10},{9,11},{10,... | collective-permute-start | bytes 884744 | tf_op jit(solution)/shard_map/ppermute | solution.py:161
  33.7 18.9 %collective-permute-start.4 = (bf16[2,96,768]{2,1,0:T(8,128)(2,1)S(1)}, bf16[2,96,768]{2,1,0:T(8,128)(2,1)S(1)}, u32[]{:S(2)}, u32[]{:S(2)}) collective-permute-start(bf16[2,96,768]{2,1,0:T(8,128)(2,1)S(1)} %pad_maximum_fusion.18), channel_id=1, source_target_pairs={{0,2},{1,3},{2,0},{3,1},{4,6},{5,7},{6,4},{7,5},{8,10},{9,11},{10,... | collective-permute-start | bytes 884744 | tf_op jit(solution)/shard_map/ppermute | solution.py:161
  35.9 27.6 %collective-permute-start.24 = (bf16[2,96,1024]{2,1,0:T(8,128)(2,1)S(1)}, bf16[2,96,1024]{2,1,0:T(8,128)(2,1)S(1)}, u32[]{:S(2)}, u32[]{:S(2)}) collective-permute-start(bf16[2,96,1024]{2,1,0:T(8,128)(2,1)S(1)} %pad_maximum_fusion.14), channel_id=1, source_target_pairs={{0,2},{1,3},{2,0},{3,1},{4,6},{5,7},{6,4},{7,5},{8,10},{9,11},{10,... | collective-permute-start | bytes 1179656 | tf_op jit(solution)/shard_map/ppermute | solution.py:161
  41.1 20.0 %collective-permute-start.37 = (bf16[4,32,768]{2,1,0:T(8,128)(2,1)S(1)}, bf16[4,32,768]{2,1,0:T(8,128)(2,1)S(1)}, u32[]{:S(2)}, u32[]{:S(2)}) collective-permute-start(bf16[4,32,768]{2,1,0:T(8,128)(2,1)S(1)} %get-tuple-element.78), channel_id=1, source_target_pairs={{0,16},{8,24},{16,0},{24,8},{1,17},{9,25},{17,1},{25,9},{2,18},{10... | collective-permute-start | bytes 589832 | tf_op jit(solution)/shard_map/ppermute | solution.py:153
  61.0 20.5 %collective-permute-start.39 = (bf16[2,4,32,768]{3,2,1,0:T(8,128)(2,1)S(1)}, bf16[2,4,32,768]{3,2,1,0:T(8,128)(2,1)S(1)}, u32[]{:S(2)}, u32[]{:S(2)}) collective-permute-start(bf16[2,4,32,768]{3,2,1,0:T(8,128)(2,1)S(1)} %pad_maximum_fusion.16.refs_0_), channel_id=1, source_target_pairs={{0,8},{8,0},{16,24},{24,16},{1,9},{9,1},{17,25},{25,17},{2,10},{10... | collective-permute-start | bytes 1179656 | tf_op jit(solution)/shard_map/ppermute | solution.py:149
  61.1 21.9 %collective-permute-start.36 = (bf16[2,4,32,768]{3,2,1,0:T(8,128)(2,1)S(1)}, bf16[2,4,32,768]{3,2,1,0:T(8,128)(2,1)}, u32[]{:S(2)}, u32[]{:S(2)}) collective-permute-start(bf16[2,4,32,768]{3,2,1,0:T(8,128)(2,1)S(1)} %pad_maximum_fusion.16.refs_0_), channel_id=1, source_target_pairs={{0,16},{8,24},{16,0},{24,8},{1,17},{9,25},{17,1},{25,9},{2,18},{10... | collective-permute-start | bytes 1179656 | tf_op jit(solution)/shard_map/ppermute | solution.py:153
  101.2 18.2 %collective-permute-start.9 = (bf16[2,4,48,768]{3,2,1,0:T(8,128)(2,1)}, bf16[2,4,48,768]{3,2,1,0:T(8,128)(2,1)}, u32[]{:S(2)}, u32[]{:S(2)}) collective-permute-start(bf16[2,4,48,768]{3,2,1,0:T(8,128)(2,1)} %pad_maximum_fusion.9.refs_0_), channel_id=1, source_target_pairs={{0,8},{8,0},{16,24},{24,16},{1,9},{9,1},{17,25},{25,17},{2,10},{10... | collective-permute-start | bytes 1769480 | tf_op jit(solution)/shard_map/ppermute | solution.py:149
  101.5 20.8 %collective-permute-start.6 = (bf16[2,4,48,768]{3,2,1,0:T(8,128)(2,1)}, bf16[2,4,48,768]{3,2,1,0:T(8,128)(2,1)}, u32[]{:S(2)}, u32[]{:S(2)}) collective-permute-start(bf16[2,4,48,768]{3,2,1,0:T(8,128)(2,1)} %pad_maximum_fusion.9.refs_0_), channel_id=1, source_target_pairs={{0,16},{8,24},{16,0},{24,8},{1,17},{9,25},{17,1},{25,9},{2,18},{10... | collective-permute-start | bytes 1769480 | tf_op jit(solution)/shard_map/ppermute | solution.py:153
  119.4 263.6 %collective-permute-start.26 = (bf16[2,4,48,1024]{3,2,1,0:T(8,128)(2,1)}, bf16[2,4,48,1024]{3,2,1,0:T(8,128)(2,1)}, u32[]{:S(2)}, u32[]{:S(2)}) collective-permute-start(bf16[2,4,48,1024]{3,2,1,0:T(8,128)(2,1)} %pad_maximum_fusion.6.refs_0_), channel_id=1, source_target_pairs={{0,16},{8,24},{16,0},{24,8},{1,17},{9,25},{17,1},{25,9},{2,18},{10... | collective-permute-start | bytes 2359304 | tf_op jit(solution)/shard_map/ppermute | solution.py:153
  122.3 260.8 %collective-permute-start.28 = (bf16[2,4,48,1024]{3,2,1,0:T(8,128)(2,1)}, bf16[2,4,48,1024]{3,2,1,0:T(8,128)(2,1)}, u32[]{:S(2)}, u32[]{:S(2)}) collective-permute-start(bf16[2,4,48,1024]{3,2,1,0:T(8,128)(2,1)} %pad_maximum_fusion.7.refs_2_), channel_id=1, source_target_pairs={{0,1},{1,0},{2,3},{3,2},{4,5},{5,4},{6,7},{7,6},{8,9},{9,8},{10,11... | collective-permute-start | bytes 2359304 | tf_op jit(solution)/shard_map/ppermute | solution.py:157
  127.9 254.6 %collective-permute-start.11 = (bf16[2,4,48,768]{3,2,1,0:T(8,128)(2,1)}, bf16[2,4,48,768]{3,2,1,0:T(8,128)(2,1)}, u32[]{:S(2)}, u32[]{:S(2)}) collective-permute-start(bf16[2,4,48,768]{3,2,1,0:T(8,128)(2,1)} %pad_maximum_fusion.10.refs_2_), channel_id=1, source_target_pairs={{0,8},{8,0},{16,24},{24,16},{1,9},{9,1},{17,25},{25,17},{2,10},{10... | collective-permute-start | bytes 1769480 | tf_op jit(solution)/shard_map/ppermute | solution.py:149
  127.9 255.6 %collective-permute-start.10 = (bf16[2,4,48,768]{3,2,1,0:T(8,128)(2,1)}, bf16[2,4,48,768]{3,2,1,0:T(8,128)(2,1)}, u32[]{:S(2)}, u32[]{:S(2)}) collective-permute-start(bf16[2,4,48,768]{3,2,1,0:T(8,128)(2,1)} %collective-permute-done.6.refs_1_), channel_id=1, source_target_pairs={{0,8},{8,0},{16,24},{24,16},{1,9},{9,1},{17,25},{25,17},{2,10},{10... | collective-permute-start | bytes 1769480 | tf_op jit(solution)/shard_map/ppermute | solution.py:149
  128.5 255.2 %collective-permute-start.12 = (bf16[2,4,48,768]{3,2,1,0:T(8,128)(2,1)}, bf16[2,4,48,768]{3,2,1,0:T(8,128)(2,1)}, u32[]{:S(2)}, u32[]{:S(2)}) collective-permute-start(bf16[2,4,48,768]{3,2,1,0:T(8,128)(2,1)} %collective-permute-done.8.refs_3_), channel_id=1, source_target_pairs={{0,8},{8,0},{16,24},{24,16},{1,9},{9,1},{17,25},{25,17},{2,10},{10... | collective-permute-start | bytes 1769480 | tf_op jit(solution)/shard_map/ppermute | solution.py:149
  382.6 203.5 %collective-permute-start.29 = (bf16[2,4,48,1024]{3,2,1,0:T(8,128)(2,1)}, bf16[2,4,48,1024]{3,2,1,0:T(8,128)(2,1)}, u32[]{:S(2)}, u32[]{:S(2)}) collective-permute-start(bf16[2,4,48,1024]{3,2,1,0:T(8,128)(2,1)} %pad_maximum_fusion.6.refs_0_), channel_id=1, source_target_pairs={{0,8},{8,0},{16,24},{24,16},{1,9},{9,1},{17,25},{25,17},{2,10},{10... | collective-permute-start | bytes 2359304 | tf_op jit(solution)/shard_map/ppermute | solution.py:149
  383.0 203.0 %collective-permute-start.31 = (bf16[2,4,48,1024]{3,2,1,0:T(8,128)(2,1)}, bf16[2,4,48,1024]{3,2,1,0:T(8,128)(2,1)}, u32[]{:S(2)}, u32[]{:S(2)}) collective-permute-start(bf16[2,4,48,1024]{3,2,1,0:T(8,128)(2,1)} %pad_maximum_fusion.7.refs_2_), channel_id=1, source_target_pairs={{0,8},{8,0},{16,24},{24,16},{1,9},{9,1},{17,25},{25,17},{2,10},{10... | collective-permute-start | bytes 2359304 | tf_op jit(solution)/shard_map/ppermute | solution.py:149
  383.1 202.9 %collective-permute-start.30 = (bf16[2,4,48,1024]{3,2,1,0:T(8,128)(2,1)}, bf16[2,4,48,1024]{3,2,1,0:T(8,128)(2,1)}, u32[]{:S(2)}, u32[]{:S(2)}) collective-permute-start(bf16[2,4,48,1024]{3,2,1,0:T(8,128)(2,1)} %collective-permute-done.26.refs_1_), channel_id=1, source_target_pairs={{0,8},{8,0},{16,24},{24,16},{1,9},{9,1},{17,25},{25,17},{2,10},{10... | collective-permute-start | bytes 2359304 | tf_op jit(solution)/shard_map/ppermute | solution.py:149
  383.5 202.5 %collective-permute-start.32 = (bf16[2,4,48,1024]{3,2,1,0:T(8,128)(2,1)}, bf16[2,4,48,1024]{3,2,1,0:T(8,128)(2,1)}, u32[]{:S(2)}, u32[]{:S(2)}) collective-permute-start(bf16[2,4,48,1024]{3,2,1,0:T(8,128)(2,1)} %collective-permute-done.28.refs_3_), channel_id=1, source_target_pairs={{0,8},{8,0},{16,24},{24,16},{1,9},{9,1},{17,25},{25,17},{2,10},{10... | collective-permute-start | bytes 2359304 | tf_op jit(solution)/shard_map/ppermute | solution.py:149
  914.8 46.5 %collective-permute-start.75 = (bf16[2,2,2,2,64,768]{5,4,1,2,0,3:T(8,128)(2,1)}, bf16[2,2,2,2,64,768]{5,4,1,2,0,3:T(8,128)(2,1)}, u32[]{:S(2)}, u32[]{:S(2)}) collective-permute-start(bf16[2,2,2,2,64,768]{5,4,1,2,0,3:T(8,128)(2,1)} %bitcast.511), channel_id=1, source_target_pairs={{0,8},{8,0},{16,24},{24,16},{1,9},{9,1},{17,25},{25,17},{2,10},{10... | collective-permute-start | bytes 4718600 | tf_op jit(solution)/shard_map/ppermute | solution.py:149
  917.6 104.4 %collective-permute-start.66 = (bf16[2,2,2,2,96,1024]{5,4,1,2,0,3:T(8,128)(2,1)}, bf16[2,2,2,2,96,1024]{5,4,1,2,0,3:T(8,128)(2,1)}, u32[]{:S(2)}, u32[]{:S(2)}) collective-permute-start(bf16[2,2,2,2,96,1024]{5,4,1,2,0,3:T(8,128)(2,1)} %bitcast.509), channel_id=1, source_target_pairs={{0,8},{8,0},{16,24},{24,16},{1,9},{9,1},{17,25},{25,17},{2,10},{10... | collective-permute-start | bytes 9437192 | tf_op jit(solution)/shard_map/ppermute | solution.py:149
  945.4 38.8 %collective-permute-start.57 = (bf16[2,2,2,2,96,768]{5,4,1,2,0,3:T(8,128)(2,1)}, bf16[2,2,2,2,96,768]{5,4,1,2,0,3:T(8,128)(2,1)}, u32[]{:S(2)}, u32[]{:S(2)}) collective-permute-start(bf16[2,2,2,2,96,768]{5,4,1,2,0,3:T(8,128)(2,1)} %bitcast.510), channel_id=1, source_target_pairs={{0,8},{8,0},{16,24},{24,16},{1,9},{9,1},{17,25},{25,17},{2,10},{10... | collective-permute-start | bytes 7077896 | tf_op jit(solution)/shard_map/ppermute | solution.py:149
  954.6 34.8 %collective-permute-start.48 = (bf16[2,2,2,2,96,768]{5,4,3,2,1,0:T(8,128)(2,1)}, bf16[2,2,2,2,96,768]{5,4,3,2,1,0:T(8,128)(2,1)}, u32[]{:S(2)}, u32[]{:S(2)}) collective-permute-start(bf16[2,2,2,2,96,768]{5,4,3,2,1,0:T(8,128)(2,1)} %dynamic-slice_bitcast_fusion), channel_id=1, source_target_pairs={{0,8},{8,0},{16,24},{24,16},{1,9},{9,1},{17,25},{25,17},{2,10},{10... | collective-permute-start | bytes 7077896 | tf_op jit(solution)/shard_map/ppermute | solution.py:149
  1004.8 22.1 %collective-permute-start.59 = (bf16[2,2,48,768]{3,2,0,1:T(8,128)(2,1)S(1)}, bf16[2,2,48,768]{3,2,0,1:T(8,128)(2,1)S(1)}, u32[]{:S(2)}, u32[]{:S(2)}) collective-permute-start(bf16[2,2,48,768]{3,2,0,1:T(8,128)(2,1)S(1)} %dynamic-slice_bitcast_fusion.11), channel_id=1, source_target_pairs={{0,1},{1,0},{2,3},{3,2},{4,5},{5,4},{6,7},{7,6},{8,9},{9,8},{10,11... | collective-permute-start | bytes 884744 | tf_op jit(solution)/shard_map/ppermute | solution.py:157
  1006.1 21.9 %collective-permute-start.61 = (bf16[2,2,48,768]{3,2,0,1:T(8,128)(2,1)S(1)}, bf16[2,2,48,768]{3,2,0,1:T(8,128)(2,1)S(1)}, u32[]{:S(2)}, u32[]{:S(2)}) collective-permute-start(bf16[2,2,48,768]{3,2,0,1:T(8,128)(2,1)S(1)} %dynamic-slice_bitcast_fusion.10), channel_id=1, source_target_pairs={{0,16},{8,24},{16,0},{24,8},{1,17},{9,25},{17,1},{25,9},{2,18},{10... | collective-permute-start | bytes 884744 | tf_op jit(solution)/shard_map/ppermute | solution.py:153
  1025.9 24.4 %collective-permute-start.67 = (bf16[2,2,2,48,1024]{4,3,0,1,2:T(8,128)(2,1)S(1)}, bf16[2,2,2,48,1024]{4,3,0,1,2:T(8,128)(2,1)S(1)}, u32[]{:S(2)}, u32[]{:S(2)}) collective-permute-start(bf16[2,2,2,48,1024]{4,3,0,1,2:T(8,128)(2,1)S(1)} %dynamic-slice_bitcast_fusion.2), channel_id=1, source_target_pairs={{0,16},{8,24},{16,0},{24,8},{1,17},{9,25},{17,1},{25,9},{2,18},{10... | collective-permute-start | bytes 2359304 | tf_op jit(solution)/shard_map/ppermute | solution.py:153
  1026.9 24.8 %collective-permute-start.69 = (bf16[2,2,2,48,1024]{4,3,1,2,0:T(8,128)(2,1)S(1)}, bf16[2,2,2,48,1024]{4,3,1,2,0:T(8,128)(2,1)S(1)}, u32[]{:S(2)}, u32[]{:S(2)}) collective-permute-start(bf16[2,2,2,48,1024]{4,3,1,2,0:T(8,128)(2,1)S(1)} %dynamic-slice_bitcast_fusion.1), channel_id=1, source_target_pairs={{0,1},{1,0},{2,3},{3,2},{4,5},{5,4},{6,7},{7,6},{8,9},{9,8},{10,11... | collective-permute-start | bytes 2359304 | tf_op jit(solution)/shard_map/ppermute | solution.py:157
  1045.1 19.4 %collective-permute-start.64 = (bf16[96,768]{1,0:T(8,128)(2,1)S(1)}, bf16[96,768]{1,0:T(8,128)(2,1)S(1)}, u32[]{:S(2)}, u32[]{:S(2)}) collective-permute-start(bf16[96,768]{1,0:T(8,128)(2,1)S(1)} %fusion.104), channel_id=1, source_target_pairs={{0,16},{8,24},{16,0},{24,8},{1,17},{9,25},{17,1},{25,9},{2,18},{10... | collective-permute-start | bytes 442376 | tf_op jit(solution)/shard_map/ppermute | solution.py:153
  1064.6 22.5 %collective-permute-start.56 = (bf16[2,96,768]{2,1,0:T(8,128)(2,1)S(1)}, bf16[2,96,768]{2,1,0:T(8,128)(2,1)S(1)}, u32[]{:S(2)}, u32[]{:S(2)}) collective-permute-start(bf16[2,96,768]{2,1,0:T(8,128)(2,1)S(1)} %maximum_select_fusion.7), channel_id=1, source_target_pairs={{0,8},{8,0},{16,24},{24,16},{1,9},{9,1},{17,25},{25,17},{2,10},{10... | collective-permute-start | bytes 884744 | tf_op jit(solution)/shard_map/ppermute | solution.py:149
  (157 other events, 2491.2 us)

commit v2 on v0

--- a/solution.py
+++ b/solution.py
@@ -3,6 +3,8 @@
 import jax
 import jax.numpy as jnp
 from jax import lax
+from jax.experimental import pallas as pl
+from jax.experimental.pallas import tpu as pltpu
 from jax.sharding import PartitionSpec as P
 
 HEADS = 12
@@ -30,6 +32,9 @@
     distance = jnp.maximum(positions[:, None] - positions[None, :], 0)
     levels = jnp.arange(BUCKETS, dtype=jnp.int32)
     return (bucket_of(distance)[None] == levels[:, None, None]).astype(jnp.bfloat16)
+
+
+PARTS = 4
 
 
 def rms_scale(values, gain):
@@ -380,6 +385,659 @@
     )
 
 
+CORE, ROW = [(i, i ^ 1) for i in range(4)], [(i, i ^ 2) for i in range(4)]
+ACROSS, NEAR, FAR = (
+    [(i, i ^ 1) for i in range(8)],
+    [(i, i ^ 2) for i in range(8)],
+    [(i, i ^ 4) for i in range(8)],
+)
+
+
+def over_core(values):
+    return lax.ppermute(values, "rep", CORE)
+
+
+def over_row(values):
+    return lax.ppermute(values, "rep", ROW)
+
+
+def over_across(values):
+    return lax.ppermute(values, "fsdp", ACROSS)
+
+
+def over_near(values):
+    return lax.ppermute(values, "fsdp", NEAR)
+
+
+def over_far(values):
+    return lax.ppermute(values, "fsdp", FAR)
+
+
+def pick(values, index, axis):
+    return lax.dynamic_index_in_dim(values, index, axis, keepdims=False)
+
+
+def gather_pieces(part):
+    held = part[None]
+    held = jnp.concatenate([held, over_far(held)], 0)
+    held = jnp.concatenate([held, over_near(held)], 0)
+    half = held.shape[1] // 2
+    first, second = held[:, :half], held[:, half:]
+    first = jnp.stack([first, over_across(first)])
+    second = jnp.stack([second, over_row(second)])
+    pieces = [first, over_row(first), second, over_across(second)]
+    return pieces + [over_core(piece) for piece in pieces]
+
+
+def gather_small(values, position):
+    held = values[None]
+    for bit, move in ((2, over_far), (1, over_near), (0, over_across)):
+        other = move(held)
+        mine = (position[1] >> bit) & 1
+        held = jnp.where(mine == 0, jnp.stack([held, other], 1), jnp.stack([other, held], 1))
+        held = held.reshape(-1, *values.shape)
+    return held
+
+
+def add_up(kept, received):
+    return (kept.astype(jnp.float32) + received.astype(jnp.float32)).astype(jnp.bfloat16)
+
+
+def scatter_parts(grads, position, by_shard=False):
+    part, shard = position[0], position[1]
+    bit = {"core": part & 1, "row": part >> 1, "across": shard & 1, "near": (shard >> 1) & 1, "far": shard >> 2}
+    move = {"core": over_core, "row": over_row, "across": over_across, "near": over_near, "far": over_far}
+    axes = ["far", "near", "across", "row", "core"] if by_shard else ["row", "core", "far", "near", "across"]
+    rows, columns = grads.shape[2], grads.shape[3]
+    half = rows // 2
+
+    def fold(values, names, name):
+        axis = names.index(name)
+        kept, sent = pick(values, bit[name], axis), pick(values, 1 - bit[name], axis)
+        return add_up(kept, move[name](sent)), [n for n in names if n != name]
+
+    sums, axes = fold(grads.reshape(2, 2, 2, 2, 2, rows, columns), axes, "core")
+    first, first_axes = fold(sums[..., :half, :], axes, "row")
+    second, second_axes = fold(sums[..., half:, :], axes, "across")
+    first, axes = fold(first, first_axes, "across")
+    second, axes = fold(second, second_axes, "row")
+    sums = jnp.concatenate([first, second], 2)
+    sums, axes = fold(sums, axes, "near")
+    sums, axes = fold(sums, axes, "far")
+    other = over_row(sums)
+    both = jnp.where(bit["row"] == 0, jnp.stack([sums, other]), jnp.stack([other, sums]))
+    others = over_core(both)
+    both = jnp.where(bit["core"] == 0, jnp.stack([both, others], 1), jnp.stack([others, both], 1))
+    return both.reshape(PARTS, rows, columns).astype(jnp.float32)
+
+
+def total_small(values):
+    for move in (over_core, over_row, over_across, over_near, over_far):
+        values = values + move(values)
+    return values
+
+
+BF16, F32 = jnp.bfloat16, jnp.float32
+VMEM_LIMIT = 58 * 1024 * 1024
+ANYWHERE = pl.BlockSpec(memory_space=pl.ANY)
+SCALARS = pl.BlockSpec(memory_space=pltpu.SMEM)
+LOCAL = pl.BlockSpec(memory_space=pltpu.VMEM)
+PAIR = 2 * HEAD
+SPAN = 256
+
+
+def mul(a, b):
+    return lax.dot_general(a, b, (((1,), (0,)), ((), ())), preferred_element_type=F32)
+
+
+def mul_right_t(a, b):
+    return lax.dot_general(a, b, (((1,), (1,)), ((), ())), preferred_element_type=F32)
+
+
+def mul_left_t(a, b):
+    return lax.dot_general(a, b, (((0,), (0,)), ((), ())), preferred_element_type=F32)
+
+
+def shape_of(*shape, kind=BF16):
+    return jax.ShapeDtypeStruct(shape, kind)
+
+
+def call(kernel, outs, operands, specs, scratch=(), flops=0, moved=0, out_specs=None):
+    return pl.pallas_call(
+        kernel,
+        out_shape=outs,
+        in_specs=specs,
+        out_specs=out_specs if out_specs is not None else [LOCAL] * len(outs),
+        scratch_shapes=list(scratch),
+        compiler_params=pltpu.CompilerParams(vmem_limit_bytes=VMEM_LIMIT),
+        cost_estimate=pl.CostEstimate(flops=flops, transcendentals=0, bytes_accessed=moved),
+    )(*operands)
+
+
+def relative(core, kind, outer, inner):
+    row, across = (kind, outer) if kind < 2 else (outer, kind - 2)
+    return core + 2 * row, across + 4 * (inner & 1) + 2 * (inner >> 1)
+
+
+def start_pieces(position_ref, sources, target_ref, semaphore_of, by_shard):
+    half = sources[0].shape[2]
+    for core in range(2):
+        for kind in range(4):
+            for outer in range(2):
+                for inner in range(4):
+                    part, shard = relative(core, kind, outer, inner)
+                    part, shard = position_ref[0] ^ part, position_ref[1] ^ shard
+                    place = (shard, part) if by_shard else (part, shard)
+                    pltpu.make_async_copy(
+                        sources[core * 4 + kind].at[outer, inner],
+                        target_ref.at[place[0], place[1], pl.ds((kind // 2) * half, half)],
+                        semaphore_of(place[0]),
+                    ).start()
+
+
+def wait_block(target_ref, index, semaphore):
+    pltpu.make_async_copy(target_ref.at[index], target_ref.at[index], semaphore).wait()
+
+
+def matrix(ref, index):
+    block = ref[index]
+    return block.reshape(-1, block.shape[-1])
+
+
+def normed(values, gain):
+    scale = lax.rsqrt(jnp.mean(values * values, axis=-1, keepdims=True) + norm_epsilon)
+    return values * scale * gain
+
+
+def norm_back(values, gain, grads):
+    scale = lax.rsqrt(jnp.mean(values * values, axis=-1, keepdims=True) + norm_epsilon)
+    weighted = grads * gain
+    mean = jnp.mean(weighted * values, axis=-1, keepdims=True)
+    return (
+        scale * weighted - values * (scale * scale * scale * mean),
+        jnp.sum(grads * values * scale, axis=0, keepdims=True),
+    )
+
+
+def spread_pair(pair):
+    low = lax.broadcasted_iota(jnp.int32, pair.shape, 1) < HEAD
+    zero = jnp.zeros_like(pair)
+    return jnp.concatenate([jnp.where(low, pair, zero), jnp.where(low, zero, pair)], 0)
+
+
+def join_pair(both):
+    rows = both.shape[0] // 2
+    low = lax.broadcasted_iota(jnp.int32, (rows, PAIR), 1) < HEAD
+    return jnp.where(low, both[:rows], both[rows:])
+
+
+def twice(values):
+    return jnp.concatenate([values, values], 0)
+
+
+def distance_levels(backward):
+    place = lax.broadcasted_iota(jnp.int32, (BUCKETS, SPAN), 1)
+    distance = (SPAN - place) % SPAN if backward else place
+    level = lax.broadcasted_iota(jnp.int32, (BUCKETS, SPAN), 0)
+    return (bucket_of(distance) == level).astype(F32)
+
+
+def fill_bias(table_ref, bias_ref, length):
+    rows = mul_left_t(table_ref[...], distance_levels(True).astype(BF16))
+    for head in range(HEADS):
+        row = jnp.broadcast_to(rows[head : head + 1], (length, SPAN))
+        bias_ref[head] = pltpu.roll(row, 0, 1, stride=1, stride_axis=0)[:, :length]
+
+
+def self_mask(column_ref, row_ref, row, length):
+    near = column_ref[pl.ds(row * length, length), :] == row_ref[pl.ds(row, 1), :]
+    i = lax.broadcasted_iota(jnp.int32, (length, length), 0)
+    j = lax.broadcasted_iota(jnp.int32, (length, length), 1)
+    return near & (j <= i)
+
+
+def cross_mask(column_ref, row_ref, row, length):
+    return column_ref[pl.ds(row * length, length), :] == row_ref[pl.ds(row, 1), :]
+
+
+def put_totals(totals_ref, row, pair, totals, length):
+    lane = lax.broadcasted_iota(jnp.int32, (length, 128), 1)
+    rows = pl.ds(row * length, length)
+    held = totals_ref[rows, :]
+    held = jnp.where(lane == 2 * pair, totals[:length], held)
+    totals_ref[rows, :] = jnp.where(lane == 2 * pair + 1, totals[length:], held)
+
+
+def get_totals(totals_ref, row, pair, length):
+    lane = lax.broadcasted_iota(jnp.int32, (length, 128), 1)
+    held = totals_ref[pl.ds(row * length, length), :]
+    of = lambda head: jnp.sum(jnp.where(lane == head, held, 0.0), axis=1, keepdims=True)
+    return jnp.concatenate([of(2 * pair), of(2 * pair + 1)], 0)
+
+
+def attend_pairs(rows, length, keys_length, mask_of, q_ref, k_ref, v_ref, c_ref, t_ref, bias_ref):
+    def step(index, carry):
+        row, pair = index // (HEADS // 2), index % (HEADS // 2)
+        lanes = pl.ds(pl.multiple_of(pair * PAIR, PAIR), PAIR)
+        mine = pl.ds(pl.multiple_of(row * length, 8), length)
+        theirs = pl.ds(pl.multiple_of(row * keys_length, 8), keys_length)
+        scores = mul_right_t(spread_pair(q_ref[mine, lanes]), k_ref[theirs, lanes])
+        if bias_ref is not None:
+            scores = scores + jnp.concatenate([bias_ref[2 * pair], bias_ref[2 * pair + 1]], 0)
+        scores = jnp.where(twice(mask_of(row)), scores, masked_score)
+        highest = jnp.max(scores, axis=1, keepdims=True)
+        expanded = jnp.exp(scores - highest)
+        totals = jnp.sum(expanded, axis=1, keepdims=True)
+        weights = (expanded * (1.0 / totals)).astype(BF16)
+        c_ref[mine, lanes] = join_pair(mul(weights, v_ref[theirs, lanes])).astype(BF16)
+        put_totals(t_ref, row, pair, highest + jnp.log(totals), length)
+        return carry
+
+    lax.fori_loop(0, rows * (HEADS // 2), step, 0)
+
+
+def attend_pairs_back(
+    rows, length, keys_length, mask_of, q_ref, k_ref, v_ref, t_ref, g_ref, dq_ref, dk_ref, dv_ref, bias_ref, sum_ref
+):
+    def step(index, carry):
+        row, pair = index // (HEADS // 2), index % (HEADS // 2)
+        lanes = pl.ds(pl.multiple_of(pair * PAIR, PAIR), PAIR)
+        mine = pl.ds(pl.multiple_of(row * length, 8), length)
+        theirs = pl.ds(pl.multiple_of(row * keys_length, 8), keys_length)
+        queries, keys, values = spread_pair(q_ref[mine, lanes]), k_ref[theirs, lanes], v_ref[theirs, lanes]
+        grads = spread_pair(g_ref[mine, lanes])
+        scores = mul_right_t(queries, keys)
+        if bias_ref is not None:
+            scores = scores + jnp.concatenate([bias_ref[2 * pair], bias_ref[2 * pair + 1]], 0)
+        scores = jnp.where(twice(mask_of(row)), scores, masked_score)
+        weights = jnp.exp(scores - get_totals(t_ref, row, pair, length))
+        weight_grads = mul_right_t(grads, values)
+        row_dot = jnp.sum(weights * weight_grads, axis=1, keepdims=True)
+        score_grads = (weights * (weight_grads - row_dot)).astype(BF16)
+        dq_ref[mine, lanes] = join_pair(mul(score_grads, keys)).astype(BF16)
+        dk_ref[theirs, lanes] = mul_left_t(score_grads, queries).astype(BF16)
+        dv_ref[theirs, lanes] = mul_left_t(weights.astype(BF16), grads).astype(BF16)
+        if sum_ref is not None:
+            for head in range(2):
+                part = score_grads[head * length : (head + 1) * length].astype(F32)
+                sum_ref[2 * pair + head] = sum_ref[2 * pair + head] + part
+        return carry
+
+    lax.fori_loop(0, rows * (HEADS // 2), step, 0)
+
+
+def self_forward(position, dec, column, row, gain, table, gain_next, pieces):
+    tokens, features = dec.shape
+    rows = row.shape[0]
+    length = tokens // rows
+
+    def kernel(position_ref, dec_ref, column_ref, row_ref, gain_ref, table_ref, next_ref, *refs):
+        sources, (n_ref, q_ref, k_ref, v_ref, c_ref, t_ref, mid_ref, nn_ref, m_ref, bias_ref, semaphores) = refs[:8], refs[8:]
+        start_pieces(position_ref, sources, m_ref, lambda index: semaphores.at[index], False)
+        fill_bias(table_ref, bias_ref, length)
+        n_ref[...] = normed(dec_ref[...].astype(F32), gain_ref[...]).astype(BF16)
+        for index in range(PARTS):
+            wait_block(m_ref, index, semaphores.at[index])
+        for out, index in ((q_ref, 0), (k_ref, 1), (v_ref, 2)):
+            out[...] = mul(n_ref[...], matrix(m_ref, index)).astype(BF16)
+        t_ref[...] = jnp.zeros_like(t_ref)
+        mask = lambda r: self_mask(column_ref, row_ref, r, length)
+        attend_pairs(rows, length, length, mask, q_ref, k_ref, v_ref, c_ref, t_ref, bias_ref)
+        mid_ref[...] = dec_ref[...].astype(F32) + mul(c_ref[...], matrix(m_ref, 3))
+        nn_ref[...] = normed(mid_ref[...], next_ref[...]).astype(BF16)
+
+    big = shape_of(tokens, features)
+    return call(
+        kernel,
+        [big, big, big, big, big, shape_of(tokens, 128, kind=F32), shape_of(tokens, features, kind=F32), big, shape_of(PARTS, 8, features // 8, features)],
+        (position, dec, column, row, gain, table, gain_next, *pieces),
+        [SCALARS] + [LOCAL] * 6 + [ANYWHERE] * 8,
+        [pltpu.VMEM((HEADS, length, length), F32), pltpu.SemaphoreType.DMA((PARTS,))],
+        flops=30 * tokens * features * features,
+        moved=8 * tokens * features * 2 + 16 * features * features,
+    )
+
+
+def cross_forward(position, middle, normed_cross, enc, column, row, gain_next, pieces):
+    tokens, features = middle.shape
+    rows, keys_length = row.shape
+    length = tokens // rows
+
+    def kernel(position_ref, mid_ref, n_ref, enc_ref, column_ref, row_ref, next_ref, *refs):
+        sources, (q_ref, k_ref, v_ref, c_ref, t_ref, late_ref, nn_ref, m_ref, semaphores) = refs[:8], refs[8:]
+        start_pieces(position_ref, sources, m_ref, lambda index: semaphores.at[index], False)
+        for index in range(PARTS):
+            wait_block(m_ref, index, semaphores.at[index])
+        q_ref[...] = mul(n_ref[...], matrix(m_ref, 0)).astype(BF16)
+        for r in range(rows):
+            at = pl.ds(r * keys_length, keys_length)
+            k_ref[at, :] = mul(enc_ref[at, :], matrix(m_ref, 1)).astype(BF16)
+            v_ref[at, :] = mul(enc_ref[at, :], matrix(m_ref, 2)).astype(BF16)
+        t_ref[...] = jnp.zeros_like(t_ref)
+        mask = lambda r: cross_mask(column_ref, row_ref, r, length)
+        attend_pairs(rows, length, keys_length, mask, q_ref, k_ref, v_ref, c_ref, t_ref, None)
+        late_ref[...] = mid_ref[...] + mul(c_ref[...], matrix(m_ref, 3))
+        nn_ref[...] = normed(late_ref[...], next_ref[...]).astype(BF16)
+
+    big, keys = shape_of(tokens, features), shape_of(enc.shape[0], features)
+    return call(
+        kernel,
+        [big, keys, keys, big, shape_of(tokens, 128, kind=F32), shape_of(tokens, features, kind=F32), big, shape_of(PARTS, 8, features // 8, features)],
+        (position, middle, normed_cross, enc, column, row, gain_next, *pieces),
+        [SCALARS] + [LOCAL] * 6 + [ANYWHERE] * 8,
+        [pltpu.SemaphoreType.DMA((PARTS,))],
+        flops=12 * (tokens + enc.shape[0]) * features * features,
+        moved=10 * tokens * features * 2 + 16 * features * features + enc.size * 6,
+    )
+
+
+def feed_forward(position, late, normed_ffn, cotangent, gain, inner, down):
+    tokens, features = late.shape
+    wide = inner[0].shape[3] // 2
+    each = wide // 2
+    blocks = 8
+    inner_shape = (PARTS, 8, features // 8, 2 * wide)
+    down_shape = (8, PARTS, each // PARTS, features)
+
+    def kernel(position_ref, late_ref, n_ref, cot_ref, gain_ref, *refs):
+        inner_sources, down_sources = refs[:8], refs[8:16]
+        out_ref, lg_ref, lgb_ref, gg_ref, di_ref, dd_ref = refs[16:22]
+        flat_ref, sum_ref, back_ref, inner_ref, down_ref, inner_done, down_done = refs[22:]
+        step = pl.program_id(0)
+
+        @pl.when(step == 0)
+        def _():
+            start_pieces(position_ref, inner_sources, inner_ref, lambda index: inner_done.at[index], False)
+            start_pieces(position_ref, down_sources, down_ref, lambda index: down_done.at[index], True)
+            flat_ref[...] = n_ref[...].T
+            sum_ref[...] = jnp.zeros_like(sum_ref)
+            back_ref[...] = jnp.zeros_like(back_ref)
+
+        @pl.when(step % 2 == 0)
+        def _():
+            wait_block(inner_ref, step // 2, inner_done.at[step // 2])
+
+        wait_block(down_ref, step, down_done.at[step])
+        inner_block = inner_ref[step // 2, :, :, pl.ds(pl.multiple_of((step % 2) * wide, wide), wide)].reshape(features, wide)
+        down_block = down_ref[step].reshape(each, features)
+        both = mul(n_ref[...], inner_block)
+        hidden_grad = mul_right_t(cot_ref[...], down_block)
+        gate, up = both[:, :each], both[:, each:]
+        inside = math.sqrt(2 / math.pi) * (gate + 0.044715 * (gate * gate * gate))
+        bent = jnp.tanh(inside)
+        half = 0.5 * (1.0 + bent)
+        swish = gate * half
+        hidden = (swish * up).astype(BF16)
+        slope = half + 0.5 * gate * (1.0 - bent * bent) * (
+            math.sqrt(2 / math.pi) * (1.0 + 3 * 0.044715 * (gate * gate))
+        )
+        grads = jnp.concatenate([hidden_grad * up * slope, hidden_grad * swish], 1).astype(BF16)
+        sum_ref[...] += mul(hidden, down_block)
+        back_ref[...] += mul_right_t(grads, inner_block)
+        di_ref[0] = mul(flat_ref[...], grads).astype(BF16)
+        dd_ref[...] = mul_left_t(hidden, cot_ref[...]).astype(BF16)
+
+        @pl.when(step == blocks - 1)
+        def _():
+            out_ref[...] = (late_ref[...] + sum_ref[...]).astype(BF16)
+            part, gain_grad = norm_back(late_ref[...], gain_ref[...], back_ref[...])
+            grad = cot_ref[...].astype(F32) + part
+            lg_ref[...] = grad
+            lgb_ref[...] = grad.astype(BF16)
+            gg_ref[...] = gain_grad
+
+    whole = lambda a: pl.BlockSpec(a.shape, lambda i: (0,) * len(a.shape))
+    big = shape_of(tokens, features)
+    outs = [big, shape_of(tokens, features, kind=F32), big, shape_of(1, features, kind=F32), shape_of(PARTS, features, 2 * wide), shape_of(8 * each, features)]
+    inner_spec = pl.BlockSpec((1, features, wide), lambda i: (i // 2, 0, i % 2))
+    down_spec = pl.BlockSpec((each, features), lambda i: (i, 0))
+    return pl.pallas_call(
+        kernel,
+        grid=(blocks,),
+        out_shape=outs,
+        in_specs=[SCALARS, whole(late), whole(normed_ffn), whole(cotangent), whole(gain)] + [ANYWHERE] * 16,
+        out_specs=[whole(o) for o in outs[:4]] + [inner_spec, down_spec],
+        scratch_shapes=[
+            pltpu.VMEM((features, tokens), BF16),
+            pltpu.VMEM((tokens, features), F32),
+            pltpu.VMEM((tokens, features), F32),
+            pltpu.VMEM(inner_shape, BF16),
+            pltpu.VMEM(down_shape, BF16),
+            pltpu.SemaphoreType.DMA((PARTS,)),
+            pltpu.SemaphoreType.DMA((8,)),
+        ],
+        compiler_params=pltpu.CompilerParams(vmem_limit_bytes=VMEM_LIMIT),
+        cost_estimate=pl.CostEstimate(
+            flops=18 * tokens * features * 8 * each, transcendentals=0, bytes_accessed=4 * 9437184
+        ),
+    )(position, late, normed_ffn, cotangent, gain, *inner, *down)
+
+
+def cross_backward(late_grad, late_gradb, middle, q, k, v, totals, column, row, gain, matrices):
+    tokens, features = middle.shape
+    rows, keys_length = row.shape
+    length = tokens // rows
+
+    def kernel(lg_ref, lgb_ref, mid_ref, q_ref, k_ref, v_ref, t_ref, column_ref, row_ref, gain_ref, m_ref, dq_ref, dk_ref, dv_ref, mg_ref, mgb_ref, gg_ref, g_ref):
+        g_ref[...] = mul_right_t(lgb_ref[...], m_ref[3]).astype(BF16)
+        mask = lambda r: cross_mask(column_ref, row_ref, r, length)
+        attend_pairs_back(rows, length, keys_length, mask, q_ref, k_ref, v_ref, t_ref, g_ref, dq_ref, dk_ref, dv_ref, None, None)
+        part, gain_grad = norm_back(mid_ref[...], gain_ref[...], mul_right_t(dq_ref[...], m_ref[0]))
+        grad = lg_ref[...] + part
+        mg_ref[...] = grad
+        mgb_ref[...] = grad.astype(BF16)
+        gg_ref[...] = gain_grad
+
+    big, keys = shape_of(tokens, features), shape_of(k.shape[0], features)
+    return call(
+        kernel,
+        [big, keys, keys, shape_of(tokens, features, kind=F32), big, shape_of(1, features, kind=F32)],
+        (late_grad, late_gradb, middle, q, k, v, totals, column, row, gain, matrices),
+        [LOCAL] * 11,
+        [pltpu.VMEM((tokens, features), BF16)],
+        flops=4 * tokens * features * features,
+        moved=30 * tokens * features * 2,
+    )
+
+
+def self_backward(middle_grad, middle_gradb, dec, q, k, v, totals, column, row, gain, table, matrices):
+    tokens, features = dec.shape
+    rows = row.shape[0]
+    length = tokens // rows
+
+    def kernel(mg_ref, mgb_ref, dec_ref, q_ref, k_ref, v_ref, t_ref, column_ref, row_ref, gain_ref, table_ref, m_ref, dq_ref, dk_ref, dv_ref, ig_ref, gg_ref, tg_ref, g_ref, bias_ref, sum_ref):
+        fill_bias(table_ref, bias_ref, length)
+        g_ref[...] = mul_right_t(mgb_ref[...], m_ref[3]).astype(BF16)
+        sum_ref[...] = jnp.zeros_like(sum_ref)
+        mask = lambda r: self_mask(column_ref, row_ref, r, length)
+        attend_pairs_back(rows, length, length, mask, q_ref, k_ref, v_ref, t_ref, g_ref, dq_ref, dk_ref, dv_ref, bias_ref, sum_ref)
+        back = mul_right_t(dq_ref[...], m_ref[0]) + mul_right_t(dk_ref[...], m_ref[1]) + mul_right_t(dv_ref[...], m_ref[2])
+        part, gain_grad = norm_back(dec_ref[...].astype(F32), gain_ref[...], back)
+        ig_ref[...] = (mg_ref[...] + part).astype(BF16)
+        gg_ref[...] = gain_grad
+        sums = []
+        i = lax.broadcasted_iota(jnp.int32, (length, length), 0)
+        j = lax.broadcasted_iota(jnp.int32, (length, length), 1)
+        flip = (i + j == length - 1).astype(F32)
+        for head in range(HEADS):
+            flipped = lax.dot_general(
+                flip, sum_ref[head], (((1,), (0,)), ((), ())),
+                precision=lax.Precision.HIGHEST, preferred_element_type=F32,
+            )
+            square = jnp.concatenate([flipped, jnp.zeros((length, SPAN - length), F32)], 1)
+            turned = pltpu.roll(square, SPAN - length + 1, 1, stride=1, stride_axis=0)
+            sums.append(jnp.sum(turned, axis=0, keepdims=True))
+        sums.append(jnp.zeros((16 - HEADS, SPAN), F32))
+        tg_ref[...] = lax.dot_general(
+            jnp.concatenate(sums, 0), distance_levels(True), (((1,), (1,)), ((), ())),
+            precision=lax.Precision.HIGHEST, preferred_element_type=F32,
+        )
+
+    big = shape_of(tokens, features)
+    return call(
+        kernel,
+        [big, big, big, big, shape_of(1, features, kind=F32), shape_of(16, BUCKETS, kind=F32)],
+        (middle_grad, middle_gradb, dec, q, k, v, totals, column, row, gain, table, matrices),
+        [LOCAL] * 12,
+        [pltpu.VMEM((tokens, features), BF16), pltpu.VMEM((HEADS, length, length), F32), pltpu.VMEM((HEADS, length, length), F32)],
+        flops=8 * tokens * features * features,
+        moved=20 * tokens * features * 2,
+    )
+
+
+def four_grads(lefts, rights):
+    features = lefts[0].shape[1]
+
+    def kernel(a0, a1, a2, a3, b0, b1, b2, b3, out_ref):
+        for index, (a, b) in enumerate(((a0, b0), (a1, b1), (a2, b2), (a3, b3))):
+            out_ref[index] = mul_left_t(a[...], b[...]).astype(BF16)
+
+    tokens = sum(a.shape[0] for a in lefts)
+    return call(
+        kernel,
+        [shape_of(4, features, features)],
+        (*lefts, *rights),
+        [LOCAL] * 8,
+        flops=2 * tokens * features * features,
+        moved=4 * tokens * features + 8 * features * features,
+    )[0]
+
+
+def key_value_back(dk, dv, key_matrix, value_matrix):
+    tokens, features = dk.shape
+    block = 512 if tokens % 512 == 0 else tokens
+
+    def kernel(dk_ref, dv_ref, k_ref, v_ref, out_ref):
+        out_ref[...] = (mul_right_t(dk_ref[...], k_ref[...]) + mul_right_t(dv_ref[...], v_ref[...])).astype(BF16)
+
+    spec = pl.BlockSpec((block, features), lambda i: (i, 0))
+    whole = pl.BlockSpec(key_matrix.shape, lambda i: (0, 0))
+    return pl.pallas_call(
+        kernel,
+        grid=(tokens // block,),
+        out_shape=shape_of(tokens, features),
+        in_specs=[spec, spec, whole, whole],
+        out_specs=spec,
+        compiler_params=pltpu.CompilerParams(vmem_limit_bytes=VMEM_LIMIT),
+        cost_estimate=pl.CostEstimate(flops=4 * tokens * features * features, transcendentals=0, bytes_accessed=6 * tokens * features + 4 * features * features),
+    )(dk, dv, key_matrix, value_matrix)
+
+
+def fast_shards(
+    dec_input,
+    enc_output,
+    dec_segments,
+    enc_segments,
+    cotangent,
+    norm_self,
+    q_self,
+    k_self,
+    v_self,
+    o_self,
+    rel_table,
+    norm_cross,
+    q_cross,
+    k_cross,
+    v_cross,
+    o_cross,
+    norm_ffn,
+    wi_gate,
+    wi_up,
+    wo_ffn,
+):
+    gain_rows = norm_self.shape[0]
+    table_rows = rel_table.shape[0]
+    features = dec_input.shape[2]
+    blocks = 2
+    each = wi_gate.shape[1] // (blocks * PARTS)
+    part = lax.axis_index("rep")
+    position = jnp.stack([part, lax.axis_index("fsdp")]).astype(jnp.int32)
+    choose = lambda *values: lax.select_n(part, *values)
+    small = jnp.concatenate([norm_self, norm_cross, norm_ffn, rel_table.reshape(-1)])
+    small_all = gather_small(small, position)
+    self_pieces = gather_pieces(choose(q_self, k_self, v_self, o_self))
+    cross_pieces = gather_pieces(choose(q_cross, k_cross, v_cross, o_cross))
+    gate_part = lax.dynamic_slice_in_dim(wi_gate, part * (blocks * each), blocks * each, 1)
+    up_part = lax.dynamic_slice_in_dim(wi_up, part * (blocks * each), blocks * each, 1)
+    inner_pieces = gather_pieces(
+        jnp.concatenate(
+            [gate_part[:, :each], up_part[:, :each], gate_part[:, each:], up_part[:, each:]], 1
+        )
+    )
+    down_rows = wo_ffn.shape[0] // PARTS
+    down_pieces = gather_pieces(lax.dynamic_slice_in_dim(wo_ffn, part * down_rows, down_rows, 0))
+    gain_of = lambda i: small_all[:, i * gain_rows : (i + 1) * gain_rows].reshape(1, -1).astype(F32)
+    gain_self, gain_cross, gain_ffn = gain_of(0), gain_of(1), gain_of(2)
+    table = small_all[:, 3 * gain_rows :].reshape(BUCKETS, HEADS)
+
+    dec = dec_input.reshape(-1, features)
+    enc = enc_output.reshape(-1, features)
+    cot = cotangent.reshape(-1, features)
+    column = dec_segments.reshape(-1, 1)
+    n_self, q, k, v, context, totals, middle, n_cross, self_matrices = self_forward(
+        position, dec, column, dec_segments, gain_self, table, gain_cross, self_pieces
+    )
+    cq, ck, cv, cross_context, cross_totals, late, n_ffn, cross_matrices = cross_forward(
+        position, middle, n_cross, enc, column, enc_segments, gain_ffn, cross_pieces
+    )
+    out, late_grad, late_gradb, grad_gain_ffn, grad_inner, grad_down = feed_forward(
+        position, late, n_ffn, cot, gain_ffn, inner_pieces, down_pieces
+    )
+    self_matrices = self_matrices.reshape(PARTS, features, features)
+    cross_matrices = cross_matrices.reshape(PARTS, features, features)
+    down_sum = scatter_parts(grad_down.reshape(8, PARTS, -1, features), position, True)
+    inner_sum = scatter_parts(grad_inner.reshape(PARTS, 8, -1, grad_inner.shape[2]), position)
+    dq, dk, dv, middle_grad, middle_gradb, grad_gain_cross = cross_backward(
+        late_grad, late_gradb, middle, cq, ck, cv, cross_totals, column, enc_segments, gain_cross, cross_matrices
+    )
+    cross_grads = four_grads((n_cross, enc, enc, cross_context), (dq, dk, dv, late_gradb))
+    enc_grad = key_value_back(dk, dv, cross_matrices[1], cross_matrices[2])
+    cross_sum = scatter_parts(cross_grads.reshape(PARTS, 8, -1, features), position)
+    sq, sk, sv, input_grad, grad_gain_self, table_gradient = self_backward(
+        middle_grad, middle_gradb, dec, q, k, v, totals, column, dec_segments, gain_self, table, self_matrices
+    )
+    self_grads = four_grads((n_self, n_self, n_self, context), (sq, sk, sv, middle_gradb))
+    self_sum = scatter_parts(self_grads.reshape(PARTS, 8, -1, features), position)
+    small_grads = jnp.concatenate(
+        [
+            grad_gain_self.reshape(8, -1),
+            grad_gain_cross.reshape(8, -1),
+            grad_gain_ffn.reshape(8, -1),
+            table_gradient[:HEADS].T.reshape(8, -1),
+        ],
+        1,
+    )
+    small_sum = pick(total_small(small_grads), position[1], 0)
+    pieces = lambda first: jnp.concatenate(
+        [
+            inner_sum[i, :, (2 * j + first) * each : (2 * j + first + 1) * each]
+            for i in range(PARTS)
+            for j in range(blocks)
+        ],
+        1,
+    )
+    return (
+        out.reshape(dec_input.shape),
+        input_grad.reshape(dec_input.shape),
+        enc_grad.reshape(enc_output.shape),
+        small_sum[:gain_rows],
+        self_sum[0],
+        self_sum[1],
+        self_sum[2],
+        self_sum[3],
+        small_sum[3 * gain_rows :].reshape(table_rows, HEADS),
+        small_sum[gain_rows : 2 * gain_rows],
+        cross_sum[0],
+        cross_sum[1],
+        cross_sum[2],
+        cross_sum[3],
+        small_sum[2 * gain_rows : 3 * gain_rows],
+        pieces(0),
+        pieces(1),
+        down_sum.reshape(wo_ffn.shape),
+    )
+
+
 def solution(mesh):
     placed = (
         P(("rep", "fsdp"), None, None),
@@ -403,8 +1061,9 @@
         P("fsdp", None),
         P("fsdp", None),
     )
+    fast = mesh.shape["rep"] == 4 and mesh.shape["fsdp"] == 8
     return jax.shard_map(
-        shards,
+        fast_shards if fast else shards,
         mesh=mesh,
         in_specs=placed,
         out_specs=(

time: 1430 us -> 442 us (0.31)
  waiting for transfers between devices: 1040 us -> 138 us
  matrix products: 185 us -> 0 us
  Pallas kernels: 0 us -> 160 us
  blocking collectives: 80.8 us -> 0 us
  starting transfers between devices: 1.71 us -> 71.7 us
  local copies, waits for them, and re-layouts: 56.1 us -> 37.4 us
  other arithmetic: 42.5 us -> 26.2 us
  between operations: 17.4 us -> 2.15 us
    reduce_scatter x9 -> x0, waiting for transfers between devices: 602 us -> none  [the longest x1 77.2 us: shards(): lax.psum_scatter(grad_up.astype(jnp.bfloat16), 'fsdp', scatter_dimension=...]
    all_gather x11 -> x0, waiting for transfers between devices: 383 us -> none  [the longest x1 56 us: shards(): lax.all_gather(wo_ffn, 'fsdp', axis=0, tiled=True)]
    dot_general x47 -> x0, matrix products: 185 us -> none  [the longest x11 49.4 us: project(): jnp.einsum('rld,de->rle', values, matrix, preferred_element_type=jnp.floa...]
    pallas_call x0 -> x8, Pallas kernels: none -> 160 us  [the longest x6 124 us: call(): pl.pallas_call(kernel, out_shape=outs, in_specs=specs, out_specs=out_spec...]
    ppermute x0 -> x84, waiting for transfers between devices: none -> 138 us  [the longest x21 38 us: over_row(): return lax.ppermute(values, 'rep', ROW)]
    ppermute x0 -> x84, starting transfers between devices: none -> 71.7 us  [the longest x21 22.5 us: over_row(): return lax.ppermute(values, 'rep', ROW)]
    unnamed x2 -> x0, blocking collectives: 58.3 us -> none
    psum x1 -> x0, waiting for transfers between devices: 45.9 us -> none  [shards(): lax.psum(cross_sums[2].astype(jnp.bfloat16), 'rep').astype(jnp.float32)]
  transfers between devices with their start and end apart: 23 -> 84, of which waited for: 20 -> 35; matrix products, arithmetic and copies ran while one was open for 15% -> 13% of each run, Pallas kernels for 0% -> 30%
where the time goes in v2:
time: 442 us; the launch traced here: 435 us
  Pallas kernels  160 us (36%)
  waiting for transfers between devices  138 us (31%)
  starting transfers between devices  71.7 us (16%)
  local copies, waits for them, and re-layouts  37.4 us (8%)
  other arithmetic  26.2 us (6%)
    pallas_call x6, Pallas kernels, call(): pl.pallas_call(kernel, out_shape=outs, in_specs=specs, out_specs=out_spec...  124 us
    ppermute x21, waiting for transfers between devices, over_row(): return lax.ppermute(values, 'rep', ROW)  38 us
    ppermute x18, waiting for transfers between devices, over_across(): return lax.ppermute(values, 'fsdp', ACROSS)  36.8 us
    ppermute x10, waiting for transfers between devices, over_near(): return lax.ppermute(values, 'fsdp', NEAR)  35 us
    pallas_call x1, Pallas kernels, feed_forward(): pl.pallas_call(kernel, grid=(blocks,), out_shape=outs, in_specs=[SCALARS,...  28.8 us
    ppermute x10, waiting for transfers between devices, over_far(): return lax.ppermute(values, 'fsdp', FAR)  27.5 us
    ppermute x21, starting transfers between devices, over_row(): return lax.ppermute(values, 'rep', ROW)  22.5 us
    ppermute x18, starting transfers between devices, over_across(): return lax.ppermute(values, 'fsdp', ACROSS)  20.6 us
  transfers between devices with their start and end apart: 84, of which 35 were waited for; matrix products, arithmetic and copies ran while one was open for 13% of the time, Pallas kernels for 30%

profile of v2, /device:TPU:0, one launch (start us, length us, event | category | flops | bytes accessed | tf_op | source)
XLA Modules:
  0.0 435.4 jit_solution(7343271207252802834)
XLA Ops:
  1.8 4.1 collective-permute-start.3
  15.4 7.8 %collective-permute-done = bf16[1,336]{1,0:T(2,128)(2,1)S(1)} collective-permute-done((bf16[1,336]{1,0:T(2,128)(2,1)S(1)}, bf16[1,336]{1,0:T(2,128)(2,1)S(1)}, u32[]{:S(2)}, u32[]{:S(2)}) %collective-permute-start) | collective-permute-done | bytes 704 | tf_op jit(solution)/shard_map/ppermute | solution.py:413
  23.4 3.6 collective-permute-done.1
  36.4 3.5 collective-permute-done.34
  41.6 4.6 %collective-permute-done.4 = bf16[2,96,768]{2,1,0:T(8,128)(2,1)S(1)} collective-permute-done((bf16[2,96,768]{2,1,0:T(8,128)(2,1)S(1)}, bf16[2,96,768]{2,1,0:T(8,128)(2,1)S(1)}, u32[]{:S(2)}, u32[]{:S(2)}) %collective-permute-start.4) | collective-permute-done | bytes 294944 | tf_op jit(solution)/shard_map/ppermute | solution.py:409
  47.9 4.6 %collective-permute-done.14 = bf16[2,96,768]{2,1,0:T(8,128)(2,1)S(1)} collective-permute-done((bf16[2,96,768]{2,1,0:T(8,128)(2,1)S(1)}, bf16[2,96,768]{2,1,0:T(8,128)(2,1)S(1)}, u32[]{:S(2)}, u32[]{:S(2)}) %collective-permute-start.14) | collective-permute-done | bytes 294944 | tf_op jit(solution)/shard_map/ppermute | solution.py:409
  64.0 5.6 %collective-permute-done.15 = bf16[4,48,768]{2,1,0:T(8,128)(2,1)S(1)} collective-permute-done((bf16[4,48,768]{2,1,0:T(8,128)(2,1)S(1)}, bf16[4,48,768]{2,1,0:T(8,128)(2,1)S(1)}, u32[]{:S(2)}, u32[]{:S(2)}) %collective-permute-start.15) | collective-permute-done | bytes 294944 | tf_op jit(solution)/shard_map/ppermute | solution.py:405
  77.2 6.4 %collective-permute-done.25 = bf16[4,48,1024]{2,1,0:T(8,128)(2,1)S(1)} collective-permute-done((bf16[4,48,1024]{2,1,0:T(8,128)(2,1)S(1)}, bf16[4,48,1024]{2,1,0:T(8,128)(2,1)S(1)}, u32[]{:S(2)}, u32[]{:S(2)}) %collective-permute-start.25) | collective-permute-done | bytes 393248 | tf_op jit(solution)/shard_map/ppermute | solution.py:405
  101.5 6.2 %collective-permute-done.16.refs_1_ = bf16[2,4,48,768]{3,2,1,0:T(8,128)(2,1)} collective-permute-done((bf16[2,4,48,768]{3,2,1,0:T(8,128)(2,1)S(1)}, bf16[2,4,48,768]{3,2,1,0:T(8,128)(2,1)}, u32[]{:S(2)}, u32[]{:S(2)}) %collective-permute-start.16) | collective-permute-done | bytes 589856 | tf_op jit(solution)/shard_map/ppermute | solution.py:401
  107.7 3.5 collective-permute-done.18.refs_3_
  114.0 21.5 %shard_map.331 = (bf16[528,768]{1,0:T(8,128)(2,1)}, bf16[528,768]{1,0:T(8,128)(2,1)}, bf16[528,768]{1,0:T(8,128)(2,1)}, bf16[528,768]{1,0:T(8,128)(2,1)}, bf16[5...) custom-call(s32[2]{0:T(128)} %pad_add_fusion.position_ref, ...), custom_call_target="tpu_custom_call" | custom-call | flops 9342812160 | bytes 15925248 | tf_op jit(solution)/shard_map/pallas_call | solution.py:506
  137.5 28.2 %shard_map.332 = (bf16[528,768]{1,0:T(8,128)(2,1)}, bf16[1536,768]{1,0:T(8,128)(2,1)}, bf16[1536,768]{1,0:T(8,128)(2,1)}, bf16[528,768]{1,0:T(8,128)(2,1)}, f32[...) custom-call(s32[2]{0:T(128)} %pad_add_fusion.position_ref, ...), custom_call_target="tpu_custom_call" | custom-call | flops 14608760832 | bytes 24625152 | tf_op jit(solution)/shard_map/pallas_call | solution.py:506
  170.3 28.8 %shard_map.333 = (bf16[528,768]{1,0:T(8,128)(2,1)}, f32[528,768]{1,0:T(8,128)}, bf16[528,768]{1,0:T(8,128)(2,1)}, f32[1,768]{1,0:T(1,128)}, bf16[4,768,1024]{2,1,0:T(8,128)(2,1)}, /*index=5*/bf16[2048,768]{1,0:T(8,128)(2,1)}) custom-call(s32[2]{0:T(128)} %pad_add_fusion.position_ref, f32[528,768]{1,0:T(8,128)} %get-tuple-element.55.late_ref, ...), custom_call_target="tpu_custom_call" | custom-call | flops 14948499456 | bytes 37748736 | tf_op jit(solution)/shard_map/pallas_call | solution.py:794
  202.2 3.9 dynamic-slice_bitcast_fusion
  206.3 26.8 %shard_map.334 = (bf16[528,768]{1,0:T(8,128)(2,1)}, bf16[1536,768]{1,0:T(8,128)(2,1)}, bf16[1536,768]{1,0:T(8,128)(2,1)}, f32[528,768]{1,0:T(8,128)}, bf16[528,768]{1,0:T(8,128)(2,1)}, /*index=5*/f32[1,768]{1,0:T(1,128)}) custom-call(f32[528,768]{1,0:T(8,128)} %get-tuple-element.58.lg_ref, bf16[528,768]{1,0:T(8,128)(2,1)} %get-tuple-element.59.lgb_ref.b3, ...), custom_call_target="tpu_custom_call" | custom-call | flops 1245708288 | bytes 24330240 | tf_op jit(solution)/shard_map/pallas_call | solution.py:506
  233.1 25.9 %shard_map.335 = (bf16[528,768]{1,0:T(8,128)(2,1)}, bf16[528,768]{1,0:T(8,128)(2,1)}, bf16[528,768]{1,0:T(8,128)(2,1)}, bf16[528,768]{1,0:T(8,128)(2,1)}, f32[1,768]{1,0:T(1,128)}, /*index=5*/f32[16,32]{1,0:T(8,128)}) custom-call(f32[528,768]{1,0:T(8,128)} %get-tuple-element.65.mg_ref, bf16[528,768]{1,0:T(8,128)(2,1)} %get-tuple-element.66.mgb_ref.b3, ...), custom_call_target="tpu_custom_call" | custom-call | flops 2491416576 | bytes 16220160 | tf_op jit(solution)/shard_map/pallas_call | solution.py:506
  261.2 12.6 %shard_map.338 = bf16[4,768,768]{2,1,0:T(8,128)(2,1)} custom-call(bf16[528,768]{1,0:T(8,128)(2,1)} %get-tuple-element.54.n_ref.a0, bf16[1536,768]{1,0:T(8,128)(2,1)} %bitcast.391, bf16[1536,768]{1,0:T(8,128)(2,1)} %bitcast.392, bf16[528,768]{1,0:T(8,128)(2,1)} %get-tuple-element.84.a3, bf16[528,768]{1,0:T(8,128)(2,1)} %get-tuple-element.85.b0, ...), custom_call_target="tpu_custom_call" | custom-call | flops 4869586944 | bytes 17399808 | tf_op jit(solution)/shard_map/pallas_call | solution.py:506
  279.4 8.8 %shard_map.337 = bf16[4,768,768]{2,1,0:T(8,128)(2,1)} custom-call(bf16[528,768]{1,0:T(8,128)(2,1)} %get-tuple-element.79.a0.a1.a2, bf16[528,768]{1,0:T(8,128)(2,1)} %get-tuple-element.79.a0.a1.a2, bf16[528,768]{1,0:T(8,128)(2,1)} %get-tuple-element.79.a0.a1.a2, bf16[528,768]{1,0:T(8,128)(2,1)} %get-tuple-element.80.a3, ...), custom_call_target="tpu_custom_call" | custom-call | flops 2491416576 | bytes 11206656 | tf_op jit(solution)/shard_map/pallas_call | solution.py:506
  295.2 3.4 collective-permute-start.47
  298.6 7.6 %shard_map.336 = bf16[1536,768]{1,0:T(8,128)(2,1)} custom-call(bf16[1536,768]{1,0:T(8,128)(2,1)} %get-tuple-element.73.dk_ref.b1, bf16[1536,768]{1,0:T(8,128)(2,1)} %get-tuple-element.74.dv_ref.b2, bf16[768,768]{1,0:T(8,128)(2,1)} %bitcast.359, bf16[768,768]{1,0:T(8,128)(2,1)} %bitcast.358), custom_call_target="tpu_custom_call" | custom-call | flops 3623878656 | bytes 9437184 | tf_op jit(solution)/shard_map/pallas_call | solution.py:915
  314.4 6.7 %collective-permute-done.78 = bf16[2,2,2,32,768]{4,3,2,1,0:T(8,128)(2,1)} collective-permute-done((bf16[2,2,2,32,768]{4,3,2,1,0:T(8,128)(2,1)}, bf16[2,2,2,32,768]{4,3,2,1,0:T(8,128)(2,1)}, u32[]{:S(2)}, u32[]{:S(2)}) %collective-permute-start.78) | collective-permute-done | bytes 393248 | tf_op jit(solution)/shard_map/ppermute | solution.py:405
  341.8 4.7 %collective-permute-done.81 = bf16[64,768]{1,0:T(8,128)(2,1)S(1)} collective-permute-done((bf16[64,768]{1,0:T(8,128)(2,1)S(1)}, bf16[64,768]{1,0:T(8,128)(2,1)S(1)}, u32[]{:S(2)}, u32[]{:S(2)}) %collective-permute-start.81) | collective-permute-done | bytes 98336 | tf_op jit(solution)/shard_map/ppermute | solution.py:413
  347.9 4.2 collective-permute-done.82
  354.7 7.1 %collective-permute-done.51 = bf16[2,2,2,48,768]{4,3,1,2,0:T(8,128)(2,1)S(1)} collective-permute-done((bf16[2,2,2,48,768]{4,3,1,2,0:T(8,128)(2,1)S(1)}, bf16[2,2,2,48,768]{4,3,1,2,0:T(8,128)(2,1)S(1)}, u32[]{:S(2)}, u32[]{:S(2)}) %collective-permute-start.51) | collective-permute-done | bytes 589856 | tf_op jit(solution)/shard_map/ppermute | solution.py:405
  362.5 5.8 %collective-permute-done.49 = bf16[2,2,2,48,768]{4,3,0,1,2:T(8,128)(2,1)S(1)} collective-permute-done((bf16[2,2,2,48,768]{4,3,0,1,2:T(8,128)(2,1)S(1)}, bf16[2,2,2,48,768]{4,3,0,1,2:T(8,128)(2,1)S(1)}, u32[]{:S(2)}, u32[]{:S(2)}) %collective-permute-start.49) | collective-permute-done | bytes 589856 | tf_op jit(solution)/shard_map/ppermute | solution.py:401
  371.5 3.4 fusion
  383.3 6.4 %collective-permute-done.62 = bf16[2,96,768]{2,1,0:T(8,128)(2,1)S(1)} collective-permute-done((bf16[2,96,768]{2,1,0:T(8,128)(2,1)S(1)}, bf16[2,96,768]{2,1,0:T(8,128)(2,1)S(1)}, u32[]{:S(2)}, u32[]{:S(2)}) %collective-permute-start.62) | collective-permute-done | bytes 294944 | tf_op jit(solution)/shard_map/ppermute | solution.py:409
  393.1 4.2 collective-permute-done.63
  402.2 4.6 %collective-permute-done.70 = bf16[2,2,48,1024]{3,2,1,0:T(8,128)(2,1)S(1)} collective-permute-done((bf16[2,2,48,1024]{3,2,1,0:T(8,128)(2,1)S(1)}, bf16[2,2,48,1024]{3,2,1,0:T(8,128)(2,1)S(1)}, u32[]{:S(2)}, u32[]{:S(2)}) %collective-permute-start.70) | collective-permute-done | bytes 393248 | tf_op jit(solution)/shard_map/ppermute | solution.py:401
  410.2 7.4 %collective-permute-done.71 = bf16[2,96,1024]{2,1,0:T(8,128)(2,1)S(1)} collective-permute-done((bf16[2,96,1024]{2,1,0:T(8,128)(2,1)S(1)}, bf16[2,96,1024]{2,1,0:T(8,128)(2,1)S(1)}, u32[]{:S(2)}, u32[]{:S(2)}) %collective-permute-start.71) | collective-permute-done | bytes 393248 | tf_op jit(solution)/shard_map/ppermute | solution.py:409
  418.1 7.8 %collective-permute-done.72 = bf16[96,1024]{1,0:T(8,128)(2,1)S(1)} collective-permute-done((bf16[96,1024]{1,0:T(8,128)(2,1)S(1)}, bf16[96,1024]{1,0:T(8,128)(2,1)S(1)}, u32[]{:S(2)}, u32[]{:S(2)}) %collective-permute-start.72) | collective-permute-done | bytes 196640 | tf_op jit(solution)/shard_map/ppermute | solution.py:413
  428.0 3.7 collective-permute-done.73
  (366 shorter events, 149.9 us)
Async XLA Ops:
  1.8 30.9 %collective-permute-start.3 = (bf16[1,96,768]{2,1,0:T(8,128)(2,1)S(1)}, bf16[1,96,768]{2,1,0:T(8,128)(2,1)S(1)}, u32[]{:S(2)}, u32[]{:S(2)}) collective-permute-start(bf16[1,96,768]{2,1,0:T(8,128)(2,1)S(1)} %select_bitcast_fusion.1), channel_id=1, source_target_pairs={{0,4},{1,5},{2,6},{3,7},{4,0},{5,1},{6,2},{7,3},{8,12},{9,13},{10,... | collective-permute-start | bytes 442376 | tf_op jit(solution)/shard_map/ppermute | solution.py:413
  8.5 25.7 %collective-permute-start.13 = (bf16[1,96,768]{2,1,0:T(8,128)(2,1)S(1)}, bf16[1,96,768]{2,1,0:T(8,128)(2,1)S(1)}, u32[]{:S(2)}, u32[]{:S(2)}) collective-permute-start(bf16[1,96,768]{2,1,0:T(8,128)(2,1)S(1)} %select_bitcast_fusion), channel_id=1, source_target_pairs={{0,4},{1,5},{2,6},{3,7},{4,0},{5,1},{6,2},{7,3},{8,12},{9,13},{10,... | collective-permute-start | bytes 442376 | tf_op jit(solution)/shard_map/ppermute | solution.py:413
  12.4 22.6 %collective-permute-start.23 = (bf16[1,96,1024]{2,1,0:T(8,128)(2,1)S(1)}, bf16[1,96,1024]{2,1,0:T(8,128)(2,1)S(1)}, u32[]{:S(2)}, u32[]{:S(2)}) collective-permute-start(bf16[1,96,1024]{2,1,0:T(8,128)(2,1)S(1)} %maximum_bitcast_fusion.2), channel_id=1, source_target_pairs={{0,4},{1,5},{2,6},{3,7},{4,0},{5,1},{6,2},{7,3},{8,12},{9,13},{10,... | collective-permute-start | bytes 589832 | tf_op jit(solution)/shard_map/ppermute | solution.py:413
  12.5 19.5 %collective-permute-start.33 = (bf16[1,64,768]{2,1,0:T(8,128)(2,1)S(1)}, bf16[1,64,768]{2,1,0:T(8,128)(2,1)S(1)}, u32[]{:S(2)}, u32[]{:S(2)}) collective-permute-start(bf16[1,64,768]{2,1,0:T(8,128)(2,1)S(1)} %dynamic-slice_bitcast_fusion.20), channel_id=1, source_target_pairs={{0,4},{1,5},{2,6},{3,7},{4,0},{5,1},{6,2},{7,3},{8,12},{9,13},{10,... | collective-permute-start | bytes 294920 | tf_op jit(solution)/shard_map/ppermute | solution.py:413
  27.0 29.4 %collective-permute-start.2 = (bf16[4,336]{1,0:T(4,128)(2,1)S(1)}, bf16[4,336]{1,0:T(4,128)(2,1)S(1)}, u32[]{:S(2)}, u32[]{:S(2)}) collective-permute-start(bf16[4,336]{1,0:T(4,128)(2,1)S(1)} %select_n.320), channel_id=1, source_target_pairs={{0,1},{1,0},{2,3},{3,2},{4,5},{5,4},{6,7},{7,6},{8,9},{9,8},{10,11... | collective-permute-start | bytes 8072 | tf_op jit(solution)/shard_map/ppermute | solution.py:405
  34.2 18.3 %collective-permute-start.14 = (bf16[2,96,768]{2,1,0:T(8,128)(2,1)S(1)}, bf16[2,96,768]{2,1,0:T(8,128)(2,1)S(1)}, u32[]{:S(2)}, u32[]{:S(2)}) collective-permute-start(bf16[2,96,768]{2,1,0:T(8,128)(2,1)S(1)} %pad_maximum_fusion.14), channel_id=1, source_target_pairs={{0,2},{1,3},{2,0},{3,1},{4,6},{5,7},{6,4},{7,5},{8,10},{9,11},{10,... | collective-permute-start | bytes 884744 | tf_op jit(solution)/shard_map/ppermute | solution.py:409
  35.0 24.2 %collective-permute-start.24 = (bf16[2,96,1024]{2,1,0:T(8,128)(2,1)S(1)}, bf16[2,96,1024]{2,1,0:T(8,128)(2,1)S(1)}, u32[]{:S(2)}, u32[]{:S(2)}) collective-permute-start(bf16[2,96,1024]{2,1,0:T(8,128)(2,1)S(1)} %pad_maximum_fusion.9), channel_id=1, source_target_pairs={{0,2},{1,3},{2,0},{3,1},{4,6},{5,7},{6,4},{7,5},{8,10},{9,11},{10,... | collective-permute-start | bytes 1179656 | tf_op jit(solution)/shard_map/ppermute | solution.py:409
  75.2 19.9 %collective-permute-start.8 = (bf16[2,4,48,768]{3,2,1,0:T(8,128)(2,1)S(1)}, bf16[2,4,48,768]{3,2,1,0:T(8,128)(2,1)}, u32[]{:S(2)}, u32[]{:S(2)}) collective-permute-start(bf16[2,4,48,768]{3,2,1,0:T(8,128)(2,1)S(1)} %pad_maximum_fusion.5.refs_2_), channel_id=1, source_target_pairs={{0,1},{1,0},{2,3},{3,2},{4,5},{5,4},{6,7},{7,6},{8,9},{9,8},{10,11... | collective-permute-start | bytes 1769480 | tf_op jit(solution)/shard_map/ppermute | solution.py:405
  77.1 19.3 %collective-permute-start.6 = (bf16[2,4,48,768]{3,2,1,0:T(8,128)(2,1)S(1)}, bf16[2,4,48,768]{3,2,1,0:T(8,128)(2,1)}, u32[]{:S(2)}, u32[]{:S(2)}) collective-permute-start(bf16[2,4,48,768]{3,2,1,0:T(8,128)(2,1)S(1)} %pad_maximum_fusion.4.refs_0_), channel_id=1, source_target_pairs={{0,16},{8,24},{16,0},{24,8},{1,17},{9,25},{17,1},{25,9},{2,18},{10... | collective-permute-start | bytes 1769480 | tf_op jit(solution)/shard_map/ppermute | solution.py:401
  77.2 19.4 %collective-permute-start.11 = (bf16[2,4,48,768]{3,2,1,0:T(8,128)(2,1)S(1)}, bf16[2,4,48,768]{3,2,1,0:T(8,128)(2,1)}, u32[]{:S(2)}, u32[]{:S(2)}) collective-permute-start(bf16[2,4,48,768]{3,2,1,0:T(8,128)(2,1)S(1)} %pad_maximum_fusion.5.refs_2_), channel_id=1, source_target_pairs={{0,8},{8,0},{16,24},{24,16},{1,9},{9,1},{17,25},{25,17},{2,10},{10... | collective-permute-start | bytes 1769480 | tf_op jit(solution)/shard_map/ppermute | solution.py:397
  107.7 27.8 %collective-permute-start.21 = (bf16[2,4,48,768]{3,2,1,0:T(8,128)(2,1)}, bf16[2,4,48,768]{3,2,1,0:T(8,128)(2,1)S(1)}, u32[]{:S(2)}, u32[]{:S(2)}) collective-permute-start(bf16[2,4,48,768]{3,2,1,0:T(8,128)(2,1)} %pad_maximum_fusion.8.refs_2_), channel_id=1, source_target_pairs={{0,8},{8,0},{16,24},{24,16},{1,9},{9,1},{17,25},{25,17},{2,10},{10... | collective-permute-start | bytes 1769480 | tf_op jit(solution)/shard_map/ppermute | solution.py:397
  111.2 25.1 %collective-permute-start.26 = (bf16[2,4,48,1024]{3,2,1,0:T(8,128)(2,1)S(1)}, bf16[2,4,48,1024]{3,2,1,0:T(8,128)(2,1)S(1)}, u32[]{:S(2)}, u32[]{:S(2)}) collective-permute-start(bf16[2,4,48,1024]{3,2,1,0:T(8,128)(2,1)S(1)} %pad_maximum_fusion.1.refs_0_), channel_id=1, source_target_pairs={{0,16},{8,24},{16,0},{24,8},{1,17},{9,25},{17,1},{25,9},{2,18},{10... | collective-permute-start | bytes 2359304 | tf_op jit(solution)/shard_map/ppermute | solution.py:401
  111.9 24.5 %collective-permute-start.28 = (bf16[2,4,48,1024]{3,2,1,0:T(8,128)(2,1)S(1)}, bf16[2,4,48,1024]{3,2,1,0:T(8,128)(2,1)S(1)}, u32[]{:S(2)}, u32[]{:S(2)}) collective-permute-start(bf16[2,4,48,1024]{3,2,1,0:T(8,128)(2,1)S(1)} %pad_maximum_fusion.2.refs_2_), channel_id=1, source_target_pairs={{0,1},{1,0},{2,3},{3,2},{4,5},{5,4},{6,7},{7,6},{8,9},{9,8},{10,11... | collective-permute-start | bytes 2359304 | tf_op jit(solution)/shard_map/ppermute | solution.py:405
  113.2 23.8 %collective-permute-start.20 = (bf16[2,4,48,768]{3,2,1,0:T(8,128)(2,1)}, bf16[2,4,48,768]{3,2,1,0:T(8,128)(2,1)}, u32[]{:S(2)}, u32[]{:S(2)}) collective-permute-start(bf16[2,4,48,768]{3,2,1,0:T(8,128)(2,1)} %collective-permute-done.16.refs_1_), channel_id=1, source_target_pairs={{0,8},{8,0},{16,24},{24,16},{1,9},{9,1},{17,25},{25,17},{2,10},{10... | collective-permute-start | bytes 1769480 | tf_op jit(solution)/shard_map/ppermute | solution.py:397
  113.2 23.8 %collective-permute-start.22 = (bf16[2,4,48,768]{3,2,1,0:T(8,128)(2,1)}, bf16[2,4,48,768]{3,2,1,0:T(8,128)(2,1)}, u32[]{:S(2)}, u32[]{:S(2)}) collective-permute-start(bf16[2,4,48,768]{3,2,1,0:T(8,128)(2,1)} %collective-permute-done.18.refs_3_), channel_id=1, source_target_pairs={{0,8},{8,0},{16,24},{24,16},{1,9},{9,1},{17,25},{25,17},{2,10},{10... | collective-permute-start | bytes 1769480 | tf_op jit(solution)/shard_map/ppermute | solution.py:397
  135.5 33.4 %collective-permute-start.42 = (bf16[2,4,32,768]{3,2,1,0:T(8,128)(2,1)S(1)}, bf16[2,4,32,768]{3,2,1,0:T(8,128)(2,1)}, u32[]{:S(2)}, u32[]{:S(2)}) collective-permute-start(bf16[2,4,32,768]{3,2,1,0:T(8,128)(2,1)S(1)} %copy-done.28), channel_id=1, source_target_pairs={{0,8},{8,0},{16,24},{24,16},{1,9},{9,1},{17,25},{25,17},{2,10},{10... | collective-permute-start | bytes 1179656 | tf_op jit(solution)/shard_map/ppermute | solution.py:397
  136.3 32.5 %collective-permute-start.29 = (bf16[2,4,48,1024]{3,2,1,0:T(8,128)(2,1)S(1)}, bf16[2,4,48,1024]{3,2,1,0:T(8,128)(2,1)S(1)}, u32[]{:S(2)}, u32[]{:S(2)}) collective-permute-start(bf16[2,4,48,1024]{3,2,1,0:T(8,128)(2,1)S(1)} %pad_maximum_fusion.1.refs_0_), channel_id=1, source_target_pairs={{0,8},{8,0},{16,24},{24,16},{1,9},{9,1},{17,25},{25,17},{2,10},{10... | collective-permute-start | bytes 2359304 | tf_op jit(solution)/shard_map/ppermute | solution.py:397
  136.5 32.5 %collective-permute-start.31 = (bf16[2,4,48,1024]{3,2,1,0:T(8,128)(2,1)S(1)}, bf16[2,4,48,1024]{3,2,1,0:T(8,128)(2,1)S(1)}, u32[]{:S(2)}, u32[]{:S(2)}) collective-permute-start(bf16[2,4,48,1024]{3,2,1,0:T(8,128)(2,1)S(1)} %pad_maximum_fusion.2.refs_2_), channel_id=1, source_target_pairs={{0,8},{8,0},{16,24},{24,16},{1,9},{9,1},{17,25},{25,17},{2,10},{10... | collective-permute-start | bytes 2359304 | tf_op jit(solution)/shard_map/ppermute | solution.py:397
  137.0 31.9 %collective-permute-start.30 = (bf16[2,4,48,1024]{3,2,1,0:T(8,128)(2,1)S(1)}, bf16[2,4,48,1024]{3,2,1,0:T(8,128)(2,1)S(1)}, u32[]{:S(2)}, u32[]{:S(2)}) collective-permute-start(bf16[2,4,48,1024]{3,2,1,0:T(8,128)(2,1)S(1)} %collective-permute-done.26.refs_1_), channel_id=1, source_target_pairs={{0,8},{8,0},{16,24},{24,16},{1,9},{9,1},{17,25},{25,17},{2,10},{10... | collective-permute-start | bytes 2359304 | tf_op jit(solution)/shard_map/ppermute | solution.py:397
  137.1 31.9 %collective-permute-start.32 = (bf16[2,4,48,1024]{3,2,1,0:T(8,128)(2,1)S(1)}, bf16[2,4,48,1024]{3,2,1,0:T(8,128)(2,1)}, u32[]{:S(2)}, u32[]{:S(2)}) collective-permute-start(bf16[2,4,48,1024]{3,2,1,0:T(8,128)(2,1)S(1)} %collective-permute-done.28.refs_3_), channel_id=1, source_target_pairs={{0,8},{8,0},{16,24},{24,16},{1,9},{9,1},{17,25},{25,17},{2,10},{10... | collective-permute-start | bytes 2359304 | tf_op jit(solution)/shard_map/ppermute | solution.py:397
  201.8 104.5 %collective-permute-start.75 = (bf16[2,2,2,2,64,768]{5,4,3,2,1,0:T(8,128)(2,1)}, bf16[2,2,2,2,64,768]{5,4,3,2,1,0:T(8,128)(2,1)}, u32[]{:S(2)}, u32[]{:S(2)}) collective-permute-start(bf16[2,2,2,2,64,768]{5,4,3,2,1,0:T(8,128)(2,1)} %dynamic-slice_bitcast_fusion.2), channel_id=1, source_target_pairs={{0,8},{8,0},{16,24},{24,16},{1,9},{9,1},{17,25},{25,17},{2,10},{10... | collective-permute-start | bytes 4718600 | tf_op jit(solution)/shard_map/ppermute | solution.py:397
  206.2 163.7 %collective-permute-start.66 = (bf16[2,2,2,2,96,1024]{5,4,3,2,1,0:T(8,128)(2,1)}, bf16[2,2,2,2,96,1024]{5,4,3,2,1,0:T(8,128)(2,1)}, u32[]{:S(2)}, u32[]{:S(2)}) collective-permute-start(bf16[2,2,2,2,96,1024]{5,4,3,2,1,0:T(8,128)(2,1)} %dynamic-slice_bitcast_fusion), channel_id=1, source_target_pairs={{0,8},{8,0},{16,24},{24,16},{1,9},{9,1},{17,25},{25,17},{2,10},{10... | collective-permute-start | bytes 9437192 | tf_op jit(solution)/shard_map/ppermute | solution.py:397
  278.8 53.3 %collective-permute-start.57 = (bf16[2,2,2,2,96,768]{5,4,3,2,1,0:T(8,128)(2,1)}, bf16[2,2,2,2,96,768]{5,4,3,2,1,0:T(8,128)(2,1)}, u32[]{:S(2)}, u32[]{:S(2)}) collective-permute-start(bf16[2,2,2,2,96,768]{5,4,3,2,1,0:T(8,128)(2,1)} %dynamic-slice_bitcast_fusion.1), channel_id=1, source_target_pairs={{0,8},{8,0},{16,24},{24,16},{1,9},{9,1},{17,25},{25,17},{2,10},{10... | collective-permute-start | bytes 7077896 | tf_op jit(solution)/shard_map/ppermute | solution.py:397
  295.2 42.0 %collective-permute-start.48 = (bf16[2,2,2,2,96,768]{5,4,1,2,0,3:T(8,128)(2,1)}, bf16[2,2,2,2,96,768]{5,4,1,2,0,3:T(8,128)(2,1)}, u32[]{:S(2)}, u32[]{:S(2)}) collective-permute-start(bf16[2,2,2,2,96,768]{5,4,1,2,0,3:T(8,128)(2,1)} %bitcast.327), channel_id=1, source_target_pairs={{0,8},{8,0},{16,24},{24,16},{1,9},{9,1},{17,25},{25,17},{2,10},{10... | collective-permute-start | bytes 7077896 | tf_op jit(solution)/shard_map/ppermute | solution.py:397
  335.6 18.0 %collective-permute-start.60 = (bf16[2,2,2,48,768]{4,3,2,1,0:T(8,128)(2,1)S(1)}, bf16[2,2,2,48,768]{4,3,2,1,0:T(8,128)(2,1)S(1)}, u32[]{:S(2)}, u32[]{:S(2)}) collective-permute-start(bf16[2,2,2,48,768]{4,3,2,1,0:T(8,128)(2,1)S(1)} %dynamic-slice_bitcast_fusion.4), channel_id=1, source_target_pairs={{0,1},{1,0},{2,3},{3,2},{4,5},{5,4},{6,7},{7,6},{8,9},{9,8},{10,11... | collective-permute-start | bytes 1769480 | tf_op jit(solution)/shard_map/ppermute | solution.py:405
  336.3 17.5 %collective-permute-start.58 = (bf16[2,2,2,48,768]{4,3,1,0,2:T(8,128)(2,1)S(1)}, bf16[2,2,2,48,768]{4,3,1,0,2:T(8,128)(2,1)S(1)}, u32[]{:S(2)}, u32[]{:S(2)}) collective-permute-start(bf16[2,2,2,48,768]{4,3,1,0,2:T(8,128)(2,1)S(1)} %bitcast.368), channel_id=1, source_target_pairs={{0,16},{8,24},{16,0},{24,8},{1,17},{9,25},{17,1},{25,9},{2,18},{10... | collective-permute-start | bytes 1769480 | tf_op jit(solution)/shard_map/ppermute | solution.py:401
  340.7 21.1 %collective-permute-start.51 = (bf16[2,2,2,48,768]{4,3,1,2,0:T(8,128)(2,1)S(1)}, bf16[2,2,2,48,768]{4,3,1,2,0:T(8,128)(2,1)S(1)}, u32[]{:S(2)}, u32[]{:S(2)}) collective-permute-start(bf16[2,2,2,48,768]{4,3,1,2,0:T(8,128)(2,1)S(1)} %dynamic-slice_bitcast_fusion.5), channel_id=1, source_target_pairs={{0,1},{1,0},{2,3},{3,2},{4,5},{5,4},{6,7},{7,6},{8,9},{9,8},{10,11... | collective-permute-start | bytes 1769480 | tf_op jit(solution)/shard_map/ppermute | solution.py:405
  353.5 54.8 %collective-permute-start.83 = (bf16[2,64,768]{2,1,0:T(8,128)(2,1)S(1)}, bf16[2,64,768]{2,1,0:T(8,128)(2,1)S(1)}, u32[]{:S(2)}, u32[]{:S(2)}) collective-permute-start(bf16[2,64,768]{2,1,0:T(8,128)(2,1)S(1)} %maximum_select_fusion.10), channel_id=1, source_target_pairs={{0,8},{8,0},{16,24},{24,16},{1,9},{9,1},{17,25},{25,17},{2,10},{10... | collective-permute-start | bytes 589832 | tf_op jit(solution)/shard_map/ppermute | solution.py:397
  353.8 21.7 %collective-permute-start.61 = (bf16[2,2,48,768]{3,2,1,0:T(8,128)(2,1)S(1)}, bf16[2,2,48,768]{3,2,1,0:T(8,128)(2,1)S(1)}, u32[]{:S(2)}, u32[]{:S(2)}) collective-permute-start(bf16[2,2,48,768]{3,2,1,0:T(8,128)(2,1)S(1)} %dynamic-slice_bitcast_fusion.10), channel_id=1, source_target_pairs={{0,16},{8,24},{16,0},{24,8},{1,17},{9,25},{17,1},{25,9},{2,18},{10... | collective-permute-start | bytes 884744 | tf_op jit(solution)/shard_map/ppermute | solution.py:401
  375.6 22.8 %collective-permute-start.69 = (bf16[2,2,2,48,1024]{4,3,2,1,0:T(8,128)(2,1)S(1)}, bf16[2,2,2,48,1024]{4,3,2,1,0:T(8,128)(2,1)S(1)}, u32[]{:S(2)}, u32[]{:S(2)}) collective-permute-start(bf16[2,2,2,48,1024]{4,3,2,1,0:T(8,128)(2,1)S(1)} %dynamic-slice_bitcast_fusion.3), channel_id=1, source_target_pairs={{0,1},{1,0},{2,3},{3,2},{4,5},{5,4},{6,7},{7,6},{8,9},{9,8},{10,11... | collective-permute-start | bytes 2359304 | tf_op jit(solution)/shard_map/ppermute | solution.py:405
  376.2 23.6 %collective-permute-start.67 = (bf16[2,2,2,48,1024]{4,3,1,0,2:T(8,128)(2,1)S(1)}, bf16[2,2,2,48,1024]{4,3,1,0,2:T(8,128)(2,1)S(1)}, u32[]{:S(2)}, u32[]{:S(2)}) collective-permute-start(bf16[2,2,2,48,1024]{4,3,1,0,2:T(8,128)(2,1)S(1)} %bitcast.365), channel_id=1, source_target_pairs={{0,16},{8,24},{16,0},{24,8},{1,17},{9,25},{17,1},{25,9},{2,18},{10... | collective-permute-start | bytes 2359304 | tf_op jit(solution)/shard_map/ppermute | solution.py:401
  409.6 22.2 %collective-permute-start.56 = (bf16[2,96,768]{2,1,0:T(8,128)(2,1)S(1)}, bf16[2,96,768]{2,1,0:T(8,128)(2,1)S(1)}, u32[]{:S(2)}, u32[]{:S(2)}) collective-permute-start(bf16[2,96,768]{2,1,0:T(8,128)(2,1)S(1)} %maximum_select_fusion.6), channel_id=1, source_target_pairs={{0,8},{8,0},{16,24},{24,16},{1,9},{9,1},{17,25},{25,17},{2,10},{10... | collective-permute-start | bytes 884744 | tf_op jit(solution)/shard_map/ppermute | solution.py:397
  (85 other events, 998.7 us)

commit v3 on v0

--- a/solution.py
+++ b/solution.py
@@ -3,6 +3,8 @@
 import jax
 import jax.numpy as jnp
 from jax import lax
+from jax.experimental import pallas as pl
+from jax.experimental.pallas import tpu as pltpu
 from jax.sharding import PartitionSpec as P
 
 HEADS = 12
@@ -30,6 +32,9 @@
     distance = jnp.maximum(positions[:, None] - positions[None, :], 0)
     levels = jnp.arange(BUCKETS, dtype=jnp.int32)
     return (bucket_of(distance)[None] == levels[:, None, None]).astype(jnp.bfloat16)
+
+
+PARTS = 4
 
 
 def rms_scale(values, gain):
@@ -380,6 +385,1049 @@
     )
 
 
+CORE, ROW = [(i, i ^ 1) for i in range(4)], [(i, i ^ 2) for i in range(4)]
+ACROSS, NEAR, FAR = (
+    [(i, i ^ 1) for i in range(8)],
+    [(i, i ^ 2) for i in range(8)],
+    [(i, i ^ 4) for i in range(8)],
+)
+
+
+def over_core(values):
+    return lax.ppermute(values, "rep", CORE)
+
+
+def over_row(values):
+    return lax.ppermute(values, "rep", ROW)
+
+
+def over_across(values):
+    return lax.ppermute(values, "fsdp", ACROSS)
+
+
+def over_near(values):
+    return lax.ppermute(values, "fsdp", NEAR)
+
+
+def over_far(values):
+    return lax.ppermute(values, "fsdp", FAR)
+
+
+def pick(values, index, axis):
+    return lax.dynamic_index_in_dim(values, index, axis, keepdims=False)
+
+
+def after(value, *others):
+    return lax.optimization_barrier((value, *others))[0]
+
+
+def gather_far(part):
+    held = part[None]
+    return jnp.concatenate([held, over_far(held)], 0)
+
+
+def gather_near(held):
+    return jnp.concatenate([held, over_near(held)], 0)
+
+
+def gather_one(held):
+    half = held.shape[1] // 16 * 8
+    first, second = held[:, :half], held[:, half:]
+    return jnp.stack([first, over_across(first)]), jnp.stack([second, over_row(second)])
+
+
+def gather_two(pair):
+    return over_row(pair[0]), over_across(pair[1])
+
+
+def gather_core(pair):
+    return over_core(pair[0]), over_core(pair[1])
+
+
+def in_order(one, two, core_one, core_two):
+    return [one[0], two[0], one[1], two[1], core_one[0], core_two[0], core_one[1], core_two[1]]
+
+
+def add_up(kept, received):
+    return (kept.astype(jnp.float32) + received.astype(jnp.float32)).astype(jnp.bfloat16)
+
+
+class Scatter:
+    MOVES = {"core": over_core, "row": over_row, "across": over_across, "near": over_near, "far": over_far}
+
+    def __init__(self, position, keep, send):
+        part, shard = position[0], position[1]
+        self.bit = {"core": part & 1, "row": part >> 1, "across": shard & 1, "near": (shard >> 1) & 1, "far": shard >> 2}
+        self.shape = keep.shape[2:]
+        full = (2, 2, 2, 2) + self.shape
+        self.keep, self.got = keep.reshape(full), over_core(send.reshape(full))
+
+    def fold(self, values, names, name):
+        axis = names.index(name)
+        kept, sent = pick(values, self.bit[name], axis), pick(values, 1 - self.bit[name], axis)
+        return kept, sent, [n for n in names if n != name]
+
+    def ready_one(self, *gates):
+        got = after(self.got, *gates)
+        sums = add_up(self.keep, got)
+        half = self.shape[0] // 16 * 8
+        names = ["row", "far", "near", "across"]
+        self.kept_first, self.sent_first, self.first = self.fold(sums[..., :half, :], names, "row")
+        self.kept_second, self.sent_second, self.second = self.fold(sums[..., half:, :], names, "across")
+        return self.sent_first, self.sent_second
+
+    def move_one(self):
+        self.got_first, self.got_second = over_row(self.sent_first), over_across(self.sent_second)
+
+    def ready_two(self, *gates):
+        first = add_up(self.kept_first, after(self.got_first, *gates))
+        second = add_up(self.kept_second, after(self.got_second, *gates))
+        self.kept_first, self.sent_first, self.first = self.fold(first, self.first, "across")
+        self.kept_second, self.sent_second, self.second = self.fold(second, self.second, "row")
+        return self.sent_first, self.sent_second
+
+    def move_two(self):
+        self.got_first, self.got_second = over_across(self.sent_first), over_row(self.sent_second)
+
+    def ready_three(self, *gates):
+        first = add_up(self.kept_first, after(self.got_first, *gates))
+        second = add_up(self.kept_second, after(self.got_second, *gates))
+        sums = jnp.concatenate([first, second], 2)
+        self.kept, self.sent, self.names = self.fold(sums, ["far", "near"], "near")
+        return (self.sent,)
+
+    def move_three(self):
+        self.got = over_near(self.sent)
+
+    def ready_four(self, *gates):
+        sums = add_up(self.kept, after(self.got, *gates))
+        self.kept, self.sent, self.names = self.fold(sums, self.names, "far")
+        return (self.sent,)
+
+    def move_four(self):
+        self.got = over_far(self.sent)
+
+    def sent_now(self):
+        return (self.sent,)
+
+    def total(self, *gates):
+        self.sums = add_up(self.kept, after(self.got, *gates))
+        return self.sums
+
+    def move_row(self):
+        self.other = over_row(self.sums)
+
+    def finish(self, *gates):
+        sums, other = self.sums, after(self.other, *gates)
+        both = jnp.where(self.bit["row"] == 0, jnp.stack([sums, other]), jnp.stack([other, sums]))
+        others = over_core(both)
+        both = jnp.where(self.bit["core"] == 0, jnp.stack([both, others], 1), jnp.stack([others, both], 1))
+        return both.reshape((PARTS,) + self.shape)
+
+
+BF16, F32 = jnp.bfloat16, jnp.float32
+VMEM_LIMIT = 58 * 1024 * 1024
+ANYWHERE = pl.BlockSpec(memory_space=pltpu.HBM)
+SCALARS = pl.BlockSpec(memory_space=pltpu.SMEM)
+LOCAL = pl.BlockSpec(memory_space=pltpu.VMEM)
+PAIR = 2 * HEAD
+SPAN = 256
+EXTRA = 8
+
+
+def mul(a, b):
+    return lax.dot_general(a, b, (((1,), (0,)), ((), ())), preferred_element_type=F32)
+
+
+def mul_right_t(a, b):
+    return lax.dot_general(a, b, (((1,), (1,)), ((), ())), preferred_element_type=F32)
+
+
+def mul_left_t(a, b):
+    return lax.dot_general(a, b, (((0,), (0,)), ((), ())), preferred_element_type=F32)
+
+
+def exact(a, b, dims):
+    return lax.dot_general(
+        a, b, (dims, ((), ())), precision=lax.Precision.HIGHEST, preferred_element_type=F32
+    )
+
+
+def shape_of(*shape, kind=BF16):
+    return jax.ShapeDtypeStruct(shape, kind)
+
+
+class Inward:
+    def __init__(self, source, target, semaphore):
+        self.copy, self.target = pltpu.make_async_copy(source, target, semaphore), target
+        self.copy.start()
+        self.waiting = True
+
+    def __call__(self):
+        if self.waiting:
+            self.copy.wait()
+            self.waiting = False
+        return self.target
+
+
+class Outward:
+    def __init__(self, source, target, semaphore):
+        self.copy, self.ref = pltpu.make_async_copy(source, target, semaphore), source
+        self.sent = False
+
+    def send(self):
+        if not self.sent:
+            self.copy.start()
+            self.sent = True
+
+
+def cost_of(micros):
+    return pl.CostEstimate(flops=int(micros * 1.15e9), transcendentals=0, bytes_accessed=0)
+
+
+def part_of(operand):
+    array, *where = operand if isinstance(operand, tuple) else (operand,)
+    if len(where) == 2:
+        return array, (pl.ds(*where),), (where[1],) + array.shape[1:]
+    if len(where) == 1:
+        return array, (where[0],), array.shape[1:]
+    return array, (), array.shape
+
+
+def call(kernel, outs, operands, raw=(), raw_outs=(), scratch=(), micros=1, position=None):
+    parts = [part_of(o) for o in operands]
+    n_in, n_out = len(parts), len(outs)
+    lead = [] if position is None else [position]
+
+    def body(*refs):
+        refs = list(refs)
+        take = lambda n: [refs.pop(0) for _ in range(n)]
+        place = take(len(lead))
+        sources, raws, targets, raw_targets = take(n_in), take(len(raw)), take(n_out), take(len(raw_outs))
+        buffers, results = take(n_in), take(n_out)
+        in_done, out_done = take(1)[0], take(1)[0]
+        inward = [
+            Inward(source.at[where] if where else source, buffer, in_done.at[i])
+            for i, (source, (_, where, _), buffer) in enumerate(zip(sources, parts, buffers))
+        ]
+        outward = [Outward(r, t, out_done.at[i]) for i, (r, t) in enumerate(zip(results, targets))]
+        kernel(inward, outward, place + raws, raw_targets, refs)
+        for each in inward:
+            each()
+        for each in outward:
+            each.send()
+        for each in outward:
+            each.copy.wait()
+
+    return pl.pallas_call(
+        body,
+        out_shape=list(outs) + list(raw_outs),
+        in_specs=[SCALARS] * len(lead) + [ANYWHERE] * (n_in + len(raw)),
+        out_specs=[ANYWHERE] * (n_out + len(raw_outs)),
+        scratch_shapes=[pltpu.VMEM(shape, array.dtype) for array, _, shape in parts]
+        + [pltpu.VMEM(o.shape, o.dtype) for o in outs]
+        + [pltpu.SemaphoreType.DMA((max(n_in, 1),)), pltpu.SemaphoreType.DMA((max(n_out, 1),))]
+        + list(scratch),
+        compiler_params=pltpu.CompilerParams(vmem_limit_bytes=VMEM_LIMIT),
+        cost_estimate=cost_of(micros),
+    )(*lead, *[array for array, _, _ in parts], *raw)
+
+
+def relative(core, kind, outer, inner):
+    row, across = (kind, outer) if kind < 2 else (outer, kind - 2)
+    return core + 2 * row, across + 4 * (inner & 1) + 2 * (inner >> 1)
+
+
+def start_pieces(position_ref, sources, target_ref, semaphore_of, by_shard):
+    total = target_ref.shape[2]
+    low = sources[0].shape[2]
+    for core in range(2):
+        for kind in range(4):
+            for outer in range(2):
+                for inner in range(4):
+                    part, shard = relative(core, kind, outer, inner)
+                    part, shard = position_ref[0] ^ part, position_ref[1] ^ shard
+                    place = (shard, part) if by_shard else (part, shard)
+                    start, size = (0, low) if kind < 2 else (low, total - low)
+                    pltpu.make_async_copy(
+                        sources[core * 4 + kind].at[outer, inner, pl.ds(0, size)],
+                        target_ref.at[place[0], place[1], pl.ds(start, size)],
+                        semaphore_of(place[0]),
+                    ).start()
+
+
+def start_extra(position_ref, sources, rows, target_ref, semaphore):
+    skip = rows - sources[0].shape[2]
+    for kind in (2, 3):
+        for inner in range(4):
+            shard = position_ref[1] ^ relative(0, kind, 0, inner)[1]
+            pltpu.make_async_copy(
+                sources[kind].at[0, inner, pl.ds(skip, EXTRA)], target_ref.at[shard], semaphore
+            ).start()
+
+
+def wait_block(target_ref, index, semaphore):
+    pltpu.make_async_copy(target_ref.at[index], target_ref.at[index], semaphore).wait()
+
+
+def flat(ref):
+    block = ref[...]
+    return block.reshape(-1, block.shape[-1])
+
+
+def matrix(ref, index):
+    block = ref[index]
+    return block.reshape(-1, block.shape[-1])
+
+
+def normed(values, gain):
+    scale = lax.rsqrt(jnp.mean(values * values, axis=-1, keepdims=True) + norm_epsilon)
+    return values * scale * gain
+
+
+def norm_back(values, gain, grads):
+    scale = lax.rsqrt(jnp.mean(values * values, axis=-1, keepdims=True) + norm_epsilon)
+    weighted = grads * gain
+    mean = jnp.mean(weighted * values, axis=-1, keepdims=True)
+    return (
+        scale * weighted - values * (scale * scale * scale * mean),
+        jnp.sum(grads * values * scale, axis=0, keepdims=True),
+    )
+
+
+def spread_pair(pair):
+    low = lax.broadcasted_iota(jnp.int32, pair.shape, 1) < HEAD
+    zero = jnp.zeros_like(pair)
+    return jnp.concatenate([jnp.where(low, pair, zero), jnp.where(low, zero, pair)], 0)
+
+
+def join_pair(both):
+    rows = both.shape[0] // 2
+    low = lax.broadcasted_iota(jnp.int32, (rows, PAIR), 1) < HEAD
+    return jnp.where(low, both[:rows], both[rows:])
+
+
+def distance_levels(backward):
+    place = lax.broadcasted_iota(jnp.int32, (BUCKETS, SPAN), 1)
+    distance = (SPAN - place) % SPAN if backward else place
+    level = lax.broadcasted_iota(jnp.int32, (BUCKETS, SPAN), 0)
+    return (bucket_of(distance) == level).astype(F32)
+
+
+def fill_bias(table, bias_ref):
+    length = bias_ref.shape[1]
+    rows = mul_left_t(table.astype(BF16), distance_levels(True).astype(BF16))
+    for head in range(HEADS):
+        row = jnp.broadcast_to(rows[head : head + 1], (length, SPAN))
+        bias_ref[head] = pltpu.roll(row, 0, 1, stride=1, stride_axis=0)[:, :length]
+
+
+def mask_twice(column_ref, row_ref, row, causal):
+    near = column_ref[...] == row_ref[row : row + 1, :]
+    if causal:
+        i = lax.broadcasted_iota(jnp.int32, near.shape, 0)
+        j = lax.broadcasted_iota(jnp.int32, near.shape, 1)
+        near = near & (j <= i)
+    return near
+
+
+def pair_scores(queries, keys, pair, near, bias_ref):
+    scores = mul_right_t(queries, keys)
+    if bias_ref is not None:
+        scores = scores + jnp.concatenate([bias_ref[2 * pair], bias_ref[2 * pair + 1]], 0)
+    return jnp.where(jnp.concatenate([near, near], 0), scores, masked_score)
+
+
+def attend_pairs(near_of, q_ref, k_ref, v_ref, c_ref, t_ref, bias_ref):
+    length = q_ref.shape[0]
+    lane = lax.broadcasted_iota(jnp.int32, (length, 128), 1)
+    t_ref[...] = jnp.zeros_like(t_ref)
+
+    def step(pair, carry):
+        lanes = pl.ds(pl.multiple_of(pair * PAIR, PAIR), PAIR)
+        scores = pair_scores(spread_pair(q_ref[:, lanes]), k_ref[:, lanes], pair, near_of(), bias_ref)
+        highest = jnp.max(scores, axis=1, keepdims=True)
+        expanded = jnp.exp(scores - highest)
+        totals = jnp.sum(expanded, axis=1, keepdims=True)
+        weights = (expanded * (1.0 / totals)).astype(BF16)
+        c_ref[:, lanes] = join_pair(mul(weights, v_ref[:, lanes])).astype(BF16)
+        totals = highest + jnp.log(totals)
+        held = jnp.where(lane == 2 * pair, totals[:length], t_ref[...])
+        t_ref[...] = jnp.where(lane == 2 * pair + 1, totals[length:], held)
+        return carry
+
+    lax.fori_loop(0, HEADS // 2, step, 0)
+
+
+def attend_pairs_back(near_of, q_ref, k_ref, v_ref, t_ref, g_ref, dq_ref, dk_ref, dv_ref, bias_ref, sum_ref):
+    length = q_ref.shape[0]
+    lane = lax.broadcasted_iota(jnp.int32, (length, 128), 1)
+
+    def step(pair, carry):
+        lanes = pl.ds(pl.multiple_of(pair * PAIR, PAIR), PAIR)
+        queries, keys, values = spread_pair(q_ref[:, lanes]), k_ref[:, lanes], v_ref[:, lanes]
+        grads = spread_pair(g_ref[:, lanes])
+        scores = pair_scores(queries, keys, pair, near_of(), bias_ref)
+        held = t_ref[...]
+        of = lambda head: jnp.sum(jnp.where(lane == head, held, 0.0), axis=1, keepdims=True)
+        weights = jnp.exp(scores - jnp.concatenate([of(2 * pair), of(2 * pair + 1)], 0))
+        weight_grads = mul_right_t(grads, values)
+        row_dot = jnp.sum(weights * weight_grads, axis=1, keepdims=True)
+        score_grads = (weights * (weight_grads - row_dot)).astype(BF16)
+        dq_ref[:, lanes] = join_pair(mul(score_grads, keys)).astype(BF16)
+        dk_ref[:, lanes] = mul_left_t(score_grads, queries).astype(BF16)
+        dv_ref[:, lanes] = mul_left_t(weights.astype(BF16), grads).astype(BF16)
+        if sum_ref is not None:
+            for head in range(2):
+                sum_ref[2 * pair + head] = score_grads[head * length : (head + 1) * length]
+        return carry
+
+    lax.fori_loop(0, HEADS // 2, step, 0)
+
+
+def self_forward(index, position, dec, column, segments, given):
+    rows = segments.shape[0]
+    length, features = dec.shape[0] // rows, dec.shape[1]
+    first = index == 0
+
+    def kernel(inward, outward, raw, raw_outs, scratch):
+        if first:
+            position_ref, sources = raw[0], raw[1:]
+            m_ref, extra_ref, done, extra_done, m_done = scratch
+            start_extra(position_ref, sources, m_ref.shape[2], extra_ref, extra_done)
+            start_pieces(position_ref, sources, m_ref, lambda i: done.at[i], False)
+            dec_in, column_in, row_in = inward
+            gain_ref, table_ref, bias_ref = (o.ref for o in outward[8:])
+            pltpu.make_async_copy(extra_ref, extra_ref, extra_done).wait()
+            total = jnp.zeros((EXTRA, features), F32)
+            for shard in range(8):
+                held = extra_ref[shard].astype(F32)
+                total = total + held
+                table_ref[4 * shard : 4 * shard + 4, :] = held[4:8, :128]
+            gain_ref[...] = total
+            fill_bias(table_ref[...], bias_ref)
+            for out in outward[8:]:
+                out.send()
+
+            def weights(i):
+                wait_block(m_ref, i, done.at[i])
+                pltpu.make_async_copy(m_ref.at[i], raw_outs[i], m_done.at[i]).start()
+                return matrix(m_ref, i)
+        else:
+            dec_in, gain_in, q_in, k_in, v_in, column_in, row_in, bias_in, o_in = inward
+            weights = lambda i: flat((q_in, k_in, v_in, o_in)[i]())
+            gain_ref = gain_in()
+        n_out, q_out, k_out, v_out, c_out, t_out, mid_out, nn_out = outward[:8]
+        n_out.ref[...] = normed(dec_in()[...].astype(F32), gain_ref[0:1, :]).astype(BF16)
+        n_out.send()
+        for out, i in ((q_out, 0), (k_out, 1), (v_out, 2)):
+            out.ref[...] = mul(n_out.ref[...], weights(i)).astype(BF16)
+            out.send()
+        column_ref, row_ref = column_in(), row_in()
+        if not first:
+            bias_ref = bias_in()
+        near_of = lambda: mask_twice(column_ref, row_ref, index, True)
+        attend_pairs(near_of, q_out.ref, k_out.ref, v_out.ref, c_out.ref, t_out.ref, bias_ref)
+        c_out.send()
+        t_out.send()
+        mid_out.ref[...] = dec_in()[...].astype(F32) + mul(c_out.ref[...], weights(3))
+        mid_out.send()
+        nn_out.ref[...] = normed(mid_out.ref[...], gain_ref[1:2, :]).astype(BF16)
+        if first:
+            for i in range(PARTS):
+                pltpu.make_async_copy(m_ref.at[i], raw_outs[i], m_done.at[i]).wait()
+
+    big = shape_of(length, features)
+    outs = [big, big, big, big, big, shape_of(length, 128, kind=F32), shape_of(length, features, kind=F32), big]
+    dec_row, column_row = (dec, index * length, length), (column, index * length, length)
+    cost = dict(micros=11 if first else 8)
+    if not first:
+        q, k, v, o, gains, bias = given
+        return call(kernel, outs, (dec_row, gains, q, k, v, column_row, segments, bias, o), **cost)
+    block = shape_of(8, features // 8, features)
+    more = [shape_of(EXTRA, features, kind=F32), shape_of(BUCKETS, 128, kind=F32), shape_of(HEADS, length, length, kind=F32)]
+    return call(
+        kernel,
+        outs + more,
+        (dec_row, column_row, segments),
+        given,
+        [block] * PARTS,
+        [
+            pltpu.VMEM((PARTS,) + block.shape, BF16),
+            pltpu.VMEM((8, EXTRA, features), BF16),
+            pltpu.SemaphoreType.DMA((PARTS,)),
+            pltpu.SemaphoreType.DMA(()),
+            pltpu.SemaphoreType.DMA((PARTS,)),
+        ],
+        position=position,
+        **cost,
+    )
+
+
+def cross_forward(index, position, middle, normed_cross, enc, column, segments, gains, given):
+    rows, keys_length = segments.shape
+    length, features = middle.shape
+    first = index == 0
+
+    def kernel(inward, outward, raw, raw_outs, scratch):
+        if first:
+            position_ref, sources = raw[0], raw[1:]
+            m_ref, done, m_done = scratch
+            start_pieces(position_ref, sources, m_ref, lambda i: done.at[i], False)
+            enc_in, n_in, column_in, row_in, mid_in, gain_in = inward
+
+            def weights(i):
+                wait_block(m_ref, i, done.at[i])
+                pltpu.make_async_copy(m_ref.at[i], raw_outs[i], m_done.at[i]).start()
+                return matrix(m_ref, i)
+        else:
+            n_in, q_in, enc_in, k_in, v_in, column_in, row_in, o_in, mid_in, gain_in = inward
+            weights = lambda i: flat((q_in, k_in, v_in, o_in)[i]())
+        q_out, k_out, v_out, c_out, t_out, late_out, nn_out = outward
+        for out, taken, i in ((q_out, n_in, 0), (k_out, enc_in, 1), (v_out, enc_in, 2)):
+            out.ref[...] = mul(taken()[...], weights(i)).astype(BF16)
+            out.send()
+        column_ref, row_ref = column_in(), row_in()
+        near_of = lambda: mask_twice(column_ref, row_ref, index, False)
+        attend_pairs(near_of, q_out.ref, k_out.ref, v_out.ref, c_out.ref, t_out.ref, None)
+        c_out.send()
+        t_out.send()
+        late_out.ref[...] = mid_in()[...] + mul(c_out.ref[...], weights(3))
+        late_out.send()
+        nn_out.ref[...] = normed(late_out.ref[...], gain_in()[2:3, :]).astype(BF16)
+        if first:
+            for i in range(PARTS):
+                pltpu.make_async_copy(m_ref.at[i], raw_outs[i], m_done.at[i]).wait()
+
+    big, keys = shape_of(length, features), shape_of(keys_length, features)
+    outs = [big, keys, keys, big, shape_of(length, 128, kind=F32), shape_of(length, features, kind=F32), big]
+    enc_row, column_row = (enc, index * keys_length, keys_length), (column, index * length, length)
+    cost = dict(micros=13 if first else 10)
+    if not first:
+        q, k, v, o = given
+        return call(kernel, outs, (normed_cross, q, enc_row, k, v, column_row, segments, o, middle, gains), **cost)
+    block = shape_of(8, features // 8, features)
+    return call(
+        kernel,
+        outs,
+        (enc_row, normed_cross, column_row, segments, middle, gains),
+        given,
+        [block] * PARTS,
+        [pltpu.VMEM((PARTS,) + block.shape, BF16), pltpu.SemaphoreType.DMA((PARTS,)), pltpu.SemaphoreType.DMA((PARTS,))],
+        position=position,
+        **cost,
+    )
+
+
+def feed_forward(position, late, normed_ffn, cotangent, gains, inner, down):
+    rows = len(late)
+    length, features = late[0].shape
+    tokens = rows * length
+    wide = inner[0].shape[3] // 2
+    each = wide // 2
+    blocks = 8
+    high, low = features // 8, each // PARTS
+    inner_shape = (PARTS, 8, high, 2 * wide)
+    down_shape = (8, PARTS, low, features)
+    inner_rows = high * (2 * wide // 128)
+    all_rows = inner_rows + low * (features // 128)
+
+    def kernel(position_ref, cot_ref, gain_ref, *refs):
+        late_refs, norm_refs, refs = refs[:rows], refs[rows : 2 * rows], refs[2 * rows :]
+        inner_sources, down_sources = refs[:8], refs[8:16]
+        out_ref, lg_ref, lgb_ref, gg_ref, keep_ref, send_ref = refs[16:22]
+        n_ref, flat_ref, sum_ref, back_ref, inner_ref, down_ref, grads_ref, inner_done, down_done, out_done = refs[22:]
+        step = pl.program_id(0)
+        core = position_ref[0] & 1
+
+        @pl.when(step == 0)
+        def _():
+            start_pieces(position_ref, inner_sources, inner_ref, lambda i: inner_done.at[i], False)
+            start_pieces(position_ref, down_sources, down_ref, lambda i: down_done.at[i], True)
+            for row in range(rows):
+                n_ref[row * length : (row + 1) * length, :] = norm_refs[row][...]
+            flat_ref[...] = n_ref[...].T
+            sum_ref[...] = jnp.zeros_like(sum_ref)
+            back_ref[...] = jnp.zeros_like(back_ref)
+
+        @pl.when(step % 2 == 0)
+        def _():
+            wait_block(inner_ref, step // 2, inner_done.at[step // 2])
+
+        wait_block(down_ref, step, down_done.at[step])
+        inner_block = inner_ref[step // 2, :, :, pl.ds(pl.multiple_of((step % 2) * wide, wide), wide)].reshape(features, wide)
+        down_block = down_ref[step].reshape(each, features)
+        both = mul(n_ref[...], inner_block)
+        hidden_grad = mul_right_t(cot_ref[...], down_block)
+        gate, up = both[:, :each], both[:, each:]
+        inside = math.sqrt(2 / math.pi) * (gate + 0.044715 * (gate * gate * gate))
+        bent = jnp.tanh(inside)
+        half = 0.5 * (1.0 + bent)
+        swish = gate * half
+        hidden = (swish * up).astype(BF16)
+        slope = half + 0.5 * gate * (1.0 - bent * bent) * (
+            math.sqrt(2 / math.pi) * (1.0 + 3 * 0.044715 * (gate * gate))
+        )
+        grads = jnp.concatenate([hidden_grad * up * slope, hidden_grad * swish], 1).astype(BF16)
+        sum_ref[...] += mul(hidden, down_block)
+        back_ref[...] += mul_right_t(grads, inner_block)
+        inner_grads = mul(flat_ref[...], grads).astype(BF16)
+        part = step // 2
+        slot, row = (part & 1) ^ core, part >> 1
+        for shard in range(8):
+            for column in range(wide // 128):
+                start = pl.multiple_of(((step % 2) * (wide // 128) + column) * high, 16)
+                grads_ref[slot, row, shard, pl.ds(start, high), :] = inner_grads[
+                    shard * high : (shard + 1) * high, column * 128 : (column + 1) * 128
+                ]
+        down_grads = mul_left_t(hidden, cot_ref[...]).astype(BF16)
+        for part in range(PARTS):
+            for column in range(features // 128):
+                start = inner_rows + column * low
+                grads_ref[(part & 1) ^ core, part >> 1, step, start : start + low, :] = down_grads[
+                    part * low : (part + 1) * low, column * 128 : (column + 1) * 128
+                ]
+
+        @pl.when(step == blocks - 1)
+        def _():
+            pltpu.make_async_copy(grads_ref.at[1], send_ref, out_done.at[1]).start()
+            pltpu.make_async_copy(grads_ref.at[0], keep_ref, out_done.at[0]).start()
+            values = jnp.concatenate([r[...] for r in late_refs], 0)
+            out_ref[...] = (values + sum_ref[...]).astype(BF16)
+            back, gain_grad = norm_back(values, gain_ref[2:3, :], back_ref[...])
+            grad = cot_ref[...].astype(F32) + back
+            lg_ref[...] = grad
+            lgb_ref[...] = grad.astype(BF16)
+            gg_ref[...] = gain_grad
+            pltpu.make_async_copy(grads_ref.at[1], send_ref, out_done.at[1]).wait()
+            pltpu.make_async_copy(grads_ref.at[0], keep_ref, out_done.at[0]).wait()
+
+    whole = lambda a: pl.BlockSpec(a.shape, lambda i: (0,) * len(a.shape))
+    big = shape_of(tokens, features)
+    half = shape_of(2, 8, all_rows, 128)
+    outs = [big, shape_of(tokens, features, kind=F32), big, shape_of(1, features, kind=F32), half, half]
+    return pl.pallas_call(
+        kernel,
+        grid=(blocks,),
+        out_shape=outs,
+        in_specs=[SCALARS, whole(cotangent), whole(gains)] + [whole(a) for a in (*late, *normed_ffn)] + [ANYWHERE] * 16,
+        out_specs=[whole(o) for o in outs[:4]] + [ANYWHERE] * 2,
+        scratch_shapes=[
+            pltpu.VMEM((tokens, features), BF16),
+            pltpu.VMEM((features, tokens), BF16),
+            pltpu.VMEM((tokens, features), F32),
+            pltpu.VMEM((tokens, features), F32),
+            pltpu.VMEM(inner_shape, BF16),
+            pltpu.VMEM(down_shape, BF16),
+            pltpu.VMEM((2, 2, 8, all_rows, 128), BF16),
+            pltpu.SemaphoreType.DMA((PARTS,)),
+            pltpu.SemaphoreType.DMA((8,)),
+            pltpu.SemaphoreType.DMA((2,)),
+        ],
+        compiler_params=pltpu.CompilerParams(vmem_limit_bytes=VMEM_LIMIT),
+        cost_estimate=cost_of(31),
+    )(position, cotangent, gains, *late, *normed_ffn, *inner, *down)
+
+
+def cross_backward(index, late_grad, late_gradb, middle, q, k, v, totals, column, segments, gains, query, output):
+    rows, keys_length = segments.shape
+    length, features = middle.shape
+
+    def kernel(inward, outward, raw, raw_outs, scratch):
+        lgb_in, o_in, k_in, q_in, v_in, t_in, column_in, row_in, m_in, mid_in, gain_in, lg_in = inward
+        dq_out, dk_out, dv_out, mg_out, mgb_out, gg_out = outward
+        (g_ref,) = scratch
+        g_ref[...] = mul_right_t(lgb_in()[...], flat(o_in())).astype(BF16)
+        column_ref, row_ref = column_in(), row_in()
+        near_of = lambda: mask_twice(column_ref, row_ref, index, False)
+        attend_pairs_back(near_of, q_in(), k_in(), v_in(), t_in(), g_ref, dq_out.ref, dk_out.ref, dv_out.ref, None, None)
+        for out in (dq_out, dk_out, dv_out):
+            out.send()
+        part, gain_grad = norm_back(mid_in()[...], gain_in()[1:2, :], mul_right_t(dq_out.ref[...], flat(m_in())))
+        gg_out.ref[...] = gain_grad
+        grad = lg_in()[...] + part
+        mg_out.ref[...] = grad
+        mgb_out.ref[...] = grad.astype(BF16)
+
+    big, keys = shape_of(length, features), shape_of(keys_length, features)
+    row_of = lambda a: (a, index * length, length)
+    return call(
+        kernel,
+        [big, keys, keys, shape_of(length, features, kind=F32), big, shape_of(1, features, kind=F32)],
+        (row_of(late_gradb), output, k, q, v, totals, row_of(column), segments, query, middle, gains, row_of(late_grad)),
+        scratch=[pltpu.VMEM((length, features), BF16)],
+        micros=10,
+    )
+
+
+def self_backward(index, middle_grad, middle_gradb, dec, q, k, v, totals, column, segments, gains, bias, weights):
+    rows = segments.shape[0]
+    length, features = middle_grad.shape
+
+    def kernel(inward, outward, raw, raw_outs, scratch):
+        mgb_in, o_in, q_in, k_in, v_in, t_in, column_in, row_in, bias_in, wq_in, wk_in, wv_in, dec_in, gain_in, mg_in = inward
+        dq_out, dk_out, dv_out, ig_out, gg_out, tg_out = outward
+        g_ref, sum_ref = scratch
+        g_ref[...] = mul_right_t(mgb_in()[...], flat(o_in())).astype(BF16)
+        column_ref, row_ref = column_in(), row_in()
+        near_of = lambda: mask_twice(column_ref, row_ref, index, True)
+        attend_pairs_back(near_of, q_in(), k_in(), v_in(), t_in(), g_ref, dq_out.ref, dk_out.ref, dv_out.ref, bias_in(), sum_ref)
+        for out in (dq_out, dk_out, dv_out):
+            out.send()
+        back = mul_right_t(dq_out.ref[...], flat(wq_in())) + mul_right_t(dk_out.ref[...], flat(wk_in())) + mul_right_t(dv_out.ref[...], flat(wv_in()))
+        part, gain_grad = norm_back(dec_in()[...].astype(F32), gain_in()[0:1, :], back)
+        ig_out.ref[...] = (mg_in()[...] + part).astype(BF16)
+        ig_out.send()
+        gg_out.ref[...] = gain_grad
+        sums = []
+        i = lax.broadcasted_iota(jnp.int32, (length, length), 0)
+        j = lax.broadcasted_iota(jnp.int32, (length, length), 1)
+        flip = (i + j == length - 1).astype(BF16)
+        for head in range(HEADS):
+            flipped = mul(flip, sum_ref[head])
+            square = jnp.concatenate([flipped, jnp.zeros((length, SPAN - length), F32)], 1)
+            turned = pltpu.roll(square, SPAN - length + 1, 1, stride=1, stride_axis=0)
+            sums.append(jnp.sum(turned, axis=0, keepdims=True))
+        sums.append(jnp.zeros((128 - HEADS, SPAN), F32))
+        tg_out.ref[...] = exact(distance_levels(True), jnp.concatenate(sums, 0), ((1,), (1,)))
+
+    big = shape_of(length, features)
+    row_of = lambda a: (a, index * length, length)
+    return call(
+        kernel,
+        [big, big, big, big, shape_of(1, features, kind=F32), shape_of(BUCKETS, 128, kind=F32)],
+        (middle_gradb, weights[3], q, k, v, totals, row_of(column), segments, bias, *weights[:3], row_of(dec), gains, middle_grad),
+        scratch=[pltpu.VMEM((length, features), BF16), pltpu.VMEM((HEADS, length, length), BF16)],
+        micros=11,
+    )
+
+
+def weight_grads(position, lefts, rights, extra=None):
+    features = rights[0][0].shape[1] if not isinstance(rights[0][0], tuple) else rights[0][0][0].shape[1]
+    high = features // 8
+    all_rows = high + (EXTRA if extra else 0)
+    known, operands = {}, []
+
+    def place_of(a):
+        key = (id(a[0]), a[1]) if isinstance(a, tuple) else (id(a), -1)
+        if key not in known:
+            known[key] = len(operands)
+            operands.append(a)
+        return known[key]
+
+    places = [([place_of(a) for a in left], [place_of(b) for b in right]) for left, right in zip(lefts, rights)]
+    more = [[place_of(a) for a in group] for group in extra] if extra else []
+
+    def kernel(inward, outward, raw, raw_outs, scratch):
+        (position_ref,) = raw
+        keep_ref, send_ref = raw_outs
+        grads_ref, done = scratch
+        core = position_ref[0] & 1
+        copies = [
+            pltpu.make_async_copy(grads_ref.at[slot, row], (keep_ref, send_ref)[slot].at[row], done.at[2 * slot + row])
+            for slot in range(2)
+            for row in range(2)
+        ]
+        if extra:
+            groups = []
+            for group in more:
+                total = inward[group[0]]()[...]
+                for i in group[1:]:
+                    total = total + inward[i]()[...]
+                groups.append(total)
+            line = lax.broadcasted_iota(jnp.int32, (EXTRA, features), 0)
+            base = jnp.zeros((EXTRA, features), F32)
+            for i in range(3):
+                base = jnp.where(line == i, groups[i], base)
+            row = lax.broadcasted_iota(jnp.int32, (EXTRA, BUCKETS), 0)
+            level = lax.broadcasted_iota(jnp.int32, (EXTRA, BUCKETS), 1)
+            for shard in range(8):
+                chosen = ((row >= 4) & (level == row - 4 + 4 * shard)).astype(F32)
+                table = exact(chosen, groups[3], ((1,), (0,)))
+                block = base + jnp.concatenate([table, jnp.zeros((EXTRA, features - 128), F32)], 1)
+                for slot in range(2):
+                    for part in range(2):
+                        grads_ref[slot, part, shard, high:, :] = block.astype(BF16)
+        for m, (left, right) in enumerate(places):
+            total = mul_left_t(inward[left[0]]()[...], inward[right[0]]()[...])
+            for i, j in zip(left[1:], right[1:]):
+                total = total + mul_left_t(inward[i]()[...], inward[j]()[...])
+            total = total.astype(BF16)
+            for shard in range(8):
+                grads_ref[(m & 1) ^ core, m >> 1, shard, :high, :] = total[shard * high : (shard + 1) * high]
+            if m == 1:
+                copies[0].start()
+                copies[2].start()
+        copies[3].start()
+        copies[1].start()
+        for copy in copies:
+            copy.wait()
+
+    half = shape_of(2, 8, all_rows, features)
+    return call(
+        kernel,
+        [],
+        operands,
+        raw_outs=[half, half],
+        scratch=[pltpu.VMEM((2, 2, 8, all_rows, features), BF16), pltpu.SemaphoreType.DMA((4,))],
+        micros=13,
+        position=position,
+    )
+
+
+def key_value_back(dk, dv, key, value):
+    rows = len(dk)
+    length, features = dk[0].shape
+
+    def kernel(inward, outward, raw, raw_outs, scratch):
+        result_ref, done = scratch
+        copies = [pltpu.make_async_copy(result_ref.at[r], raw_outs[0].at[r], done.at[r]) for r in range(rows)]
+        for row in range(rows):
+            k_in, v_in = (inward[0], inward[2]) if row == 0 else (inward[2 + 2 * row], inward[3 + 2 * row])
+            result_ref[row] = (
+                mul_right_t(k_in()[...], flat(inward[1]())) + mul_right_t(v_in()[...], flat(inward[3]()))
+            ).astype(BF16)
+            copies[row].start()
+        for copy in copies:
+            copy.wait()
+
+    operands = [dk[0], key, dv[0], value]
+    for row in range(1, rows):
+        operands += [dk[row], dv[row]]
+    whole = shape_of(rows, length, features)
+    return call(
+        kernel,
+        [],
+        operands,
+        raw_outs=[whole],
+        scratch=[pltpu.VMEM(whole.shape, BF16), pltpu.SemaphoreType.DMA((rows,))],
+        micros=8,
+    )[0]
+
+
+def fast_shards(
+    dec_input,
+    enc_output,
+    dec_segments,
+    enc_segments,
+    cotangent,
+    norm_self,
+    q_self,
+    k_self,
+    v_self,
+    o_self,
+    rel_table,
+    norm_cross,
+    q_cross,
+    k_cross,
+    v_cross,
+    o_cross,
+    norm_ffn,
+    wi_gate,
+    wi_up,
+    wo_ffn,
+):
+    rows = dec_input.shape[0]
+    gain_rows = norm_self.shape[0]
+    table_rows = rel_table.shape[0]
+    features = dec_input.shape[2]
+    blocks = 2
+    each = wi_gate.shape[1] // (blocks * PARTS)
+    part, shard = lax.axis_index("rep"), lax.axis_index("fsdp")
+    position = jnp.stack([part, shard]).astype(jnp.int32)
+    choose = lambda *values: lax.select_n(part, *values)
+
+    extra = jnp.zeros((EXTRA, features), BF16)
+    gains_here = jnp.stack([norm_self, norm_cross, norm_ffn])
+    extra = lax.dynamic_update_slice(extra, gains_here, (0, shard * gain_rows))
+    extra = lax.dynamic_update_slice(extra, rel_table, (4, 0))
+    self_part = jnp.concatenate([choose(q_self, k_self, v_self, o_self), extra], 0)
+    cross_part = choose(q_cross, k_cross, v_cross, o_cross)
+    gate_part = lax.dynamic_slice_in_dim(wi_gate, part * (blocks * each), blocks * each, 1)
+    up_part = lax.dynamic_slice_in_dim(wi_up, part * (blocks * each), blocks * each, 1)
+    inner_part = jnp.concatenate(
+        [gate_part[:, :each], up_part[:, :each], gate_part[:, each:], up_part[:, each:]], 1
+    )
+    down_rows = wo_ffn.shape[0] // PARTS
+    down_part = lax.dynamic_slice_in_dim(wo_ffn, part * down_rows, down_rows, 0)
+
+    s0 = gather_far(self_part)
+    c0 = gather_far(after(cross_part, s0))
+    s1 = gather_near(s0)
+    i0 = gather_far(after(inner_part, c0, s1))
+    c1 = gather_near(after(c0, s1))
+    s2 = gather_one(s1)
+    s3 = gather_two(s2)
+    c1 = after(c1, *s2)
+    d0 = gather_far(after(down_part, i0, *s2))
+    i1 = gather_near(after(i0, *s2))
+    s4 = gather_core(s2)
+    c2 = gather_one(after(c1, *s3))
+    s5 = gather_core(s3)
+    self_pieces = in_order(s2, s3, s4, s5)
+
+    dec = dec_input.reshape(-1, features)
+    enc = enc_output.reshape(-1, features)
+    cot = cotangent.reshape(-1, features)
+    column = dec_segments.reshape(-1, 1)
+
+    made = self_forward(0, position, after(dec, c1), column, dec_segments, self_pieces)
+    selfs = [made[:8]]
+    gains, table, bias, *self_matrices = made[8:]
+    given = (*self_matrices, gains, bias)
+    c2 = tuple(after(c, made[0]) for c in c2)
+    c3 = gather_two(c2)
+    i1 = after(i1, made[0])
+    d1 = gather_near(after(d0, made[0]))
+    c4 = gather_core(c2)
+    i2 = gather_one(i1)
+    selfs.append(self_forward(1, position, after(dec, *c2, i1), column, dec_segments, given))
+    d1 = after(d1, selfs[1][0])
+    selfs.append(self_forward(2, position, after(dec, selfs[1][0]), column, dec_segments, given))
+    c3 = tuple(after(c, selfs[2][0]) for c in c3)
+    i2 = tuple(after(i, selfs[2][0]) for i in i2)
+    c5 = gather_core(c3)
+    i3 = gather_two(i2)
+    given = in_order(c2, c3, c4, c5)
+    crosses = []
+    cross = lambda row, n, *given: cross_forward(row, position, selfs[row][6], n, enc, column, enc_segments, gains, given)
+    made = cross(0, after(selfs[0][7], *i2, d1), *given)
+    cross_matrices = made[7:]
+    crosses = [made[:7]]
+    d1 = after(d1, made[0])
+    d2 = gather_one(d1)
+    i4 = gather_core(i2)
+    crosses.append(cross(1, after(selfs[1][7], d1), *cross_matrices))
+    d2 = tuple(after(d, crosses[1][0]) for d in d2)
+    d3 = gather_two(d2)
+    i3 = tuple(after(i, crosses[1][0]) for i in i3)
+    i5 = gather_core(i3)
+    d4 = gather_core(d2)
+    crosses.append(cross(2, after(selfs[2][7], *i3, *d2), *cross_matrices))
+    d3 = tuple(after(d, crosses[2][0]) for d in d3)
+    d5 = gather_core(d3)
+    out, late_grad, late_gradb, grad_gain_ffn, keep, send = feed_forward(
+        position,
+        [c[5] for c in crosses],
+        [c[6] for c in crosses],
+        cot,
+        gains,
+        in_order(i2, i3, i4, i5),
+        in_order(d2, d3, d4, d5),
+    )
+
+    ffn_sums = Scatter(position, keep, send)
+
+    def cross_back(row, *gates):
+        q, k, v, context, totals, late, n_ffn = crosses[row]
+        return cross_backward(
+            row, after(late_grad, *gates), late_gradb, selfs[row][6], q, k, v, totals, column, enc_segments, gains, cross_matrices[0], cross_matrices[3]
+        )
+
+    def self_back(row, made, *gates):
+        n, q, k, v, context, totals, middle, n_cross = selfs[row]
+        return self_backward(
+            row, after(made[3], *gates), made[4], dec, q, k, v, totals, column, dec_segments, gains, bias, self_matrices
+        )
+
+    length = dec_input.shape[1]
+    enc_rows = [(enc, i * enc_output.shape[1], enc_output.shape[1]) for i in range(rows)]
+    column_of = lambda group, i: [g[i] for g in group]
+    cb = [cross_back(0)]
+    ready = ffn_sums.ready_one(cb[0][3])
+    ffn_sums.move_one()
+    cb.append(cross_back(1, *ready))
+    cb.append(cross_back(2, cb[1][3]))
+    ready = ffn_sums.ready_two(cb[2][3])
+    ffn_sums.move_two()
+    cross_keep, cross_send = weight_grads(
+        position,
+        [[after(selfs[0][7], *ready)] + column_of(selfs[1:], 7), enc_rows, enc_rows, column_of(crosses, 3)],
+        [column_of(cb, 0), column_of(cb, 1), column_of(cb, 2), [(late_gradb, i * length, length) for i in range(rows)]],
+    )
+    cross_sums = Scatter(position, cross_keep, cross_send)
+    ready = ffn_sums.ready_three(cross_keep)
+    ffn_sums.move_three()
+    sb = [self_back(0, cb[0], *ready)]
+    ready = ffn_sums.ready_four(sb[0][3]) + cross_sums.ready_one(sb[0][3])
+    ffn_sums.move_four()
+    cross_sums.move_one()
+    sb.append(self_back(1, cb[1], *ready))
+    ffn_total = ffn_sums.total(sb[1][3])
+    ffn_sums.move_row()
+    ready = cross_sums.ready_two(sb[1][3])
+    cross_sums.move_two()
+    sb.append(self_back(2, cb[2], ffn_total, *ready))
+    ready = cross_sums.ready_three(sb[2][3])
+    cross_sums.move_three()
+    norms = column_of(selfs, 0)
+    self_keep, self_send = weight_grads(
+        position,
+        [norms, norms, norms, column_of(selfs, 4)],
+        [column_of(sb, 0), column_of(sb, 1), column_of(sb, 2), column_of(cb, 4)],
+        [column_of(sb, 4), column_of(cb, 5), [after(grad_gain_ffn, *ready)], column_of(sb, 5)],
+    )
+    self_sums = Scatter(position, self_keep, self_send)
+    ready = self_sums.ready_one()
+    self_sums.move_one()
+    enc_grad = key_value_back(column_of(cb, 1), column_of(cb, 2), after(cross_matrices[1], *ready), cross_matrices[2])
+    self_sums.ready_two(enc_grad)
+    self_sums.move_two()
+    cross_sums.ready_four(self_keep)
+    cross_sums.move_four()
+    self_sums.ready_three()
+    self_sums.move_three()
+    cross_sums.total(*self_sums.sent_now())
+    cross_sums.move_row()
+    self_sums.ready_four()
+    self_sums.move_four()
+    ffn_sum = ffn_sums.finish(self_keep)
+    cross_sum = cross_sums.finish().astype(F32)
+    self_sums.total()
+    self_sums.move_row()
+    self_sum = self_sums.finish().astype(F32)
+    inner_rows = features // 8
+    pieces = lambda first: jnp.concatenate(
+        [
+            ffn_sum[p, (4 * b + 2 * first + i) * inner_rows : (4 * b + 2 * first + i + 1) * inner_rows]
+            for p in range(PARTS)
+            for b in range(blocks)
+            for i in range(each // 128)
+        ],
+        1,
+    ).astype(F32)
+    start = inner_rows * (4 * each // 128)
+    down_sum = jnp.concatenate(
+        [
+            ffn_sum[:, start + i * down_rows : start + (i + 1) * down_rows]
+            for i in range(features // 128)
+        ],
+        2,
+    ).astype(F32)
+    small = self_sum[0, inner_rows:]
+    small_gains = lax.dynamic_slice(small, (0, shard * gain_rows), (3, gain_rows))
+    return (
+        out.reshape(dec_input.shape),
+        jnp.stack(column_of(sb, 3)),
+        enc_grad,
+        small_gains[0],
+        self_sum[0, :inner_rows],
+        self_sum[1, :inner_rows],
+        self_sum[2, :inner_rows],
+        self_sum[3, :inner_rows],
+        small[4 : 4 + table_rows, :HEADS],
+        small_gains[1],
+        cross_sum[0],
+        cross_sum[1],
+        cross_sum[2],
+        cross_sum[3],
+        small_gains[2],
+        pieces(0),
+        pieces(1),
+        down_sum.reshape(wo_ffn.shape),
+    )
+
+
 def solution(mesh):
     placed = (
         P(("rep", "fsdp"), None, None),
@@ -403,8 +1451,9 @@
         P("fsdp", None),
         P("fsdp", None),
     )
+    fast = mesh.shape["rep"] == 4 and mesh.shape["fsdp"] == 8
     return jax.shard_map(
-        shards,
+        fast_shards if fast else shards,
         mesh=mesh,
         in_specs=placed,
         out_specs=(

time: 1430 us -> 403 us (0.28)
  waiting for transfers between devices: 1040 us -> 101 us
  Pallas kernels: 0 us -> 190 us
  matrix products: 185 us -> 0 us
  blocking collectives: 80.8 us -> 0 us
  starting transfers between devices: 1.71 us -> 65.2 us
  local copies, waits for them, and re-layouts: 56.1 us -> 15.7 us
  other arithmetic: 42.5 us -> 20.8 us
  between operations: 17.4 us -> 2.41 us
    reduce_scatter x9 -> x0, waiting for transfers between devices: 602 us -> none  [the longest x1 77.2 us: shards(): lax.psum_scatter(grad_up.astype(jnp.bfloat16), 'fsdp', scatter_dimension=...]
    all_gather x11 -> x0, waiting for transfers between devices: 383 us -> none  [the longest x1 56 us: shards(): lax.all_gather(wo_ffn, 'fsdp', axis=0, tiled=True)]
    pallas_call x0 -> x16, Pallas kernels: none -> 190 us  [the longest x15 159 us: call(): pl.pallas_call(body, out_shape=list(outs) + list(raw_outs), in_specs=[SCA...]
    dot_general x47 -> x0, matrix products: 185 us -> none  [the longest x11 49.4 us: project(): jnp.einsum('rld,de->rle', values, matrix, preferred_element_type=jnp.floa...]
    ppermute x0 -> x67, waiting for transfers between devices: none -> 101 us  [the longest x14 37.6 us: over_across(): return lax.ppermute(values, 'fsdp', ACROSS)]
    ppermute x0 -> x67, starting transfers between devices: none -> 65.2 us  [the longest x17 21.4 us: over_row(): return lax.ppermute(values, 'rep', ROW)]
    unnamed x2 -> x0, blocking collectives: 58.3 us -> none
    psum x1 -> x0, waiting for transfers between devices: 45.9 us -> none  [shards(): lax.psum(cross_sums[2].astype(jnp.bfloat16), 'rep').astype(jnp.float32)]
  transfers between devices with their start and end apart: 23 -> 67, of which waited for: 20 -> 29; matrix products, arithmetic and copies ran while one was open for 15% -> 5% of each run, Pallas kernels for 0% -> 37%
where the time goes in v3:
time: 403 us; the launch traced here: 396 us
  Pallas kernels  190 us (47%)
  waiting for transfers between devices  101 us (25%)
  starting transfers between devices  65.2 us (16%)
  other arithmetic  20.8 us (5%)
  local copies, waits for them, and re-layouts  15.7 us (4%)
    pallas_call x15, Pallas kernels, call(): pl.pallas_call(body, out_shape=list(outs) + list(raw_outs), in_specs=[SCA...  159 us
    ppermute x14, waiting for transfers between devices, over_across(): return lax.ppermute(values, 'fsdp', ACROSS)  37.6 us
    pallas_call x1, Pallas kernels, feed_forward(): pl.pallas_call(kernel, grid=(blocks,), out_shape=outs, in_specs=[SCALARS,...  31.3 us
    ppermute x17, starting transfers between devices, over_row(): return lax.ppermute(values, 'rep', ROW)  21.4 us
    ppermute x7, waiting for transfers between devices, over_far(): return lax.ppermute(values, 'fsdp', FAR)  21 us
    ppermute x7, waiting for transfers between devices, over_near(): return lax.ppermute(values, 'fsdp', NEAR)  20.5 us
    ppermute x17, waiting for transfers between devices, over_row(): return lax.ppermute(values, 'rep', ROW)  16.7 us
    ppermute x7, starting transfers between devices, over_far(): return lax.ppermute(values, 'fsdp', FAR)  16.3 us
  transfers between devices with their start and end apart: 67, of which 29 were waited for; matrix products, arithmetic and copies ran while one was open for 5% of the time, Pallas kernels for 37%

profile of v3, /device:TPU:0, one launch (start us, length us, event | category | flops | bytes accessed | tf_op | source)
XLA Modules:
  0.0 395.9 jit_solution(11804272970259909879)
XLA Ops:
  4.3 4.1 %collective-permute-start = (bf16[1,104,768]{2,1,0:T(8,128)(2,1)S(1)}, bf16[1,104,768]{2,1,0:T(8,128)(2,1)S(1)}, u32[]{:S(2)}, u32[]{:S(2)}) collective-permute-start(bf16[1,104,768]{2,1,0:T(8,128)(2,1)S(1)} %maximum_bitcast_fusion), channel_id=1, source_target_pairs={{0,4},{1,5},{2,6},{3,7},{4,0},{5,1},{6,2},{7,3},{8,12},{9,13},{10,... | collective-permute-start | bytes 479240 | tf_op jit(solution)/shard_map/ppermute | solution.py:413
  8.4 7.5 %collective-permute-done = bf16[1,104,768]{2,1,0:T(8,128)(2,1)S(1)} collective-permute-done((bf16[1,104,768]{2,1,0:T(8,128)(2,1)S(1)}, bf16[1,104,768]{2,1,0:T(8,128)(2,1)S(1)}, u32[]{:S(2)}, u32[]{:S(2)}) %collective-permute-start) | collective-permute-done | bytes 159776 | tf_op jit(solution)/shard_map/ppermute | solution.py:413
  16.8 8.0 %collective-permute-done.2 = bf16[2,104,768]{2,1,0:T(8,128)(2,1)S(1)} collective-permute-done((bf16[2,104,768]{2,1,0:T(8,128)(2,1)S(1)}, bf16[2,104,768]{2,1,0:T(8,128)(2,1)S(1)}, u32[]{:S(2)}, u32[]{:S(2)}) %collective-permute-start.2) | collective-permute-done | bytes 319520 | tf_op jit(solution)/shard_map/ppermute | solution.py:409
  29.0 3.4 collective-permute-start.1
  38.5 3.5 collective-permute-start.12
  43.4 6.3 %collective-permute-done.12 = bf16[1,96,1024]{2,1,0:T(8,128)(2,1)S(1)} collective-permute-done((bf16[1,96,1024]{2,1,0:T(8,128)(2,1)S(1)}, bf16[1,96,1024]{2,1,0:T(8,128)(2,1)S(1)}, u32[]{:S(2)}, u32[]{:S(2)}) %collective-permute-start.12) | collective-permute-done | bytes 196640 | tf_op jit(solution)/shard_map/ppermute | solution.py:413
  57.7 3.5 collective-permute-done.18
  63.6 8.9 %collective-permute-done.15 = bf16[4,48,768]{2,1,0:T(8,128)(2,1)S(1)} collective-permute-done((bf16[4,48,768]{2,1,0:T(8,128)(2,1)S(1)}, bf16[4,48,768]{2,1,0:T(8,128)(2,1)S(1)}, u32[]{:S(2)}, u32[]{:S(2)}) %collective-permute-start.15) | collective-permute-done | bytes 294944 | tf_op jit(solution)/shard_map/ppermute | solution.py:405
  73.6 10.9 %shard_map.331 = (bf16[176,768]{1,0:T(8,128)(2,1)}, bf16[176,768]{1,0:T(8,128)(2,1)}, bf16[176,768]{1,0:T(8,128)(2,1)}, bf16[176,768]{1,0:T(8,128)(2,1)}, bf16[1...) custom-call(s32[2]{0:T(128)} %pad_add_fusion.refs_0_.position_ref, ...), custom_call_target="tpu_custom_call" | custom-call | flops 12650000384 | tf_op jit(solution)/shard_map/pallas_call | solution.py:622
  87.4 8.2 %shard_map.332 = (bf16[176,768]{1,0:T(8,128)(2,1)}, bf16[176,768]{1,0:T(8,128)(2,1)}, bf16[176,768]{1,0:T(8,128)(2,1)}, bf16[176,768]{1,0:T(8,128)(2,1)}, bf16[1...) custom-call(bf16[528,768]{1,0:T(8,128)(2,1)} %bitcast.410, ...), custom_call_target="tpu_custom_call" | custom-call | flops 9200000000 | tf_op jit(solution)/shard_map/pallas_call | solution.py:622
  98.8 8.3 %shard_map.333 = (bf16[176,768]{1,0:T(8,128)(2,1)}, bf16[176,768]{1,0:T(8,128)(2,1)}, bf16[176,768]{1,0:T(8,128)(2,1)}, bf16[176,768]{1,0:T(8,128)(2,1)}, bf16[1...) custom-call(bf16[528,768]{1,0:T(8,128)(2,1)} %bitcast.411, ...), custom_call_target="tpu_custom_call" | custom-call | flops 9200000000 | tf_op jit(solution)/shard_map/pallas_call | solution.py:622
  110.5 10.0 %collective-permute-done.14 = bf16[4,48,1024]{2,1,0:T(8,128)(2,1)S(1)} collective-permute-done((bf16[4,48,1024]{2,1,0:T(8,128)(2,1)S(1)}, bf16[4,48,1024]{2,1,0:T(8,128)(2,1)S(1)}, u32[]{:S(2)}, u32[]{:S(2)}) %collective-permute-start.14) | collective-permute-done | bytes 393248 | tf_op jit(solution)/shard_map/ppermute | solution.py:405
  124.3 12.8 %shard_map.334 = (bf16[176,768]{1,0:T(8,128)(2,1)}, bf16[512,768]{1,0:T(8,128)(2,1)}, bf16[512,768]{1,0:T(8,128)(2,1)}, bf16[176,768]{1,0:T(8,128)(2,1)}, f32[17...) custom-call(s32[2]{0:T(128)} %pad_add_fusion.refs_0_.position_ref, ...), custom_call_target="tpu_custom_call" | custom-call | flops 14949999616 | tf_op jit(solution)/shard_map/pallas_call | solution.py:622
  140.1 10.4 %shard_map.335 = (bf16[176,768]{1,0:T(8,128)(2,1)}, bf16[512,768]{1,0:T(8,128)(2,1)}, bf16[512,768]{1,0:T(8,128)(2,1)}, bf16[176,768]{1,0:T(8,128)(2,1)}, f32[17...) custom-call(bf16[176,768]{1,0:T(8,128)(2,1)} %get-tuple-element.208.refs_0_.refs_2_, ...), custom_call_target="tpu_custom_call" | custom-call | flops 11500000256 | tf_op jit(solution)/shard_map/pallas_call | solution.py:622
  152.5 6.8 %collective-permute-done.35.refs_17_ = bf16[2,4,32,768]{3,2,1,0:T(8,128)(2,1)S(1)} collective-permute-done((bf16[2,4,32,768]{3,2,1,0:T(8,128)(2,1)S(1)}, bf16[2,4,32,768]{3,2,1,0:T(8,128)(2,1)S(1)}, u32[]{:S(2)}, u32[]{:S(2)}) %collective-permute-start.35) | collective-permute-done | bytes 393248 | tf_op jit(solution)/shard_map/ppermute | solution.py:405
  159.8 10.4 %shard_map.336 = (bf16[176,768]{1,0:T(8,128)(2,1)}, bf16[512,768]{1,0:T(8,128)(2,1)}, bf16[512,768]{1,0:T(8,128)(2,1)}, bf16[176,768]{1,0:T(8,128)(2,1)}, f32[17...) custom-call(bf16[176,768]{1,0:T(8,128)(2,1)} %get-tuple-element.221.refs_0_.refs_3_, ...), custom_call_target="tpu_custom_call" | custom-call | flops 11500000256 | tf_op jit(solution)/shard_map/pallas_call | solution.py:622
  173.9 31.3 %shard_map.337 = (bf16[528,768]{1,0:T(8,128)(2,1)}, f32[528,768]{1,0:T(8,128)}, bf16[528,768]{1,0:T(8,128)(2,1)}, f32[1,768]{1,0:T(1,128)}, bf16[2,8,1152,128]{3...) custom-call(s32[2]{0:T(128)} %pad_add_fusion.refs_0_.position_ref, bf16[528,768]{1,0:T(8,128)(2,1)} %bitcast.408, ...), custom_call_target="tpu_custom_call" | custom-call | flops 35649998848 | tf_op jit(solution)/shard_map/pallas_call | solution.py:1009
  205.9 9.8 %shard_map.338 = (bf16[176,768]{1,0:T(8,128)(2,1)}, bf16[512,768]{1,0:T(8,128)(2,1)}, bf16[512,768]{1,0:T(8,128)(2,1)}, f32[176,768]{1,0:T(8,128)}, bf16[176,768]{1,0:T(8,128)(2,1)}, /*index=5*/f32[1,768]{1,0:T(1,128)}) custom-call(bf16[528,768]{1,0:T(8,128)(2,1)} %get-tuple-element.231.refs_0_.refs_19_.refs_20_.refs_21_, ...), custom_call_target="tpu_custom_call" | custom-call | flops 11500000256 | tf_op jit(solution)/shard_map/pallas_call | solution.py:622
  215.7 3.6 fusion
  224.1 9.7 %shard_map.339 = (bf16[176,768]{1,0:T(8,128)(2,1)}, bf16[512,768]{1,0:T(8,128)(2,1)}, bf16[512,768]{1,0:T(8,128)(2,1)}, f32[176,768]{1,0:T(8,128)}, bf16[176,768]{1,0:T(8,128)(2,1)}, /*index=5*/f32[1,768]{1,0:T(1,128)}) custom-call(bf16[528,768]{1,0:T(8,128)(2,1)} %get-tuple-element.231.refs_0_.refs_19_.refs_20_.refs_21_, ...), custom_call_target="tpu_custom_call" | custom-call | flops 11500000256 | tf_op jit(solution)/shard_map/pallas_call | solution.py:622
  233.8 10.1 %shard_map.340 = (bf16[176,768]{1,0:T(8,128)(2,1)}, bf16[512,768]{1,0:T(8,128)(2,1)}, bf16[512,768]{1,0:T(8,128)(2,1)}, f32[176,768]{1,0:T(8,128)}, bf16[176,768]{1,0:T(8,128)(2,1)}, /*index=5*/f32[1,768]{1,0:T(1,128)}) custom-call(bf16[528,768]{1,0:T(8,128)(2,1)} %get-tuple-element.231.refs_0_.refs_19_.refs_20_.refs_21_, ...), custom_call_target="tpu_custom_call" | custom-call | flops 11500000256 | tf_op jit(solution)/shard_map/pallas_call | solution.py:622
  243.8 5.3 %collective-permute-done.43 = bf16[2,2,2,576,128]{4,3,2,1,0:T(8,128)(2,1)} collective-permute-done((bf16[2,2,2,576,128]{4,3,2,1,0:T(8,128)(2,1)S(1)}, bf16[2,2,2,576,128]{4,3,2,1,0:T(8,128)(2,1)}, u32[]{:S(2)}, u32[]{:S(2)}) %collective-permute-start.43) | collective-permute-done | bytes 1179680 | tf_op jit(solution)/shard_map/ppermute | solution.py:405
  254.2 13.7 %shard_map.341 = (bf16[2,8,96,768]{3,2,1,0:T(8,128)(2,1)}, bf16[2,8,96,768]{3,2,1,0:T(8,128)(2,1)}) custom-call(s32[2]{0:T(128)} %pad_add_fusion.refs_0_.position_ref, bf16[176,768]{1,0:T(8,128)(2,1)} %get-tuple-element.257.refs_2_.refs_1_, bf16[176,768]{1,0:T(8,128)(2,1)} %get-tuple-element.208.refs_0_.refs_2_, ...), custom_call_target="tpu_custom_call" | custom-call | flops 14949999616 | tf_op jit(solution)/shard_map/pallas_call | solution.py:622
  268.8 11.0 %shard_map.342 = (bf16[176,768]{1,0:T(8,128)(2,1)}, bf16[176,768]{1,0:T(8,128)(2,1)}, bf16[176,768]{1,0:T(8,128)(2,1)}, bf16[176,768]{1,0:T(8,128)(2,1)}, f32[1,768]{1,0:T(1,128)}, /*index=5*/f32[32,128]{1,0:T(8,128)}) custom-call(bf16[176,768]{1,0:T(8,128)(2,1)} %get-tuple-element.236.refs_0_.refs_16_, ...), custom_call_target="tpu_custom_call" | custom-call | flops 12650000384 | tf_op jit(solution)/shard_map/pallas_call | solution.py:622
  279.8 4.3 %collective-permute-done.45 = bf16[2,1152,128]{2,1,0:T(8,128)(2,1)S(1)} collective-permute-done((bf16[2,1152,128]{2,1,0:T(8,128)(2,1)S(1)}, bf16[2,1152,128]{2,1,0:T(8,128)(2,1)S(1)}, u32[]{:S(2)}, u32[]{:S(2)}) %collective-permute-start.45) | collective-permute-done | bytes 589856 | tf_op jit(solution)/shard_map/ppermute | solution.py:409
  289.7 10.8 %shard_map.343 = (bf16[176,768]{1,0:T(8,128)(2,1)}, bf16[176,768]{1,0:T(8,128)(2,1)}, bf16[176,768]{1,0:T(8,128)(2,1)}, bf16[176,768]{1,0:T(8,128)(2,1)}, f32[1,768]{1,0:T(1,128)}, /*index=5*/f32[32,128]{1,0:T(8,128)}) custom-call(bf16[176,768]{1,0:T(8,128)(2,1)} %get-tuple-element.275.refs_0_.refs_17_, ...), custom_call_target="tpu_custom_call" | custom-call | flops 12650000384 | tf_op jit(solution)/shard_map/pallas_call | solution.py:622
  306.9 11.1 %shard_map.344 = (bf16[176,768]{1,0:T(8,128)(2,1)}, bf16[176,768]{1,0:T(8,128)(2,1)}, bf16[176,768]{1,0:T(8,128)(2,1)}, bf16[176,768]{1,0:T(8,128)(2,1)}, f32[1,768]{1,0:T(1,128)}, /*index=5*/f32[32,128]{1,0:T(8,128)}) custom-call(bf16[176,768]{1,0:T(8,128)(2,1)} %get-tuple-element.285.refs_0_.refs_18_, ...), custom_call_target="tpu_custom_call" | custom-call | flops 12650000384 | tf_op jit(solution)/shard_map/pallas_call | solution.py:622
  322.3 13.8 %shard_map.345 = (bf16[2,8,104,768]{3,2,1,0:T(8,128)(2,1)}, bf16[2,8,104,768]{3,2,1,0:T(8,128)(2,1)}) custom-call(s32[2]{0:T(128)} %pad_add_fusion.refs_0_.position_ref, bf16[176,768]{1,0:T(8,128)(2,1)} %get-tuple-element.181.refs_1_, bf16[176,768]{1,0:T(8,128)(2,1)} %get-tuple-element.192.refs_2_, bf16[176,768]{1,0:T(8,128)(2,1)} %get-tuple-element.194.refs_3_, ...), custom_call_target="tpu_custom_call" | custom-call | flops 14949999616 | tf_op jit(solution)/shard_map/pallas_call | solution.py:622
  343.7 8.4 %shard_map.346 = bf16[3,512,768]{2,1,0:T(8,128)(2,1)} custom-call(bf16[512,768]{1,0:T(8,128)(2,1)} %get-tuple-element.261.refs_10_.refs_0_, bf16[8,96,768]{2,1,0:T(8,128)(2,1)} %get-tuple-element.322.refs_3_.refs_1_, bf16[512,768]{1,0:T(8,128)(2,1)} %get-tuple-element.264.refs_13_.refs_2_, bf16[8,96,768]{2,1,0:T(8,128)(2,1)} %get-tuple-element.211.refs_4_.refs_3_, ...), custom_call_target="tpu_custom_call" | custom-call | flops 9200000000 | tf_op jit(solution)/shard_map/pallas_call | solution.py:622
  352.1 6.6 %collective-permute-done.53 = bf16[2,2,2,48,768]{4,3,1,0,2:T(8,128)(2,1)S(1)} collective-permute-done((bf16[2,2,2,48,768]{4,3,1,0,2:T(8,128)(2,1)S(1)}, bf16[2,2,2,48,768]{4,3,1,0,2:T(8,128)(2,1)S(1)}, u32[]{:S(2)}, u32[]{:S(2)}) %collective-permute-start.53) | collective-permute-done | bytes 589856 | tf_op jit(solution)/shard_map/ppermute | solution.py:401
  373.5 4.2 %collective-permute-done.57 = bf16[2,104,768]{2,1,0:T(8,128)(2,1)S(1)} collective-permute-done((bf16[2,104,768]{2,1,0:T(8,128)(2,1)S(1)}, bf16[2,104,768]{2,1,0:T(8,128)(2,1)S(1)}, u32[]{:S(2)}, u32[]{:S(2)}) %collective-permute-start.57) | collective-permute-done | bytes 319520 | tf_op jit(solution)/shard_map/ppermute | solution.py:409
  384.1 3.9 collective-permute-start.59
  (309 shorter events, 113.2 us)
Async XLA Ops:
  33.5 19.8 %collective-permute-start.7 = (bf16[2,4,56,768]{3,2,1,0:T(8,128)(2,1)S(1)}, bf16[2,4,56,768]{3,2,1,0:T(8,128)(2,1)}, u32[]{:S(2)}, u32[]{:S(2)}) collective-permute-start(bf16[2,4,56,768]{3,2,1,0:T(8,128)(2,1)S(1)} %pad_maximum_fusion.4.refs_6_), channel_id=1, source_target_pairs={{0,1},{1,0},{2,3},{3,2},{4,5},{5,4},{6,7},{7,6},{8,9},{9,8},{10,11... | collective-permute-start | bytes 2064392 | tf_op jit(solution)/shard_map/ppermute | solution.py:405
  35.9 17.4 %collective-permute-start.6 = (bf16[2,4,48,768]{3,2,1,0:T(8,128)(2,1)}, bf16[2,4,48,768]{3,2,1,0:T(8,128)(2,1)}, u32[]{:S(2)}, u32[]{:S(2)}) collective-permute-start(bf16[2,4,48,768]{3,2,1,0:T(8,128)(2,1)} %pad_maximum_fusion.7.refs_4_), channel_id=1, source_target_pairs={{0,16},{8,24},{16,0},{24,8},{1,17},{9,25},{17,1},{25,9},{2,18},{10... | collective-permute-start | bytes 1769480 | tf_op jit(solution)/shard_map/ppermute | solution.py:401
  56.3 16.2 %collective-permute-start.10 = (bf16[2,4,56,768]{3,2,1,0:T(8,128)(2,1)S(1)}, bf16[2,4,56,768]{3,2,1,0:T(8,128)(2,1)}, u32[]{:S(2)}, u32[]{:S(2)}) collective-permute-start(bf16[2,4,56,768]{3,2,1,0:T(8,128)(2,1)S(1)} %pad_maximum_fusion.4.refs_6_), channel_id=1, source_target_pairs={{0,8},{8,0},{16,24},{24,16},{1,9},{9,1},{17,25},{25,17},{2,10},{10... | collective-permute-start | bytes 2064392 | tf_op jit(solution)/shard_map/ppermute | solution.py:397
  56.3 16.3 %collective-permute-start.11 = (bf16[2,4,56,768]{3,2,1,0:T(8,128)(2,1)}, bf16[2,4,56,768]{3,2,1,0:T(8,128)(2,1)}, u32[]{:S(2)}, u32[]{:S(2)}) collective-permute-start(bf16[2,4,56,768]{3,2,1,0:T(8,128)(2,1)} %collective-permute-done.7.refs_7_), channel_id=1, source_target_pairs={{0,8},{8,0},{16,24},{24,16},{1,9},{9,1},{17,25},{25,17},{2,10},{10... | collective-permute-start | bytes 2064392 | tf_op jit(solution)/shard_map/ppermute | solution.py:397
  84.5 22.7 %collective-permute-start.21 = (bf16[2,4,48,768]{3,2,1,0:T(8,128)(2,1)S(1)}, bf16[2,4,48,768]{3,2,1,0:T(8,128)(2,1)}, u32[]{:S(2)}, u32[]{:S(2)}) collective-permute-start(bf16[2,4,48,768]{3,2,1,0:T(8,128)(2,1)S(1)} %pad_maximum_fusion.9.refs_9_), channel_id=1, source_target_pairs={{0,1},{1,0},{2,3},{3,2},{4,5},{5,4},{6,7},{7,6},{8,9},{9,8},{10,11... | collective-permute-start | bytes 1769480 | tf_op jit(solution)/shard_map/ppermute | solution.py:405
  84.9 22.6 %collective-permute-start.20 = (bf16[2,4,48,768]{3,2,1,0:T(8,128)(2,1)S(1)}, bf16[2,4,48,768]{3,2,1,0:T(8,128)(2,1)}, u32[]{:S(2)}, u32[]{:S(2)}) collective-permute-start(bf16[2,4,48,768]{3,2,1,0:T(8,128)(2,1)S(1)} %pad_maximum_fusion.8.refs_7_), channel_id=1, source_target_pairs={{0,16},{8,24},{16,0},{24,8},{1,17},{9,25},{17,1},{25,9},{2,18},{10... | collective-permute-start | bytes 1769480 | tf_op jit(solution)/shard_map/ppermute | solution.py:401
  87.3 33.6 %collective-permute-start.24 = (bf16[2,4,48,768]{3,2,1,0:T(8,128)(2,1)S(1)}, bf16[2,4,48,768]{3,2,1,0:T(8,128)(2,1)}, u32[]{:S(2)}, u32[]{:S(2)}) collective-permute-start(bf16[2,4,48,768]{3,2,1,0:T(8,128)(2,1)S(1)} %pad_maximum_fusion.9.refs_9_), channel_id=1, source_target_pairs={{0,8},{8,0},{16,24},{24,16},{1,9},{9,1},{17,25},{25,17},{2,10},{10... | collective-permute-start | bytes 1769480 | tf_op jit(solution)/shard_map/ppermute | solution.py:397
  107.2 14.6 %collective-permute-start.22 = (bf16[2,4,48,768]{3,2,1,0:T(8,128)(2,1)S(1)}, bf16[2,4,48,768]{3,2,1,0:T(8,128)(2,1)S(1)}, u32[]{:S(2)}, u32[]{:S(2)}) collective-permute-start(bf16[2,4,48,768]{3,2,1,0:T(8,128)(2,1)S(1)} %pad_maximum_fusion.8.refs_7_), channel_id=1, source_target_pairs={{0,8},{8,0},{16,24},{24,16},{1,9},{9,1},{17,25},{25,17},{2,10},{10... | collective-permute-start | bytes 1769480 | tf_op jit(solution)/shard_map/ppermute | solution.py:397
  107.5 15.1 %collective-permute-start.25 = (bf16[2,4,48,768]{3,2,1,0:T(8,128)(2,1)}, bf16[2,4,48,768]{3,2,1,0:T(8,128)(2,1)S(1)}, u32[]{:S(2)}, u32[]{:S(2)}) collective-permute-start(bf16[2,4,48,768]{3,2,1,0:T(8,128)(2,1)} %collective-permute-done.21.refs_10_), channel_id=1, source_target_pairs={{0,8},{8,0},{16,24},{24,16},{1,9},{9,1},{17,25},{25,17},{2,10},{10... | collective-permute-start | bytes 1769480 | tf_op jit(solution)/shard_map/ppermute | solution.py:397
  107.8 15.7 %collective-permute-start.23 = (bf16[2,4,48,768]{3,2,1,0:T(8,128)(2,1)}, bf16[2,4,48,768]{3,2,1,0:T(8,128)(2,1)S(1)}, u32[]{:S(2)}, u32[]{:S(2)}) collective-permute-start(bf16[2,4,48,768]{3,2,1,0:T(8,128)(2,1)} %collective-permute-done.20.refs_8_), channel_id=1, source_target_pairs={{0,8},{8,0},{16,24},{24,16},{1,9},{9,1},{17,25},{25,17},{2,10},{10... | collective-permute-start | bytes 1769480 | tf_op jit(solution)/shard_map/ppermute | solution.py:397
  120.5 31.3 %collective-permute-start.27 = (bf16[2,4,48,1024]{3,2,1,0:T(8,128)(2,1)S(1)}, bf16[2,4,48,1024]{3,2,1,0:T(8,128)(2,1)S(1)}, u32[]{:S(2)}, u32[]{:S(2)}) collective-permute-start(bf16[2,4,48,1024]{3,2,1,0:T(8,128)(2,1)S(1)} %pad_maximum_fusion.3.refs_8_), channel_id=1, source_target_pairs={{0,1},{1,0},{2,3},{3,2},{4,5},{5,4},{6,7},{7,6},{8,9},{9,8},{10,11... | collective-permute-start | bytes 2359304 | tf_op jit(solution)/shard_map/ppermute | solution.py:405
  120.9 31.5 %collective-permute-start.26 = (bf16[2,4,48,1024]{3,2,1,0:T(8,128)(2,1)S(1)}, bf16[2,4,48,1024]{3,2,1,0:T(8,128)(2,1)S(1)}, u32[]{:S(2)}, u32[]{:S(2)}) collective-permute-start(bf16[2,4,48,1024]{3,2,1,0:T(8,128)(2,1)S(1)} %pad_maximum_fusion.2.refs_6_), channel_id=1, source_target_pairs={{0,16},{8,24},{16,0},{24,8},{1,17},{9,25},{17,1},{25,9},{2,18},{10... | collective-permute-start | bytes 2359304 | tf_op jit(solution)/shard_map/ppermute | solution.py:401
  137.1 13.4 %collective-permute-start.29 = (bf16[4,32,768]{2,1,0:T(8,128)(2,1)S(1)}, bf16[4,32,768]{2,1,0:T(8,128)(2,1)S(1)}, u32[]{:S(2)}, u32[]{:S(2)}) collective-permute-start(bf16[4,32,768]{2,1,0:T(8,128)(2,1)S(1)} %get-tuple-element.400), channel_id=1, source_target_pairs={{0,16},{8,24},{16,0},{24,8},{1,17},{9,25},{17,1},{25,9},{2,18},{10... | collective-permute-start | bytes 589832 | tf_op jit(solution)/shard_map/ppermute | solution.py:401
  151.9 18.4 %collective-permute-start.32 = (bf16[2,4,48,1024]{3,2,1,0:T(8,128)(2,1)S(1)}, bf16[2,4,48,1024]{3,2,1,0:T(8,128)(2,1)S(1)}, u32[]{:S(2)}, u32[]{:S(2)}) collective-permute-start(bf16[2,4,48,1024]{3,2,1,0:T(8,128)(2,1)S(1)} %pad_maximum_fusion.3.refs_8_), channel_id=1, source_target_pairs={{0,8},{8,0},{16,24},{24,16},{1,9},{9,1},{17,25},{25,17},{2,10},{10... | collective-permute-start | bytes 2359304 | tf_op jit(solution)/shard_map/ppermute | solution.py:397
  151.9 18.6 %collective-permute-start.30 = (bf16[2,4,48,1024]{3,2,1,0:T(8,128)(2,1)S(1)}, bf16[2,4,48,1024]{3,2,1,0:T(8,128)(2,1)}, u32[]{:S(2)}, u32[]{:S(2)}) collective-permute-start(bf16[2,4,48,1024]{3,2,1,0:T(8,128)(2,1)S(1)} %pad_maximum_fusion.2.refs_6_), channel_id=1, source_target_pairs={{0,8},{8,0},{16,24},{24,16},{1,9},{9,1},{17,25},{25,17},{2,10},{10... | collective-permute-start | bytes 2359304 | tf_op jit(solution)/shard_map/ppermute | solution.py:397
  152.4 19.6 %collective-permute-start.33 = (bf16[2,4,48,1024]{3,2,1,0:T(8,128)(2,1)S(1)}, bf16[2,4,48,1024]{3,2,1,0:T(8,128)(2,1)}, u32[]{:S(2)}, u32[]{:S(2)}) collective-permute-start(bf16[2,4,48,1024]{3,2,1,0:T(8,128)(2,1)S(1)} %collective-permute-done.27.refs_9_), channel_id=1, source_target_pairs={{0,8},{8,0},{16,24},{24,16},{1,9},{9,1},{17,25},{25,17},{2,10},{10... | collective-permute-start | bytes 2359304 | tf_op jit(solution)/shard_map/ppermute | solution.py:397
  221.0 28.1 %collective-permute-start.43 = (bf16[2,2,2,576,128]{4,3,2,1,0:T(8,128)(2,1)S(1)}, bf16[2,2,2,576,128]{4,3,2,1,0:T(8,128)(2,1)}, u32[]{:S(2)}, u32[]{:S(2)}) collective-permute-start(bf16[2,2,2,576,128]{4,3,2,1,0:T(8,128)(2,1)S(1)} %dynamic-slice_bitcast_fusion), channel_id=1, source_target_pairs={{0,1},{1,0},{2,3},{3,2},{4,5},{5,4},{6,7},{7,6},{8,9},{9,8},{10,11... | collective-permute-start | bytes 3538952 | tf_op jit(solution)/shard_map/ppermute | solution.py:405
  222.6 28.1 %collective-permute-start.41 = (bf16[2,2,2,576,128]{4,3,1,0,2:T(8,128)(2,1)}, bf16[2,2,2,576,128]{4,3,1,0,2:T(8,128)(2,1)S(1)}, u32[]{:S(2)}, u32[]{:S(2)}) collective-permute-start(bf16[2,2,2,576,128]{4,3,1,0,2:T(8,128)(2,1)} %bitcast.328), channel_id=1, source_target_pairs={{0,16},{8,24},{16,0},{24,8},{1,17},{9,25},{17,1},{25,9},{2,18},{10... | collective-permute-start | bytes 3538952 | tf_op jit(solution)/shard_map/ppermute | solution.py:401
  251.1 16.8 %collective-permute-start.44 = (bf16[2,2,576,128]{3,2,1,0:T(8,128)(2,1)S(1)}, bf16[2,2,576,128]{3,2,1,0:T(8,128)(2,1)S(1)}, u32[]{:S(2)}, u32[]{:S(2)}) collective-permute-start(bf16[2,2,576,128]{3,2,1,0:T(8,128)(2,1)S(1)} %dynamic-slice_bitcast_fusion.3), channel_id=1, source_target_pairs={{0,16},{8,24},{16,0},{24,8},{1,17},{9,25},{17,1},{25,9},{2,18},{10... | collective-permute-start | bytes 1769480 | tf_op jit(solution)/shard_map/ppermute | solution.py:401
  252.6 15.5 %collective-permute-start.42 = (bf16[2,2,576,128]{3,2,1,0:T(8,128)(2,1)S(1)}, bf16[2,2,576,128]{3,2,1,0:T(8,128)(2,1)S(1)}, u32[]{:S(2)}, u32[]{:S(2)}) collective-permute-start(bf16[2,2,576,128]{3,2,1,0:T(8,128)(2,1)S(1)} %dynamic-slice_bitcast_fusion.4), channel_id=1, source_target_pairs={{0,1},{1,0},{2,3},{3,2},{4,5},{5,4},{6,7},{7,6},{8,9},{9,8},{10,11... | collective-permute-start | bytes 1769480 | tf_op jit(solution)/shard_map/ppermute | solution.py:405
  267.9 17.9 %collective-permute-start.46 = (bf16[2,2,2,2,96,768]{5,4,3,2,1,0:T(8,128)(2,1)}, bf16[2,2,2,2,96,768]{5,4,3,2,1,0:T(8,128)(2,1)}, u32[]{:S(2)}, u32[]{:S(2)}) collective-permute-start(bf16[2,2,2,2,96,768]{5,4,3,2,1,0:T(8,128)(2,1)} %bitcast.407), channel_id=1, source_target_pairs={{0,8},{8,0},{16,24},{24,16},{1,9},{9,1},{17,25},{25,17},{2,10},{10... | collective-permute-start | bytes 7077896 | tf_op jit(solution)/shard_map/ppermute | solution.py:397
  268.4 15.8 %collective-permute-start.45 = (bf16[2,1152,128]{2,1,0:T(8,128)(2,1)S(1)}, bf16[2,1152,128]{2,1,0:T(8,128)(2,1)S(1)}, u32[]{:S(2)}, u32[]{:S(2)}) collective-permute-start(bf16[2,1152,128]{2,1,0:T(8,128)(2,1)S(1)} %fusion.18), channel_id=1, source_target_pairs={{0,2},{1,3},{2,0},{3,1},{4,6},{5,7},{6,4},{7,5},{8,10},{9,11},{10,... | collective-permute-start | bytes 1769480 | tf_op jit(solution)/shard_map/ppermute | solution.py:409
  284.4 16.2 %collective-permute-start.47 = (bf16[1152,128]{1,0:T(8,128)(2,1)S(1)}, bf16[1152,128]{1,0:T(8,128)(2,1)S(1)}, u32[]{:S(2)}, u32[]{:S(2)}) collective-permute-start(bf16[1152,128]{1,0:T(8,128)(2,1)S(1)} %dynamic-slice_bitcast_fusion.9), channel_id=1, source_target_pairs={{0,4},{1,5},{2,6},{3,7},{4,0},{5,1},{6,2},{7,3},{8,12},{9,13},{10,... | collective-permute-start | bytes 884744 | tf_op jit(solution)/shard_map/ppermute | solution.py:413
  288.6 15.0 %collective-permute-start.49 = (bf16[2,2,2,48,768]{4,3,2,1,0:T(8,128)(2,1)S(1)}, bf16[2,2,2,48,768]{4,3,2,1,0:T(8,128)(2,1)S(1)}, u32[]{:S(2)}, u32[]{:S(2)}) collective-permute-start(bf16[2,2,2,48,768]{4,3,2,1,0:T(8,128)(2,1)S(1)} %dynamic-slice_bitcast_fusion.2), channel_id=1, source_target_pairs={{0,1},{1,0},{2,3},{3,2},{4,5},{5,4},{6,7},{7,6},{8,9},{9,8},{10,11... | collective-permute-start | bytes 1769480 | tf_op jit(solution)/shard_map/ppermute | solution.py:405
  289.1 15.5 %collective-permute-start.48 = (bf16[2,2,2,48,768]{4,3,1,0,2:T(8,128)(2,1)S(1)}, bf16[2,2,2,48,768]{4,3,1,0,2:T(8,128)(2,1)S(1)}, u32[]{:S(2)}, u32[]{:S(2)}) collective-permute-start(bf16[2,2,2,48,768]{4,3,1,0,2:T(8,128)(2,1)S(1)} %bitcast.369), channel_id=1, source_target_pairs={{0,16},{8,24},{16,0},{24,8},{1,17},{9,25},{17,1},{25,9},{2,18},{10... | collective-permute-start | bytes 1769480 | tf_op jit(solution)/shard_map/ppermute | solution.py:401
  300.6 35.5 %collective-permute-start.65 = (bf16[1152,128]{1,0:T(8,128)(2,1)S(1)}, bf16[1152,128]{1,0:T(8,128)(2,1)S(1)}, u32[]{:S(2)}, u32[]{:S(2)}) collective-permute-start(bf16[1152,128]{1,0:T(8,128)(2,1)S(1)} %fusion.24), channel_id=1, source_target_pairs={{0,16},{8,24},{16,0},{24,8},{1,17},{9,25},{17,1},{25,9},{2,18},{10... | collective-permute-start | bytes 884744 | tf_op jit(solution)/shard_map/ppermute | solution.py:401
  304.7 15.2 %collective-permute-start.51 = (bf16[2,2,48,768]{3,2,1,0:T(8,128)(2,1)S(1)}, bf16[2,2,48,768]{3,2,1,0:T(8,128)(2,1)S(1)}, u32[]{:S(2)}, u32[]{:S(2)}) collective-permute-start(bf16[2,2,48,768]{3,2,1,0:T(8,128)(2,1)S(1)} %dynamic-slice_bitcast_fusion.7), channel_id=1, source_target_pairs={{0,16},{8,24},{16,0},{24,8},{1,17},{9,25},{17,1},{25,9},{2,18},{10... | collective-permute-start | bytes 884744 | tf_op jit(solution)/shard_map/ppermute | solution.py:401
  304.9 15.1 %collective-permute-start.50 = (bf16[2,2,48,768]{3,2,1,0:T(8,128)(2,1)S(1)}, bf16[2,2,48,768]{3,2,1,0:T(8,128)(2,1)S(1)}, u32[]{:S(2)}, u32[]{:S(2)}) collective-permute-start(bf16[2,2,48,768]{3,2,1,0:T(8,128)(2,1)S(1)} %dynamic-slice_bitcast_fusion.8), channel_id=1, source_target_pairs={{0,1},{1,0},{2,3},{3,2},{4,5},{5,4},{6,7},{7,6},{8,9},{9,8},{10,11... | collective-permute-start | bytes 884744 | tf_op jit(solution)/shard_map/ppermute | solution.py:405
  320.2 16.7 %collective-permute-start.61 = (bf16[2,96,768]{2,1,0:T(8,128)(2,1)S(1)}, bf16[2,96,768]{2,1,0:T(8,128)(2,1)S(1)}, u32[]{:S(2)}, u32[]{:S(2)}) collective-permute-start(bf16[2,96,768]{2,1,0:T(8,128)(2,1)S(1)} %fusion.33), channel_id=1, source_target_pairs={{0,2},{1,3},{2,0},{3,1},{4,6},{5,7},{6,4},{7,5},{8,10},{9,11},{10,... | collective-permute-start | bytes 884744 | tf_op jit(solution)/shard_map/ppermute | solution.py:409
  337.7 34.3 %collective-permute-start.62 = (bf16[96,768]{1,0:T(8,128)(2,1)}, bf16[96,768]{1,0:T(8,128)(2,1)}, u32[]{:S(2)}, u32[]{:S(2)}) collective-permute-start(bf16[96,768]{1,0:T(8,128)(2,1)} %dynamic-slice_bitcast_fusion.11), channel_id=1, source_target_pairs={{0,4},{1,5},{2,6},{3,7},{4,0},{5,1},{6,2},{7,3},{8,12},{9,13},{10,... | collective-permute-start | bytes 442376 | tf_op jit(solution)/shard_map/ppermute | solution.py:413
  343.3 15.4 %collective-permute-start.53 = (bf16[2,2,2,48,768]{4,3,1,0,2:T(8,128)(2,1)S(1)}, bf16[2,2,2,48,768]{4,3,1,0,2:T(8,128)(2,1)S(1)}, u32[]{:S(2)}, u32[]{:S(2)}) collective-permute-start(bf16[2,2,2,48,768]{4,3,1,0,2:T(8,128)(2,1)S(1)} %bitcast.370), channel_id=1, source_target_pairs={{0,16},{8,24},{16,0},{24,8},{1,17},{9,25},{17,1},{25,9},{2,18},{10... | collective-permute-start | bytes 1769480 | tf_op jit(solution)/shard_map/ppermute | solution.py:401
  343.4 17.5 %collective-permute-start.55 = (bf16[2,2,2,56,768]{4,3,2,1,0:T(8,128)(2,1)S(1)}, bf16[2,2,2,56,768]{4,3,2,1,0:T(8,128)(2,1)S(1)}, u32[]{:S(2)}, u32[]{:S(2)}) collective-permute-start(bf16[2,2,2,56,768]{4,3,2,1,0:T(8,128)(2,1)S(1)} %dynamic-slice_bitcast_fusion.1), channel_id=1, source_target_pairs={{0,1},{1,0},{2,3},{3,2},{4,5},{5,4},{6,7},{7,6},{8,9},{9,8},{10,11... | collective-permute-start | bytes 2064392 | tf_op jit(solution)/shard_map/ppermute | solution.py:405
  (68 other events, 674.9 us)
